TPU v7x, 32 devices: a whole 2x2x4 slice. The times are simulated.
32 devices in a mesh: groups: 2 (over x), seq: 16 (over z, y, core).
Axes of the slice: x: 2, y: 2, z: 4, core: 2. Of those that a mesh axis runs over, the one named last changes fastest.
Arguments:
- queries: bfloat16 [8192, 4096], P(('groups', 'seq')), parts along dimension 0, may hold values from -6 to 6
- key_rows: bfloat16 [8192, 2048], P(('groups', 'seq')), parts along dimension 0, may hold values from -6 to 6
- value_matrix: bfloat16 [8192, 2048], P(('groups', 'seq')), parts along dimension 0, may hold values from -6 to 6
Outputs:
- attended: bfloat16 [8192, 4096], P(('groups', 'seq')), parts along dimension 0
There are 2 independent parts, one for each index of `groups`. A program takes and returns all parts, laid end to end along the dimension named above; each array names one. Nothing has to cross between parts.
All inputs are finite; a program needn't handle non-finite values.
Results may differ from a plain program's by a relative error of at most 0.0045.
Values may be sent and summed in bfloat16 or wider, within the bound.
No kernel may reach another device: no remote copies, remote signals or barrier semaphores. Data moves between devices by JAX's collectives and lax.ppermute only.
A program may use at most 64 MiB of HBM per device.

v0:
```python
from functools import reduce

import jax
import jax.numpy as jnp
from jax import lax
from jax.sharding import PartitionSpec as P

QUERY_HEADS = 32
KEY_VALUE_HEADS = 16
HEAD_WIDTH = 128
WINDOW = 1024


score_scale = 168.0 ** (-0.5)
masked_value = -1e30


def passed_along(shard, axis, by):
    length = lax.axis_size(axis)
    pairs = [(i, i + by) for i in range(length) if 0 <= i + by < length]
    return lax.ppermute(shard, axis, pairs)


def visible_pairs(query_pos, key_pos):
    return (
        (key_pos[None, :] <= query_pos[:, None])
        & (key_pos[None, :] > query_pos[:, None] - WINDOW)
        & (key_pos[None, :] >= 0)
    )


def per_device(queries, key_rows, value_matrix):
    length = queries.shape[0]
    hops_back = (WINDOW - 1) // length + 1
    query_groups = QUERY_HEADS // KEY_VALUE_HEADS
    local_kv = jnp.stack([key_rows, value_matrix])
    arrived = [local_kv]
    moving = local_kv
    for hop_count in range(hops_back):
        moving = passed_along(moving, "seq", 1)
        arrived.append(moving)
    device = lax.axis_index("seq")
    offsets = jnp.arange(length, dtype=jnp.int32)
    query_pos = device * length + offsets
    visible_sets = [
        visible_pairs(query_pos, (device - hop_count) * length + offsets)
        for hop_count in range(hops_back + 1)
    ]

    def head_count_ratio(head_index, output):
        query_head = lax.dynamic_slice_in_dim(
            queries, head_index * query_groups * HEAD_WIDTH, query_groups * HEAD_WIDTH, 1
        ).reshape(length, query_groups, HEAD_WIDTH)
        score_list = []
        for hop_count in range(hops_back + 1):
            key_head = lax.dynamic_slice_in_dim(
                arrived[hop_count][0], head_index * HEAD_WIDTH, HEAD_WIDTH, 1
            )
            raw_scores = (
                jnp.einsum("tgd,kd->gtk", query_head, key_head, preferred_element_type=jnp.float32)
                * score_scale
            )
            score_list.append(jnp.where(visible_sets[hop_count][None], raw_scores, masked_value))
        row_max = reduce(jnp.maximum, [jnp.max(entry, axis=2) for entry in score_list])
        row_total = jnp.zeros(row_max.shape, jnp.float32)
        weighted = jnp.zeros((length, query_groups, HEAD_WIDTH), jnp.float32)
        for hop_count in range(hops_back + 1):
            weights_full = jnp.where(
                visible_sets[hop_count][None],
                jnp.exp(score_list[hop_count] - row_max[:, :, None]),
                0.0,
            )
            row_total = row_total + jnp.sum(weights_full, axis=2)
            value_head = lax.dynamic_slice_in_dim(
                arrived[hop_count][1], head_index * HEAD_WIDTH, HEAD_WIDTH, 1
            )
            weighted = weighted + jnp.einsum(
                "gtk,kd->tgd",
                weights_full.astype(jnp.bfloat16),
                value_head,
                preferred_element_type=jnp.float32,
            )
        result = weighted / jnp.transpose(row_total)[:, :, None]
        result = result.reshape(length, query_groups * HEAD_WIDTH).astype(jnp.bfloat16)
        return lax.dynamic_update_slice_in_dim(
            output, result, head_index * query_groups * HEAD_WIDTH, 1
        )

    return lax.fori_loop(
        0, KEY_VALUE_HEADS, head_count_ratio, jnp.zeros(queries.shape, jnp.bfloat16)
    )


def solution(mesh):
    return jax.shard_map(
        per_device,
        mesh=mesh,
        in_specs=(
            P(("groups", "seq"), None),
            P(("groups", "seq"), None),
            P(("groups", "seq"), None),
        ),
        out_specs=P(("groups", "seq"), None),
        check_vma=False,
    )
```

profile of v0, /device:TPU:26, one launch (start us, length us, event | category | flops | bytes accessed | tf_op | source)
XLA Modules:
  0.0 283.5 jit_solution(13030155471916844959)
XLA Ops:
  0.0 1.7 pad_maximum_fusion
  1.7 1.9 collective-permute-start
  3.7 26.3 %collective-permute-done = bf16[2,256,2048]{2,1,0:T(8,128)(2,1)S(1)} collective-permute-done((bf16[2,256,2048]{2,1,0:T(8,128)(2,1)S(1)}, bf16[2,256,2048]{2,1,0:T(8,128)(2,1)S(1)}, u32[]{:S(2)}, u32[]{:S(2)}) %collective-permute-start) | collective-permute-done | bytes 2097184 | tf_op jit(solution)/shard_map/ppermute | solution.py:21
  30.0 1.9 collective-permute-start.1
  31.9 26.3 %collective-permute-done.1 = bf16[2,256,2048]{2,1,0:T(8,128)(2,1)S(1)} collective-permute-done((bf16[2,256,2048]{2,1,0:T(8,128)(2,1)S(1)}, bf16[2,256,2048]{2,1,0:T(8,128)(2,1)S(1)}, u32[]{:S(2)}, u32[]{:S(2)}) %collective-permute-start.1) | collective-permute-done | bytes 2097184 | tf_op jit(solution)/shard_map/ppermute | solution.py:21
  58.2 1.3 copy-done
  59.6 1.9 collective-permute-start.2
  61.5 26.4 %collective-permute-done.2 = bf16[2,256,2048]{2,1,0:T(8,128)(2,1)} collective-permute-done((bf16[2,256,2048]{2,1,0:T(8,128)(2,1)S(1)}, bf16[2,256,2048]{2,1,0:T(8,128)(2,1)}, u32[]{:S(2)}, u32[]{:S(2)}) %collective-permute-start.2) | collective-permute-done | bytes 2097184 | tf_op jit(solution)/shard_map/ppermute | solution.py:21
  87.9 1.9 collective-permute-start.3
  89.9 26.5 %collective-permute-done.3 = bf16[2,256,2048]{2,1,0:T(8,128)(2,1)} collective-permute-done((bf16[2,256,2048]{2,1,0:T(8,128)(2,1)}, bf16[2,256,2048]{2,1,0:T(8,128)(2,1)}, u32[]{:S(2)}, u32[]{:S(2)}) %collective-permute-start.3) | collective-permute-done | bytes 2097184 | tf_op jit(solution)/shard_map/ppermute | solution.py:21
  116.5 1.6 broadcast_in_dim.185.clone
  118.0 165.5 %while.17 = (s32[]{:T(128)}, bf16[256,4096]{1,0:T(8,128)(2,1)}, bf16[256,2048]{1,0:T(8,128)(2,1)}, bf16[256,2048]{1,0:T(8,128)(2,1)}, bf16[256,4096]{1,0:T(8,128...) while((s32[]{:T(128)}, bf16[256,4096]{1,0:T(8,128)(2,1)}, ...), condition=%wide.region_11.12_spmd.clone.clone, body=%wide.region_0.11_spmd.clone.clone.sunk | while | flops 343145472 | bytes 38995596 | solution.py:89
  119.7 2.9 %fusion.146 = (bf16[1,256,2048]{2,1,0:T(8,128)(2,1)S(1)}, bf16[1,256,2048]{2,1,0:T(8,128)(2,1)S(1)}, bf16[1,256,2048]{2,1,0:T(8,128)(2,1)S(1)}, bf16[1,256,2048]{2,1,0:T(8,128)(2,1)S(1)}) fusion(bf16[2,256,2048]{2,1,0:T(8,128)(2,1)} %get-tuple-element.820, bf16[2,256,2048]{2,1,0:T(8,128)(2,1)} %get-tuple-element.819), kind=kLoop, calls=%fused_computation.114.clone.1 | loop fusion | bytes 8388608 | tf_op jit(solution)/shard_map/while/body/eval_jaxpr/slice | solution.py:75
  125.5 1.1 fusion.152
  130.0 2.9 %fusion.146 = (bf16[1,256,2048]{2,1,0:T(8,128)(2,1)S(1)}, bf16[1,256,2048]{2,1,0:T(8,128)(2,1)S(1)}, bf16[1,256,2048]{2,1,0:T(8,128)(2,1)S(1)}, bf16[1,256,2048]{2,1,0:T(8,128)(2,1)S(1)}) fusion(bf16[2,256,2048]{2,1,0:T(8,128)(2,1)} %get-tuple-element.820, bf16[2,256,2048]{2,1,0:T(8,128)(2,1)} %get-tuple-element.819), kind=kLoop, calls=%fused_computation.114.clone.1 | loop fusion | bytes 8388608 | tf_op jit(solution)/shard_map/while/body/eval_jaxpr/slice | solution.py:75
  135.8 1.1 fusion.152
  140.4 2.9 %fusion.146 = (bf16[1,256,2048]{2,1,0:T(8,128)(2,1)S(1)}, bf16[1,256,2048]{2,1,0:T(8,128)(2,1)S(1)}, bf16[1,256,2048]{2,1,0:T(8,128)(2,1)S(1)}, bf16[1,256,2048]{2,1,0:T(8,128)(2,1)S(1)}) fusion(bf16[2,256,2048]{2,1,0:T(8,128)(2,1)} %get-tuple-element.820, bf16[2,256,2048]{2,1,0:T(8,128)(2,1)} %get-tuple-element.819), kind=kLoop, calls=%fused_computation.114.clone.1 | loop fusion | bytes 8388608 | tf_op jit(solution)/shard_map/while/body/eval_jaxpr/slice | solution.py:75
  146.2 1.1 fusion.152
  150.7 2.9 %fusion.146 = (bf16[1,256,2048]{2,1,0:T(8,128)(2,1)S(1)}, bf16[1,256,2048]{2,1,0:T(8,128)(2,1)S(1)}, bf16[1,256,2048]{2,1,0:T(8,128)(2,1)S(1)}, bf16[1,256,2048]{2,1,0:T(8,128)(2,1)S(1)}) fusion(bf16[2,256,2048]{2,1,0:T(8,128)(2,1)} %get-tuple-element.820, bf16[2,256,2048]{2,1,0:T(8,128)(2,1)} %get-tuple-element.819), kind=kLoop, calls=%fused_computation.114.clone.1 | loop fusion | bytes 8388608 | tf_op jit(solution)/shard_map/while/body/eval_jaxpr/slice | solution.py:75
  156.5 1.1 fusion.152
  161.0 2.9 %fusion.146 = (bf16[1,256,2048]{2,1,0:T(8,128)(2,1)S(1)}, bf16[1,256,2048]{2,1,0:T(8,128)(2,1)S(1)}, bf16[1,256,2048]{2,1,0:T(8,128)(2,1)S(1)}, bf16[1,256,2048]{2,1,0:T(8,128)(2,1)S(1)}) fusion(bf16[2,256,2048]{2,1,0:T(8,128)(2,1)} %get-tuple-element.820, bf16[2,256,2048]{2,1,0:T(8,128)(2,1)} %get-tuple-element.819), kind=kLoop, calls=%fused_computation.114.clone.1 | loop fusion | bytes 8388608 | tf_op jit(solution)/shard_map/while/body/eval_jaxpr/slice | solution.py:75
  171.4 2.9 %fusion.146 = (bf16[1,256,2048]{2,1,0:T(8,128)(2,1)S(1)}, bf16[1,256,2048]{2,1,0:T(8,128)(2,1)S(1)}, bf16[1,256,2048]{2,1,0:T(8,128)(2,1)S(1)}, bf16[1,256,2048]{2,1,0:T(8,128)(2,1)S(1)}) fusion(bf16[2,256,2048]{2,1,0:T(8,128)(2,1)} %get-tuple-element.820, bf16[2,256,2048]{2,1,0:T(8,128)(2,1)} %get-tuple-element.819), kind=kLoop, calls=%fused_computation.114.clone.1 | loop fusion | bytes 8388608 | tf_op jit(solution)/shard_map/while/body/eval_jaxpr/slice | solution.py:75
  181.7 2.9 %fusion.146 = (bf16[1,256,2048]{2,1,0:T(8,128)(2,1)S(1)}, bf16[1,256,2048]{2,1,0:T(8,128)(2,1)S(1)}, bf16[1,256,2048]{2,1,0:T(8,128)(2,1)S(1)}, bf16[1,256,2048]{2,1,0:T(8,128)(2,1)S(1)}) fusion(bf16[2,256,2048]{2,1,0:T(8,128)(2,1)} %get-tuple-element.820, bf16[2,256,2048]{2,1,0:T(8,128)(2,1)} %get-tuple-element.819), kind=kLoop, calls=%fused_computation.114.clone.1 | loop fusion | bytes 8388608 | tf_op jit(solution)/shard_map/while/body/eval_jaxpr/slice | solution.py:75
  192.1 2.9 %fusion.146 = (bf16[1,256,2048]{2,1,0:T(8,128)(2,1)S(1)}, bf16[1,256,2048]{2,1,0:T(8,128)(2,1)S(1)}, bf16[1,256,2048]{2,1,0:T(8,128)(2,1)S(1)}, bf16[1,256,2048]{2,1,0:T(8,128)(2,1)S(1)}) fusion(bf16[2,256,2048]{2,1,0:T(8,128)(2,1)} %get-tuple-element.820, bf16[2,256,2048]{2,1,0:T(8,128)(2,1)} %get-tuple-element.819), kind=kLoop, calls=%fused_computation.114.clone.1 | loop fusion | bytes 8388608 | tf_op jit(solution)/shard_map/while/body/eval_jaxpr/slice | solution.py:75
  202.4 2.9 %fusion.146 = (bf16[1,256,2048]{2,1,0:T(8,128)(2,1)S(1)}, bf16[1,256,2048]{2,1,0:T(8,128)(2,1)S(1)}, bf16[1,256,2048]{2,1,0:T(8,128)(2,1)S(1)}, bf16[1,256,2048]{2,1,0:T(8,128)(2,1)S(1)}) fusion(bf16[2,256,2048]{2,1,0:T(8,128)(2,1)} %get-tuple-element.820, bf16[2,256,2048]{2,1,0:T(8,128)(2,1)} %get-tuple-element.819), kind=kLoop, calls=%fused_computation.114.clone.1 | loop fusion | bytes 8388608 | tf_op jit(solution)/shard_map/while/body/eval_jaxpr/slice | solution.py:75
  212.7 2.9 %fusion.146 = (bf16[1,256,2048]{2,1,0:T(8,128)(2,1)S(1)}, bf16[1,256,2048]{2,1,0:T(8,128)(2,1)S(1)}, bf16[1,256,2048]{2,1,0:T(8,128)(2,1)S(1)}, bf16[1,256,2048]{2,1,0:T(8,128)(2,1)S(1)}) fusion(bf16[2,256,2048]{2,1,0:T(8,128)(2,1)} %get-tuple-element.820, bf16[2,256,2048]{2,1,0:T(8,128)(2,1)} %get-tuple-element.819), kind=kLoop, calls=%fused_computation.114.clone.1 | loop fusion | bytes 8388608 | tf_op jit(solution)/shard_map/while/body/eval_jaxpr/slice | solution.py:75
  223.1 2.9 %fusion.146 = (bf16[1,256,2048]{2,1,0:T(8,128)(2,1)S(1)}, bf16[1,256,2048]{2,1,0:T(8,128)(2,1)S(1)}, bf16[1,256,2048]{2,1,0:T(8,128)(2,1)S(1)}, bf16[1,256,2048]{2,1,0:T(8,128)(2,1)S(1)}) fusion(bf16[2,256,2048]{2,1,0:T(8,128)(2,1)} %get-tuple-element.820, bf16[2,256,2048]{2,1,0:T(8,128)(2,1)} %get-tuple-element.819), kind=kLoop, calls=%fused_computation.114.clone.1 | loop fusion | bytes 8388608 | tf_op jit(solution)/shard_map/while/body/eval_jaxpr/slice | solution.py:75
  233.4 2.9 %fusion.146 = (bf16[1,256,2048]{2,1,0:T(8,128)(2,1)S(1)}, bf16[1,256,2048]{2,1,0:T(8,128)(2,1)S(1)}, bf16[1,256,2048]{2,1,0:T(8,128)(2,1)S(1)}, bf16[1,256,2048]{2,1,0:T(8,128)(2,1)S(1)}) fusion(bf16[2,256,2048]{2,1,0:T(8,128)(2,1)} %get-tuple-element.820, bf16[2,256,2048]{2,1,0:T(8,128)(2,1)} %get-tuple-element.819), kind=kLoop, calls=%fused_computation.114.clone.1 | loop fusion | bytes 8388608 | tf_op jit(solution)/shard_map/while/body/eval_jaxpr/slice | solution.py:75
  243.8 2.9 %fusion.146 = (bf16[1,256,2048]{2,1,0:T(8,128)(2,1)S(1)}, bf16[1,256,2048]{2,1,0:T(8,128)(2,1)S(1)}, bf16[1,256,2048]{2,1,0:T(8,128)(2,1)S(1)}, bf16[1,256,2048]{2,1,0:T(8,128)(2,1)S(1)}) fusion(bf16[2,256,2048]{2,1,0:T(8,128)(2,1)} %get-tuple-element.820, bf16[2,256,2048]{2,1,0:T(8,128)(2,1)} %get-tuple-element.819), kind=kLoop, calls=%fused_computation.114.clone.1 | loop fusion | bytes 8388608 | tf_op jit(solution)/shard_map/while/body/eval_jaxpr/slice | solution.py:75
  254.1 2.9 %fusion.146 = (bf16[1,256,2048]{2,1,0:T(8,128)(2,1)S(1)}, bf16[1,256,2048]{2,1,0:T(8,128)(2,1)S(1)}, bf16[1,256,2048]{2,1,0:T(8,128)(2,1)S(1)}, bf16[1,256,2048]{2,1,0:T(8,128)(2,1)S(1)}) fusion(bf16[2,256,2048]{2,1,0:T(8,128)(2,1)} %get-tuple-element.820, bf16[2,256,2048]{2,1,0:T(8,128)(2,1)} %get-tuple-element.819), kind=kLoop, calls=%fused_computation.114.clone.1 | loop fusion | bytes 8388608 | tf_op jit(solution)/shard_map/while/body/eval_jaxpr/slice | solution.py:75
  264.4 2.9 %fusion.146 = (bf16[1,256,2048]{2,1,0:T(8,128)(2,1)S(1)}, bf16[1,256,2048]{2,1,0:T(8,128)(2,1)S(1)}, bf16[1,256,2048]{2,1,0:T(8,128)(2,1)S(1)}, bf16[1,256,2048]{2,1,0:T(8,128)(2,1)S(1)}) fusion(bf16[2,256,2048]{2,1,0:T(8,128)(2,1)} %get-tuple-element.820, bf16[2,256,2048]{2,1,0:T(8,128)(2,1)} %get-tuple-element.819), kind=kLoop, calls=%fused_computation.114.clone.1 | loop fusion | bytes 8388608 | tf_op jit(solution)/shard_map/while/body/eval_jaxpr/slice | solution.py:75
  274.8 2.9 %fusion.146 = (bf16[1,256,2048]{2,1,0:T(8,128)(2,1)S(1)}, bf16[1,256,2048]{2,1,0:T(8,128)(2,1)S(1)}, bf16[1,256,2048]{2,1,0:T(8,128)(2,1)S(1)}, bf16[1,256,2048]{2,1,0:T(8,128)(2,1)S(1)}) fusion(bf16[2,256,2048]{2,1,0:T(8,128)(2,1)} %get-tuple-element.820, bf16[2,256,2048]{2,1,0:T(8,128)(2,1)} %get-tuple-element.819), kind=kLoop, calls=%fused_computation.114.clone.1 | loop fusion | bytes 8388608 | tf_op jit(solution)/shard_map/while/body/eval_jaxpr/slice | solution.py:75
  (339 shorter events, 112.8 us)
Async XLA Ops:
  1.7 28.3 %collective-permute-start = (bf16[2,256,2048]{2,1,0:T(8,128)(2,1)S(1)}, bf16[2,256,2048]{2,1,0:T(8,128)(2,1)S(1)}, u32[]{:S(2)}, u32[]{:S(2)}) collective-permute-start(bf16[2,256,2048]{2,1,0:T(8,128)(2,1)S(1)} %pad_maximum_fusion), channel_id=1, source_target_pairs={{0,1},{1,2},{2,3},{3,4},{4,5},{5,6},{6,7},{7,8},{8,9},{9,10},{10,1... | collective-permute-start | bytes 6291464 | tf_op jit(solution)/shard_map/ppermute | solution.py:21
  30.0 28.2 %collective-permute-start.1 = (bf16[2,256,2048]{2,1,0:T(8,128)(2,1)S(1)}, bf16[2,256,2048]{2,1,0:T(8,128)(2,1)S(1)}, u32[]{:S(2)}, u32[]{:S(2)}) collective-permute-start(bf16[2,256,2048]{2,1,0:T(8,128)(2,1)S(1)} %collective-permute-done), channel_id=1, source_target_pairs={{0,1},{1,2},{2,3},{3,4},{4,5},{5,6},{6,7},{7,8},{8,9},{9,10},{10,1... | collective-permute-start | bytes 6291464 | tf_op jit(solution)/shard_map/ppermute | solution.py:21
  58.2 1.4 copy-start
  59.6 28.3 %collective-permute-start.2 = (bf16[2,256,2048]{2,1,0:T(8,128)(2,1)S(1)}, bf16[2,256,2048]{2,1,0:T(8,128)(2,1)}, u32[]{:S(2)}, u32[]{:S(2)}) collective-permute-start(bf16[2,256,2048]{2,1,0:T(8,128)(2,1)S(1)} %collective-permute-done.1), channel_id=1, source_target_pairs={{0,1},{1,2},{2,3},{3,4},{4,5},{5,6},{6,7},{7,8},{8,9},{9,10},{10,1... | collective-permute-start | bytes 6291464 | tf_op jit(solution)/shard_map/ppermute | solution.py:21
  87.9 28.6 %collective-permute-start.3 = (bf16[2,256,2048]{2,1,0:T(8,128)(2,1)}, bf16[2,256,2048]{2,1,0:T(8,128)(2,1)}, u32[]{:S(2)}, u32[]{:S(2)}) collective-permute-start(bf16[2,256,2048]{2,1,0:T(8,128)(2,1)} %collective-permute-done.2), channel_id=1, source_target_pairs={{0,1},{1,2},{2,3},{3,4},{4,5},{5,6},{6,7},{7,8},{8,9},{9,10},{10,1... | collective-permute-start | bytes 6291464 | tf_op jit(solution)/shard_map/ppermute | solution.py:21
  119.7 3.4 %copy-start.1 = (bf16[2,256,2048]{2,1,0:T(8,128)(2,1)S(1)}, bf16[2,256,2048]{2,1,0:T(8,128)(2,1)}, u32[]{:S(2)}) copy-start(bf16[2,256,2048]{2,1,0:T(8,128)(2,1)} %get-tuple-element.818) | copy-start | bytes 6291460 | tf_op jit(solution)/shard_map/while
  130.0 3.4 %copy-start.1 = (bf16[2,256,2048]{2,1,0:T(8,128)(2,1)S(1)}, bf16[2,256,2048]{2,1,0:T(8,128)(2,1)}, u32[]{:S(2)}) copy-start(bf16[2,256,2048]{2,1,0:T(8,128)(2,1)} %get-tuple-element.818) | copy-start | bytes 6291460 | tf_op jit(solution)/shard_map/while
  140.3 3.4 %copy-start.1 = (bf16[2,256,2048]{2,1,0:T(8,128)(2,1)S(1)}, bf16[2,256,2048]{2,1,0:T(8,128)(2,1)}, u32[]{:S(2)}) copy-start(bf16[2,256,2048]{2,1,0:T(8,128)(2,1)} %get-tuple-element.818) | copy-start | bytes 6291460 | tf_op jit(solution)/shard_map/while
  150.7 3.4 %copy-start.1 = (bf16[2,256,2048]{2,1,0:T(8,128)(2,1)S(1)}, bf16[2,256,2048]{2,1,0:T(8,128)(2,1)}, u32[]{:S(2)}) copy-start(bf16[2,256,2048]{2,1,0:T(8,128)(2,1)} %get-tuple-element.818) | copy-start | bytes 6291460 | tf_op jit(solution)/shard_map/while
  161.0 3.4 %copy-start.1 = (bf16[2,256,2048]{2,1,0:T(8,128)(2,1)S(1)}, bf16[2,256,2048]{2,1,0:T(8,128)(2,1)}, u32[]{:S(2)}) copy-start(bf16[2,256,2048]{2,1,0:T(8,128)(2,1)} %get-tuple-element.818) | copy-start | bytes 6291460 | tf_op jit(solution)/shard_map/while
  171.4 3.4 %copy-start.1 = (bf16[2,256,2048]{2,1,0:T(8,128)(2,1)S(1)}, bf16[2,256,2048]{2,1,0:T(8,128)(2,1)}, u32[]{:S(2)}) copy-start(bf16[2,256,2048]{2,1,0:T(8,128)(2,1)} %get-tuple-element.818) | copy-start | bytes 6291460 | tf_op jit(solution)/shard_map/while
  181.7 3.4 %copy-start.1 = (bf16[2,256,2048]{2,1,0:T(8,128)(2,1)S(1)}, bf16[2,256,2048]{2,1,0:T(8,128)(2,1)}, u32[]{:S(2)}) copy-start(bf16[2,256,2048]{2,1,0:T(8,128)(2,1)} %get-tuple-element.818) | copy-start | bytes 6291460 | tf_op jit(solution)/shard_map/while
  192.1 3.4 %copy-start.1 = (bf16[2,256,2048]{2,1,0:T(8,128)(2,1)S(1)}, bf16[2,256,2048]{2,1,0:T(8,128)(2,1)}, u32[]{:S(2)}) copy-start(bf16[2,256,2048]{2,1,0:T(8,128)(2,1)} %get-tuple-element.818) | copy-start | bytes 6291460 | tf_op jit(solution)/shard_map/while
  202.4 3.4 %copy-start.1 = (bf16[2,256,2048]{2,1,0:T(8,128)(2,1)S(1)}, bf16[2,256,2048]{2,1,0:T(8,128)(2,1)}, u32[]{:S(2)}) copy-start(bf16[2,256,2048]{2,1,0:T(8,128)(2,1)} %get-tuple-element.818) | copy-start | bytes 6291460 | tf_op jit(solution)/shard_map/while
  212.7 3.4 %copy-start.1 = (bf16[2,256,2048]{2,1,0:T(8,128)(2,1)S(1)}, bf16[2,256,2048]{2,1,0:T(8,128)(2,1)}, u32[]{:S(2)}) copy-start(bf16[2,256,2048]{2,1,0:T(8,128)(2,1)} %get-tuple-element.818) | copy-start | bytes 6291460 | tf_op jit(solution)/shard_map/while
  223.1 3.4 %copy-start.1 = (bf16[2,256,2048]{2,1,0:T(8,128)(2,1)S(1)}, bf16[2,256,2048]{2,1,0:T(8,128)(2,1)}, u32[]{:S(2)}) copy-start(bf16[2,256,2048]{2,1,0:T(8,128)(2,1)} %get-tuple-element.818) | copy-start | bytes 6291460 | tf_op jit(solution)/shard_map/while
  233.4 3.4 %copy-start.1 = (bf16[2,256,2048]{2,1,0:T(8,128)(2,1)S(1)}, bf16[2,256,2048]{2,1,0:T(8,128)(2,1)}, u32[]{:S(2)}) copy-start(bf16[2,256,2048]{2,1,0:T(8,128)(2,1)} %get-tuple-element.818) | copy-start | bytes 6291460 | tf_op jit(solution)/shard_map/while
  243.8 3.4 %copy-start.1 = (bf16[2,256,2048]{2,1,0:T(8,128)(2,1)S(1)}, bf16[2,256,2048]{2,1,0:T(8,128)(2,1)}, u32[]{:S(2)}) copy-start(bf16[2,256,2048]{2,1,0:T(8,128)(2,1)} %get-tuple-element.818) | copy-start | bytes 6291460 | tf_op jit(solution)/shard_map/while
  254.1 3.4 %copy-start.1 = (bf16[2,256,2048]{2,1,0:T(8,128)(2,1)S(1)}, bf16[2,256,2048]{2,1,0:T(8,128)(2,1)}, u32[]{:S(2)}) copy-start(bf16[2,256,2048]{2,1,0:T(8,128)(2,1)} %get-tuple-element.818) | copy-start | bytes 6291460 | tf_op jit(solution)/shard_map/while
  264.4 3.4 %copy-start.1 = (bf16[2,256,2048]{2,1,0:T(8,128)(2,1)S(1)}, bf16[2,256,2048]{2,1,0:T(8,128)(2,1)}, u32[]{:S(2)}) copy-start(bf16[2,256,2048]{2,1,0:T(8,128)(2,1)} %get-tuple-element.818) | copy-start | bytes 6291460 | tf_op jit(solution)/shard_map/while
  274.8 3.4 %copy-start.1 = (bf16[2,256,2048]{2,1,0:T(8,128)(2,1)S(1)}, bf16[2,256,2048]{2,1,0:T(8,128)(2,1)}, u32[]{:S(2)}) copy-start(bf16[2,256,2048]{2,1,0:T(8,128)(2,1)} %get-tuple-element.818) | copy-start | bytes 6291460 | tf_op jit(solution)/shard_map/while
where the time goes:
time: 285 us; the launch traced here: 284 us
  waiting for transfers between devices  106 us (37%)
  local copies, waits for them, and re-layouts  82.8 us (29%)
  matrix products  65.3 us (23%)
  other arithmetic  20 us (7%)
  starting transfers between devices  7.65 us (3%)
    ppermute x4, waiting for transfers between devices, passed_along(): return lax.ppermute(shard, axis, pairs)  106 us
    slice x32, local copies, waits for them, and re-layouts, head_count_ratio(): arrived[hop_count][1]  51.3 us
    dot_general x80, matrix products, head_count_ratio(): jnp.einsum('gtk,kd->tgd', weights_full.astype(jnp.bfloat16), value_head,...  33.7 us
    dot_general x80, matrix products, head_count_ratio(): jnp.einsum('tgd,kd->gtk', query_head, key_head, preferred_element_type=jn...  31.6 us
    dynamic_slice x32, local copies, waits for them, and re-layouts, head_count_ratio(): lax.dynamic_slice_in_dim(queries, head_index * query_groups * HEAD_WIDTH,...  16.2 us
    dynamic_update_slice x32, local copies, waits for them, and re-layouts, head_count_ratio(): lax.dynamic_update_slice_in_dim(output, result, head_index * query_groups...  12.3 us
    and x16, other arithmetic, visible_pairs(): (key_pos[None, :] <= query_pos[:, None]) & (key_pos[None, :] > query_pos[...  9.25 us
    reduce_sum x16, other arithmetic, head_count_ratio(): row_total = row_total + jnp.sum(weights_full, axis=2)  8.73 us
  transfers between devices with their start and end apart: 4, of which 4 were waited for; matrix products, arithmetic and copies ran while one was open for 0% of the time, Pallas kernels for 0%

commit v1 on v0

v1 whole, which is shorter than its diff:
```python
import functools

import jax
import jax.numpy as jnp
from jax import lax
from jax.experimental import pallas as pl
from jax.experimental.pallas import tpu as pltpu
from jax.sharding import PartitionSpec as P

QUERY_HEADS = 32
KEY_VALUE_HEADS = 16
HEAD_WIDTH = 128
WINDOW = 1024
GROUP = QUERY_HEADS // KEY_VALUE_HEADS

score_scale = 168.0 ** (-0.5)
LOG2_E = 1.4426950408889634
masked_value = -1e30
ROWS = 64
CHUNKS = (5, 5, 4, 2)


def attend_kernel(block_ref, q_ref, own_ref, far_ref, mid_ref, pair1_ref, pair2_ref, *rest):
    o_ref = rest[-1]
    length = q_ref.shape[0]
    block = block_ref[0]
    odd = lax.rem(block, 2)

    def bias_of(back):
        return jnp.where(block >= back, 0.0, masked_value).astype(jnp.float32)

    far_bias = bias_of(4)
    biases = (0.0, bias_of(2), bias_of(3 - 2 * odd), bias_of(1 + 2 * odd))
    refs = (own_ref, far_ref, mid_ref, pair1_ref, pair2_ref)
    across = (((1,), (1,)), ((), ()))
    scale = score_scale * LOG2_E
    for start in range(0, length, ROWS):
        rows = slice(start, start + ROWS)
        query = jnp.concatenate(
            [q_ref[rows, g * HEAD_WIDTH : (g + 1) * HEAD_WIDTH] for g in range(GROUP)], axis=0
        )
        raw = [
            lax.dot_general(query, ref[0], across, preferred_element_type=jnp.float32)
            for ref in refs
        ]
        query_pos = lax.broadcasted_iota(jnp.int32, (ROWS, length), 0) + start
        key_pos = lax.broadcasted_iota(jnp.int32, (ROWS, length), 1)
        causal = jnp.concatenate([key_pos <= query_pos] * GROUP, axis=0)
        scores = [jnp.where(causal, raw[0], raw[1] + far_bias)] + raw[2:]
        row_max = functools.reduce(
            jnp.maximum,
            [jnp.max(s, axis=1, keepdims=True) + b for s, b in zip(scores, biases)],
        )
        weights = [jnp.exp2(s * scale + (b - row_max) * scale) for s, b in zip(scores, biases)]
        own_weights = jnp.where(causal, weights[0], 0.0)
        far_weights = jnp.where(causal, 0.0, weights[0])
        weights = [
            w.astype(jnp.bfloat16) for w in [own_weights, far_weights] + weights[1:]
        ]
        values = jnp.concatenate([ref[1] for ref in refs], axis=0)
        values = jnp.concatenate([values, jnp.ones_like(values)], axis=1)
        weighted = jnp.dot(
            jnp.concatenate(weights, axis=1), values, preferred_element_type=jnp.float32
        )
        result = weighted[:, :HEAD_WIDTH] / weighted[:, HEAD_WIDTH:]
        for g in range(GROUP):
            o_ref[rows, g * HEAD_WIDTH : (g + 1) * HEAD_WIDTH] = result[
                g * ROWS : (g + 1) * ROWS
            ].astype(o_ref.dtype)


def attend(block, queries, pieces, first, heads, output):
    length = queries.shape[0]
    kv_spec = pl.BlockSpec((2, length, HEAD_WIDTH), lambda h: (0, 0, h))
    q_spec = pl.BlockSpec((length, GROUP * HEAD_WIDTH), lambda h: (0, h + first))
    specs = [pl.BlockSpec(memory_space=pltpu.SMEM), q_spec] + [kv_spec] * len(pieces)
    args = [block, queries, *pieces]
    aliases = {}
    if output is not None:
        aliases = {len(args): 0}
        specs.append(pl.BlockSpec(memory_space=pl.ANY))
        args.append(output)
    keys = len(pieces) * length
    return pl.pallas_call(
        attend_kernel,
        name=f"attend_{first}",
        out_shape=jax.ShapeDtypeStruct(queries.shape, queries.dtype),
        grid=(heads,),
        in_specs=specs,
        out_specs=q_spec,
        input_output_aliases=aliases,
        compiler_params=pltpu.CompilerParams(vmem_limit_bytes=24 << 20),
        cost_estimate=pl.CostEstimate(
            flops=heads * GROUP * length * keys * HEAD_WIDTH * 4,
            transcendentals=heads * GROUP * length * WINDOW,
            bytes_accessed=heads * HEAD_WIDTH * length * 2 * (2 * len(pieces) + 2 * GROUP),
        ),
    )(*args)


def per_device(queries, key_rows, value_matrix):
    length = queries.shape[0]
    devices = lax.axis_size("seq")
    assert WINDOW == 4 * length and devices % 4 == 0
    far = [(i, i + 4) for i in range(devices - 4)]
    swap = [(i, i + 2 if i % 4 < 2 else i - 2) for i in range(devices)]
    pair = [(i, i ^ 1) for i in range(devices)]
    block = lax.axis_index("seq")
    upper = lax.rem(block, 4) >= 2
    odd = lax.rem(block, 2) == 1
    block = block.astype(jnp.int32).reshape(1)

    bounds = [0]
    for heads in CHUNKS:
        bounds.append(bounds[-1] + heads)
    assert bounds[-1] == KEY_VALUE_HEADS
    own = []
    for first, last in zip(bounds, bounds[1:]):
        columns = slice(first * HEAD_WIDTH, last * HEAD_WIDTH)
        own.append(jnp.stack([key_rows[:, columns], value_matrix[:, columns]]))
    from_far = [lax.ppermute(piece, "seq", far) for piece in own]
    output = None
    for chunk, heads in enumerate(CHUNKS):
        mine, distant = own[chunk], from_far[chunk]
        middle = lax.ppermute(jnp.where(upper, distant, mine), "seq", swap)
        pair1 = lax.ppermute(jnp.where(odd, distant, mine), "seq", pair)
        pair2 = lax.ppermute(middle, "seq", pair)
        output = attend(
            block, queries, (mine, distant, middle, pair1, pair2), bounds[chunk], heads, output
        )
    return output


def solution(mesh):
    return jax.shard_map(
        per_device,
        mesh=mesh,
        in_specs=(
            P(("groups", "seq"), None),
            P(("groups", "seq"), None),
            P(("groups", "seq"), None),
        ),
        out_specs=P(("groups", "seq"), None),
        check_vma=False,
    )
```

time: 285 us -> 93.1 us (0.33)
  local copies, waits for them, and re-layouts: 82.8 us -> 5.02 us
  matrix products: 65.3 us -> 0 us
  waiting for transfers between devices: 106 us -> 44.5 us
  Pallas kernels: 0 us -> 26.7 us
  other arithmetic: 20 us -> 2.74 us
  starting transfers between devices: 7.65 us -> 13.1 us
    dot_general x160 -> x0, matrix products: 65.3 us -> none  [the longest x80 33.7 us: head_count_ratio(): jnp.einsum('gtk,kd->tgd', weights_full.astype(jnp.bfloat16), value_head,...]
    ppermute x4 -> x16, waiting for transfers between devices: 106 us -> 44.5 us  [the longest x4 41.6 us: per_device(): from_far = [lax.ppermute(piece, 'seq', far) for piece in own]]
    slice x32 -> x0, local copies, waits for them, and re-layouts: 51.3 us -> none  [head_count_ratio(): arrived[hop_count][1]]
    pallas_call x0 -> x4, Pallas kernels: none -> 26.7 us  [attend(): pl.pallas_call(attend_kernel, name=f'attend_{first}', out_shape=jax.Shape...]
    dynamic_slice x32 -> x0, local copies, waits for them, and re-layouts: 16.2 us -> none  [head_count_ratio(): lax.dynamic_slice_in_dim(queries, head_index * query_groups * HEAD_WIDTH,...]
    dynamic_update_slice x32 -> x0, local copies, waits for them, and re-layouts: 12.3 us -> none  [head_count_ratio(): lax.dynamic_update_slice_in_dim(output, result, head_index * query_groups...]
    and x16 -> x0, other arithmetic: 9.25 us -> none  [visible_pairs(): (key_pos[None, :] <= query_pos[:, None]) & (key_pos[None, :] > query_pos[...]
    reduce_sum x16 -> x0, other arithmetic: 8.73 us -> none  [head_count_ratio(): row_total = row_total + jnp.sum(weights_full, axis=2)]
  transfers between devices with their start and end apart: 4 -> 16, of which waited for: 4 -> 5; matrix products, arithmetic and copies ran while one was open for 0% -> 5% of each run, Pallas kernels for 0% -> 25%
where the time goes in v1:
time: 93.1 us; the launch traced here: 92.2 us
  waiting for transfers between devices  44.5 us (48%)
  Pallas kernels  26.7 us (29%)
  starting transfers between devices  13.1 us (14%)
  local copies, waits for them, and re-layouts  5.02 us (5%)
  other arithmetic  2.74 us (3%)
    ppermute x4, waiting for transfers between devices, per_device(): from_far = [lax.ppermute(piece, 'seq', far) for piece in own]  41.6 us
    pallas_call x4, Pallas kernels, attend(): pl.pallas_call(attend_kernel, name=f'attend_{first}', out_shape=jax.Shape...  26.7 us
    ppermute x4, starting transfers between devices, per_device(): middle = lax.ppermute(jnp.where(upper, distant, mine), 'seq', swap)  6.34 us
    ppermute x4, starting transfers between devices, per_device(): from_far = [lax.ppermute(piece, 'seq', far) for piece in own]  5.16 us
    another operation x3, local copies, waits for them, and re-layouts, per_device(): own.append(jnp.stack([key_rows[:, columns], value_matrix[:, columns]]))  3.45 us
    ppermute x4, waiting for transfers between devices, per_device(): middle = lax.ppermute(jnp.where(upper, distant, mine), 'seq', swap)  2.95 us
    select_n x4, other arithmetic, per_device(): pair1 = lax.ppermute(jnp.where(odd, distant, mine), 'seq', pair)  2.52 us
  transfers between devices with their start and end apart: 16, of which 5 were waited for; matrix products, arithmetic and copies ran while one was open for 5% of the time, Pallas kernels for 25%

profile of v1, /device:TPU:26, one launch (start us, length us, event | category | flops | bytes accessed | tf_op | source)
XLA Modules:
  0.0 92.2 jit_solution(13833629958622020771)
XLA Ops:
  0.0 1.4 %slice_bitcast_fusion = (bf16[1,256,640]{2,1,0:T(8,128)(2,1)S(1)}, bf16[1,256,640]{2,1,0:T(8,128)(2,1)S(1)}, bf16[1,256,640]{2,1,0:T(8,128)(2,1)S(1)}, bf16[1,256,640]{2,1,0:T(8,128)(2,1)S(1)}) fusion(bf16[256,2048]{1,0:T(8,128)(2,1)} %param.5, bf16[256,2048]{1,0:T(8,128)(2,1)} %param.4), kind=kLoop, calls=%fused_computation.9 | loop fusion | bytes 2621440 | tf_op jit(solution)/shard_map/stack | solution.py:120
  1.4 0.7 copy-done.3
  2.1 0.1 copy-done.4
  2.2 0.1 pad_maximum_fusion.1.own_ref
  2.3 1.3 %collective-permute-start.12 = (bf16[2,256,640]{2,1,0:T(8,128)(2,1)S(1)}, bf16[2,256,640]{2,1,0:T(8,128)(2,1)S(1)}, u32[]{:S(2)}, u32[]{:S(2)}) collective-permute-start(bf16[2,256,640]{2,1,0:T(8,128)(2,1)S(1)} %pad_maximum_fusion.1.own_ref), channel_id=1, source_target_pairs={{0,4},{1,5},{2,6},{3,7},{4,8},{5,9},{6,10},{7,11},{8,12},{9,13},{1... | collective-permute-start | bytes 1966088 | tf_op jit(solution)/shard_map/ppermute | solution.py:121
  3.6 0.1 pad_maximum_fusion.own_ref
  3.7 1.3 %collective-permute-start.8 = (bf16[2,256,640]{2,1,0:T(8,128)(2,1)S(1)}, bf16[2,256,640]{2,1,0:T(8,128)(2,1)S(1)}, u32[]{:S(2)}, u32[]{:S(2)}) collective-permute-start(bf16[2,256,640]{2,1,0:T(8,128)(2,1)S(1)} %pad_maximum_fusion.own_ref), channel_id=1, source_target_pairs={{0,4},{1,5},{2,6},{3,7},{4,8},{5,9},{6,10},{7,11},{8,12},{9,13},{1... | collective-permute-start | bytes 1966088 | tf_op jit(solution)/shard_map/ppermute | solution.py:121
  5.0 1.1 %slice_bitcast_fusion.4 = (bf16[1,256,512]{2,1,0:T(8,128)(2,1)S(1)}, bf16[1,256,512]{2,1,0:T(8,128)(2,1)S(1)}) fusion(bf16[256,2048]{1,0:T(8,128)(2,1)} %param.5, bf16[256,2048]{1,0:T(8,128)(2,1)} %param.4), kind=kLoop, calls=%fused_computation.14 | loop fusion | bytes 1048576 | tf_op jit(solution)/shard_map/stack | solution.py:120
  6.1 0.7 copy-done.5
  6.9 1.3 %collective-permute-start.4 = (bf16[2,256,512]{2,1,0:T(8,128)(2,1)S(1)}, bf16[2,256,512]{2,1,0:T(8,128)(2,1)}, u32[]{:S(2)}, u32[]{:S(2)}) collective-permute-start(bf16[2,256,512]{2,1,0:T(8,128)(2,1)S(1)} %pad_maximum_fusion.2.own_ref), channel_id=1, source_target_pairs={{0,4},{1,5},{2,6},{3,7},{4,8},{5,9},{6,10},{7,11},{8,12},{9,13},{1... | collective-permute-start | bytes 1572872 | tf_op jit(solution)/shard_map/ppermute | solution.py:121
  8.2 13.6 %collective-permute-done.12.far_ref = bf16[2,256,640]{2,1,0:T(8,128)(2,1)S(1)} collective-permute-done((bf16[2,256,640]{2,1,0:T(8,128)(2,1)S(1)}, bf16[2,256,640]{2,1,0:T(8,128)(2,1)S(1)}, u32[]{:S(2)}, u32[]{:S(2)}) %collective-permute-start.12) | collective-permute-done | bytes 655392 | tf_op jit(solution)/shard_map/ppermute | solution.py:121
  21.8 1.2 %broadcast_select_fusion = (bf16[2,256,640]{2,1,0:T(8,128)(2,1)S(1)}, bf16[2,256,640]{2,1,0:T(8,128)(2,1)S(1)}) fusion(bf16[2,256,640]{2,1,0:T(8,128)(2,1)S(1)} %collective-permute-done.12.far_ref, pred[]{:T(512)S(6)} %eq.3, bf16[1,256,640]{2,1,0:T(8,128)(2,1)} %copy-done.3, bf16[1,256,640]{2,1,0:T(8,128)(2,1)} %copy-done.4, pred[]{:T(512)S(6)} %ge.3), kind=kLoop, calls=%fused_computation.2 | loop fusion | flops 983040 | bytes 2621442 | tf_op jit(solution)/shard_map/jit(_where)/select_n | solution.py:126
  23.1 1.6 %collective-permute-start.13 = (bf16[2,256,640]{2,1,0:T(8,128)(2,1)S(1)}, bf16[2,256,640]{2,1,0:T(8,128)(2,1)S(1)}, u32[]{:S(2)}, u32[]{:S(2)}) collective-permute-start(bf16[2,256,640]{2,1,0:T(8,128)(2,1)S(1)} %get-tuple-element.6), channel_id=1, source_target_pairs={{0,2},{1,3},{2,0},{3,1},{4,6},{5,7},{6,4},{7,5},{8,10},{9,11},{10,... | collective-permute-start | bytes 1966088 | tf_op jit(solution)/shard_map/ppermute | solution.py:125
  24.6 11.2 %collective-permute-done.8.far_ref = bf16[2,256,640]{2,1,0:T(8,128)(2,1)S(1)} collective-permute-done((bf16[2,256,640]{2,1,0:T(8,128)(2,1)S(1)}, bf16[2,256,640]{2,1,0:T(8,128)(2,1)S(1)}, u32[]{:S(2)}, u32[]{:S(2)}) %collective-permute-start.8) | collective-permute-done | bytes 655392 | tf_op jit(solution)/shard_map/ppermute | solution.py:121
  35.9 0.2 broadcast_select_fusion.1
  36.0 1.6 %collective-permute-start.9 = (bf16[2,256,640]{2,1,0:T(8,128)(2,1)S(1)}, bf16[2,256,640]{2,1,0:T(8,128)(2,1)S(1)}, u32[]{:S(2)}, u32[]{:S(2)}) collective-permute-start(bf16[2,256,640]{2,1,0:T(8,128)(2,1)S(1)} %get-tuple-element.8), channel_id=1, source_target_pairs={{0,2},{1,3},{2,0},{3,1},{4,6},{5,7},{6,4},{7,5},{8,10},{9,11},{10,... | collective-permute-start | bytes 1966088 | tf_op jit(solution)/shard_map/ppermute | solution.py:125
  37.6 1.0 %slice_bitcast_fusion.6 = (bf16[1,256,256]{2,1,0:T(8,128)(2,1)S(1)}, bf16[1,256,256]{2,1,0:T(8,128)(2,1)S(1)}) fusion(bf16[256,2048]{1,0:T(8,128)(2,1)} %param.5, bf16[256,2048]{1,0:T(8,128)(2,1)} %param.4), kind=kLoop, calls=%fused_computation.18 | loop fusion | bytes 524288 | tf_op jit(solution)/shard_map/stack | solution.py:120
  38.6 0.1 collective-permute-start.14
  38.7 7.4 %collective-permute-done.4.far_ref = bf16[2,256,512]{2,1,0:T(8,128)(2,1)} collective-permute-done((bf16[2,256,512]{2,1,0:T(8,128)(2,1)S(1)}, bf16[2,256,512]{2,1,0:T(8,128)(2,1)}, u32[]{:S(2)}, u32[]{:S(2)}) %collective-permute-start.4) | collective-permute-done | bytes 524320 | tf_op jit(solution)/shard_map/ppermute | solution.py:121
  46.1 1.1 %broadcast_select_fusion.4 = (bf16[2,256,512]{2,1,0:T(8,128)(2,1)S(1)}, bf16[2,256,512]{2,1,0:T(8,128)(2,1)S(1)}) fusion(bf16[2,256,512]{2,1,0:T(8,128)(2,1)} %collective-permute-done.4.far_ref, pred[]{:T(512)S(6)} %eq.3, bf16[1,256,512]{2,1,0:T(8,128)(2,1)S(1)} %copy-done.6, bf16[1,256,512]{2,1,0:T(8,128)(2,1)S(1)} %copy-done.8, pred[]{:T(512)S(6)} %ge.3), kind=kLoop, calls=%fused_computation.7 | loop fusion | flops 786432 | bytes 2097154 | tf_op jit(solution)/shard_map/jit(_where)/select_n | solution.py:126
  47.2 1.6 %collective-permute-start.5 = (bf16[2,256,512]{2,1,0:T(8,128)(2,1)S(1)}, bf16[2,256,512]{2,1,0:T(8,128)(2,1)S(1)}, u32[]{:S(2)}, u32[]{:S(2)}) collective-permute-start(bf16[2,256,512]{2,1,0:T(8,128)(2,1)S(1)} %get-tuple-element.14), channel_id=1, source_target_pairs={{0,2},{1,3},{2,0},{3,1},{4,6},{5,7},{6,4},{7,5},{8,10},{9,11},{10,... | collective-permute-start | bytes 1572872 | tf_op jit(solution)/shard_map/ppermute | solution.py:125
  48.8 1.3 %collective-permute-start = (bf16[2,256,256]{2,1,0:T(8,128)(2,1)S(1)}, bf16[2,256,256]{2,1,0:T(8,128)(2,1)S(1)}, u32[]{:S(2)}, u32[]{:S(2)}) collective-permute-start(bf16[2,256,256]{2,1,0:T(8,128)(2,1)S(1)} %pad_maximum_fusion.3.own_ref), channel_id=1, source_target_pairs={{0,4},{1,5},{2,6},{3,7},{4,8},{5,9},{6,10},{7,11},{8,12},{9,13},{1... | collective-permute-start | bytes 786440 | tf_op jit(solution)/shard_map/ppermute | solution.py:121
  50.1 9.3 %collective-permute-done.far_ref = bf16[2,256,256]{2,1,0:T(8,128)(2,1)S(1)} collective-permute-done((bf16[2,256,256]{2,1,0:T(8,128)(2,1)S(1)}, bf16[2,256,256]{2,1,0:T(8,128)(2,1)S(1)}, u32[]{:S(2)}, u32[]{:S(2)}) %collective-permute-start) | collective-permute-done | bytes 262176 | tf_op jit(solution)/shard_map/ppermute | solution.py:121
  59.4 0.5 collective-permute-start.11
  59.9 2.9 %collective-permute-done.5.mid_ref = bf16[2,256,512]{2,1,0:T(8,128)(2,1)S(1)} collective-permute-done((bf16[2,256,512]{2,1,0:T(8,128)(2,1)S(1)}, bf16[2,256,512]{2,1,0:T(8,128)(2,1)S(1)}, u32[]{:S(2)}, u32[]{:S(2)}) %collective-permute-start.5) | collective-permute-done | bytes 524320 | tf_op jit(solution)/shard_map/ppermute | solution.py:125
  62.9 0.5 collective-permute-start.7
  63.5 1.6 %collective-permute-start.1 = (bf16[2,256,256]{2,1,0:T(8,128)(2,1)S(1)}, bf16[2,256,256]{2,1,0:T(8,128)(2,1)S(1)}, u32[]{:S(2)}, u32[]{:S(2)}) collective-permute-start(bf16[2,256,256]{2,1,0:T(8,128)(2,1)S(1)} %get-tuple-element.16), channel_id=1, source_target_pairs={{0,2},{1,3},{2,0},{3,1},{4,6},{5,7},{6,4},{7,5},{8,10},{9,11},{10,... | collective-permute-start | bytes 786440 | tf_op jit(solution)/shard_map/ppermute | solution.py:125
  65.0 7.9 %attend_0.1.rest_0_ = bf16[256,4096]{1,0:T(8,128)(2,1)} custom-call(s32[1]{0:T(128)} %bitcast.block_ref, bf16[256,4096]{1,0:T(8,128)(2,1)S(1)} %copy-done, bf16[2,256,640]{2,1,0:T(8,128)(2,1)S(1)} %pad_maximum_fusion.1.own_ref, bf16[2,256,640]{2,1,0:T(8,128)(2,1)S(1)} %collective-permute-done.12.far_ref, ...), custom_call_target="tpu_custom_call" | custom-call | flops 1677721600 | bytes 4587520 | tf_op jit(solution)/shard_map/attend_0/pallas_call | solution.py:84
  73.0 0.5 collective-permute-start.3
  73.5 8.0 %attend_5.1.rest_0_ = bf16[256,4096]{1,0:T(8,128)(2,1)} custom-call(s32[1]{0:T(128)} %bitcast.block_ref, bf16[256,4096]{1,0:T(8,128)(2,1)S(1)} %copy-done, bf16[2,256,640]{2,1,0:T(8,128)(2,1)S(1)} %pad_maximum_fusion.own_ref, bf16[2,256,640]{2,1,0:T(8,128)(2,1)S(1)} %collective-permute-done.8.far_ref, ...), custom_call_target="tpu_custom_call", output_to_operand_aliasing={{}: (7, {})} | custom-call | flops 1677721600 | bytes 4587520 | tf_op jit(solution)/shard_map/attend_5/pallas_call | solution.py:84
  81.5 7.1 %attend_10.1.rest_0_ = bf16[256,4096]{1,0:T(8,128)(2,1)} custom-call(s32[1]{0:T(128)} %bitcast.block_ref, bf16[256,4096]{1,0:T(8,128)(2,1)S(1)} %copy-done, bf16[2,256,512]{2,1,0:T(8,128)(2,1)S(1)} %pad_maximum_fusion.2.own_ref, bf16[2,256,512]{2,1,0:T(8,128)(2,1)} %collective-permute-done.4.far_ref, ...), custom_call_target="tpu_custom_call", output_to_operand_aliasing={{}: (7, {})} | custom-call | flops 1342177280 | bytes 3670016 | tf_op jit(solution)/shard_map/attend_10/pallas_call | solution.py:84
  88.6 3.6 %attend_14.1 = bf16[256,4096]{1,0:T(8,128)(2,1)} custom-call(s32[1]{0:T(128)} %bitcast.block_ref, bf16[256,4096]{1,0:T(8,128)(2,1)S(1)} %copy-done, bf16[2,256,256]{2,1,0:T(8,128)(2,1)S(1)} %pad_maximum_fusion.3.own_ref, bf16[2,256,256]{2,1,0:T(8,128)(2,1)S(1)} %collective-permute-done.far_ref, ...), custom_call_target="tpu_custom_call", output_to_operand_aliasing={{}: (7, {})} | custom-call | flops 671088640 | bytes 1835008 | tf_op jit(solution)/shard_map/attend_14/pallas_call | solution.py:84
  (33 shorter events, 0.2 us)
Async XLA Ops:
  1.4 0.7 copy-start.3
  1.4 0.8 copy-start.4
  1.4 4.7 %copy-start.1 = (bf16[1,256,640]{2,1,0:T(8,128)(2,1)}, bf16[1,256,640]{2,1,0:T(8,128)(2,1)S(1)}, u32[]{:S(2)}) copy-start(bf16[1,256,640]{2,1,0:T(8,128)(2,1)S(1)} %get-tuple-element.21) | copy-start | bytes 983044
  2.3 19.5 %collective-permute-start.12 = (bf16[2,256,640]{2,1,0:T(8,128)(2,1)S(1)}, bf16[2,256,640]{2,1,0:T(8,128)(2,1)S(1)}, u32[]{:S(2)}, u32[]{:S(2)}) collective-permute-start(bf16[2,256,640]{2,1,0:T(8,128)(2,1)S(1)} %pad_maximum_fusion.1.own_ref), channel_id=1, source_target_pairs={{0,4},{1,5},{2,6},{3,7},{4,8},{5,9},{6,10},{7,11},{8,12},{9,13},{1... | collective-permute-start | bytes 1966088 | tf_op jit(solution)/shard_map/ppermute | solution.py:121
  3.7 32.2 %collective-permute-start.8 = (bf16[2,256,640]{2,1,0:T(8,128)(2,1)S(1)}, bf16[2,256,640]{2,1,0:T(8,128)(2,1)S(1)}, u32[]{:S(2)}, u32[]{:S(2)}) collective-permute-start(bf16[2,256,640]{2,1,0:T(8,128)(2,1)S(1)} %pad_maximum_fusion.own_ref), channel_id=1, source_target_pairs={{0,4},{1,5},{2,6},{3,7},{4,8},{5,9},{6,10},{7,11},{8,12},{9,13},{1... | collective-permute-start | bytes 1966088 | tf_op jit(solution)/shard_map/ppermute | solution.py:121
  6.1 0.7 copy-start.5
  6.1 0.8 copy-start.7
  6.9 39.2 %collective-permute-start.4 = (bf16[2,256,512]{2,1,0:T(8,128)(2,1)S(1)}, bf16[2,256,512]{2,1,0:T(8,128)(2,1)}, u32[]{:S(2)}, u32[]{:S(2)}) collective-permute-start(bf16[2,256,512]{2,1,0:T(8,128)(2,1)S(1)} %pad_maximum_fusion.2.own_ref), channel_id=1, source_target_pairs={{0,4},{1,5},{2,6},{3,7},{4,8},{5,9},{6,10},{7,11},{8,12},{9,13},{1... | collective-permute-start | bytes 1572872 | tf_op jit(solution)/shard_map/ppermute | solution.py:121
  8.2 27.7 %copy-start.2 = (bf16[1,256,640]{2,1,0:T(8,128)(2,1)S(1)}, bf16[1,256,640]{2,1,0:T(8,128)(2,1)}, u32[]{:S(2)}) copy-start(bf16[1,256,640]{2,1,0:T(8,128)(2,1)} %copy-done.1) | copy-start | bytes 983044
  23.0 23.0 %copy-start.6 = (bf16[1,256,512]{2,1,0:T(8,128)(2,1)S(1)}, bf16[1,256,512]{2,1,0:T(8,128)(2,1)}, u32[]{:S(2)}) copy-start(bf16[1,256,512]{2,1,0:T(8,128)(2,1)} %copy-done.5) | copy-start | bytes 786436
  23.0 23.0 %copy-start.8 = (bf16[1,256,512]{2,1,0:T(8,128)(2,1)S(1)}, bf16[1,256,512]{2,1,0:T(8,128)(2,1)}, u32[]{:S(2)}) copy-start(bf16[1,256,512]{2,1,0:T(8,128)(2,1)} %copy-done.7) | copy-start | bytes 786436
  23.1 25.7 %collective-permute-start.13 = (bf16[2,256,640]{2,1,0:T(8,128)(2,1)S(1)}, bf16[2,256,640]{2,1,0:T(8,128)(2,1)S(1)}, u32[]{:S(2)}, u32[]{:S(2)}) collective-permute-start(bf16[2,256,640]{2,1,0:T(8,128)(2,1)S(1)} %get-tuple-element.6), channel_id=1, source_target_pairs={{0,2},{1,3},{2,0},{3,1},{4,6},{5,7},{6,4},{7,5},{8,10},{9,11},{10,... | collective-permute-start | bytes 1966088 | tf_op jit(solution)/shard_map/ppermute | solution.py:125
  36.0 29.0 %copy-start = (bf16[256,4096]{1,0:T(8,128)(2,1)S(1)}, bf16[256,4096]{1,0:T(8,128)(2,1)}, u32[]{:S(2)}) copy-start(bf16[256,4096]{1,0:T(8,128)(2,1)} %q_ref.7) | copy-start | bytes 6291460
  36.0 23.4 %collective-permute-start.9 = (bf16[2,256,640]{2,1,0:T(8,128)(2,1)S(1)}, bf16[2,256,640]{2,1,0:T(8,128)(2,1)S(1)}, u32[]{:S(2)}, u32[]{:S(2)}) collective-permute-start(bf16[2,256,640]{2,1,0:T(8,128)(2,1)S(1)} %get-tuple-element.8), channel_id=1, source_target_pairs={{0,2},{1,3},{2,0},{3,1},{4,6},{5,7},{6,4},{7,5},{8,10},{9,11},{10,... | collective-permute-start | bytes 1966088 | tf_op jit(solution)/shard_map/ppermute | solution.py:125
  38.6 24.3 %collective-permute-start.14 = (bf16[2,256,640]{2,1,0:T(8,128)(2,1)S(1)}, bf16[2,256,640]{2,1,0:T(8,128)(2,1)S(1)}, u32[]{:S(2)}, u32[]{:S(2)}) collective-permute-start(bf16[2,256,640]{2,1,0:T(8,128)(2,1)S(1)} %get-tuple-element.5), channel_id=1, source_target_pairs={{0,1},{1,0},{2,3},{3,2},{4,5},{5,4},{6,7},{7,6},{8,9},{9,8},{10,11... | collective-permute-start | bytes 1966088 | tf_op jit(solution)/shard_map/ppermute | solution.py:126
  47.2 15.7 %collective-permute-start.5 = (bf16[2,256,512]{2,1,0:T(8,128)(2,1)S(1)}, bf16[2,256,512]{2,1,0:T(8,128)(2,1)S(1)}, u32[]{:S(2)}, u32[]{:S(2)}) collective-permute-start(bf16[2,256,512]{2,1,0:T(8,128)(2,1)S(1)} %get-tuple-element.14), channel_id=1, source_target_pairs={{0,2},{1,3},{2,0},{3,1},{4,6},{5,7},{6,4},{7,5},{8,10},{9,11},{10,... | collective-permute-start | bytes 1572872 | tf_op jit(solution)/shard_map/ppermute | solution.py:125
  48.8 14.7 %collective-permute-start.15 = (bf16[2,256,640]{2,1,0:T(8,128)(2,1)S(1)}, bf16[2,256,640]{2,1,0:T(8,128)(2,1)S(1)}, u32[]{:S(2)}, u32[]{:S(2)}) collective-permute-start(bf16[2,256,640]{2,1,0:T(8,128)(2,1)S(1)} %collective-permute-done.13.mid_ref), channel_id=1, source_target_pairs={{0,1},{1,0},{2,3},{3,2},{4,5},{5,4},{6,7},{7,6},{8,9},{9,8},{10,11... | collective-permute-start | bytes 1966088 | tf_op jit(solution)/shard_map/ppermute | solution.py:127
  48.8 10.6 %collective-permute-start = (bf16[2,256,256]{2,1,0:T(8,128)(2,1)S(1)}, bf16[2,256,256]{2,1,0:T(8,128)(2,1)S(1)}, u32[]{:S(2)}, u32[]{:S(2)}) collective-permute-start(bf16[2,256,256]{2,1,0:T(8,128)(2,1)S(1)} %pad_maximum_fusion.3.own_ref), channel_id=1, source_target_pairs={{0,4},{1,5},{2,6},{3,7},{4,8},{5,9},{6,10},{7,11},{8,12},{9,13},{1... | collective-permute-start | bytes 786440 | tf_op jit(solution)/shard_map/ppermute | solution.py:121
  59.4 13.6 %collective-permute-start.10 = (bf16[2,256,640]{2,1,0:T(8,128)(2,1)S(1)}, bf16[2,256,640]{2,1,0:T(8,128)(2,1)S(1)}, u32[]{:S(2)}, u32[]{:S(2)}) collective-permute-start(bf16[2,256,640]{2,1,0:T(8,128)(2,1)S(1)} %get-tuple-element.7), channel_id=1, source_target_pairs={{0,1},{1,0},{2,3},{3,2},{4,5},{5,4},{6,7},{7,6},{8,9},{9,8},{10,11... | collective-permute-start | bytes 1966088 | tf_op jit(solution)/shard_map/ppermute | solution.py:126
  59.4 14.1 %collective-permute-start.11 = (bf16[2,256,640]{2,1,0:T(8,128)(2,1)S(1)}, bf16[2,256,640]{2,1,0:T(8,128)(2,1)S(1)}, u32[]{:S(2)}, u32[]{:S(2)}) collective-permute-start(bf16[2,256,640]{2,1,0:T(8,128)(2,1)S(1)} %collective-permute-done.9.mid_ref), channel_id=1, source_target_pairs={{0,1},{1,0},{2,3},{3,2},{4,5},{5,4},{6,7},{7,6},{8,9},{9,8},{10,11... | collective-permute-start | bytes 1966088 | tf_op jit(solution)/shard_map/ppermute | solution.py:127
  62.9 18.6 %collective-permute-start.6 = (bf16[2,256,512]{2,1,0:T(8,128)(2,1)S(1)}, bf16[2,256,512]{2,1,0:T(8,128)(2,1)S(1)}, u32[]{:S(2)}, u32[]{:S(2)}) collective-permute-start(bf16[2,256,512]{2,1,0:T(8,128)(2,1)S(1)} %get-tuple-element.13), channel_id=1, source_target_pairs={{0,1},{1,0},{2,3},{3,2},{4,5},{5,4},{6,7},{7,6},{8,9},{9,8},{10,11... | collective-permute-start | bytes 1572872 | tf_op jit(solution)/shard_map/ppermute | solution.py:126
  62.9 18.6 %collective-permute-start.7 = (bf16[2,256,512]{2,1,0:T(8,128)(2,1)S(1)}, bf16[2,256,512]{2,1,0:T(8,128)(2,1)S(1)}, u32[]{:S(2)}, u32[]{:S(2)}) collective-permute-start(bf16[2,256,512]{2,1,0:T(8,128)(2,1)S(1)} %collective-permute-done.5.mid_ref), channel_id=1, source_target_pairs={{0,1},{1,0},{2,3},{3,2},{4,5},{5,4},{6,7},{7,6},{8,9},{9,8},{10,11... | collective-permute-start | bytes 1572872 | tf_op jit(solution)/shard_map/ppermute | solution.py:127
  63.5 9.5 %collective-permute-start.1 = (bf16[2,256,256]{2,1,0:T(8,128)(2,1)S(1)}, bf16[2,256,256]{2,1,0:T(8,128)(2,1)S(1)}, u32[]{:S(2)}, u32[]{:S(2)}) collective-permute-start(bf16[2,256,256]{2,1,0:T(8,128)(2,1)S(1)} %get-tuple-element.16), channel_id=1, source_target_pairs={{0,2},{1,3},{2,0},{3,1},{4,6},{5,7},{6,4},{7,5},{8,10},{9,11},{10,... | collective-permute-start | bytes 786440 | tf_op jit(solution)/shard_map/ppermute | solution.py:125
  73.0 15.6 %collective-permute-start.2 = (bf16[2,256,256]{2,1,0:T(8,128)(2,1)S(1)}, bf16[2,256,256]{2,1,0:T(8,128)(2,1)S(1)}, u32[]{:S(2)}, u32[]{:S(2)}) collective-permute-start(bf16[2,256,256]{2,1,0:T(8,128)(2,1)S(1)} %get-tuple-element.15), channel_id=1, source_target_pairs={{0,1},{1,0},{2,3},{3,2},{4,5},{5,4},{6,7},{7,6},{8,9},{9,8},{10,11... | collective-permute-start | bytes 786440 | tf_op jit(solution)/shard_map/ppermute | solution.py:126
  73.0 15.6 %collective-permute-start.3 = (bf16[2,256,256]{2,1,0:T(8,128)(2,1)S(1)}, bf16[2,256,256]{2,1,0:T(8,128)(2,1)S(1)}, u32[]{:S(2)}, u32[]{:S(2)}) collective-permute-start(bf16[2,256,256]{2,1,0:T(8,128)(2,1)S(1)} %collective-permute-done.1.mid_ref), channel_id=1, source_target_pairs={{0,1},{1,0},{2,3},{3,2},{4,5},{5,4},{6,7},{7,6},{8,9},{9,8},{10,11... | collective-permute-start | bytes 786440 | tf_op jit(solution)/shard_map/ppermute | solution.py:127

commit v2 on v1

v2 whole, which is shorter than its diff:
```python
import jax
import jax.numpy as jnp
from jax import lax
from jax.experimental import pallas as pl
from jax.experimental.pallas import tpu as pltpu
from jax.sharding import PartitionSpec as P


QUERY_HEADS = 32
KEY_VALUE_HEADS = 16
HEAD_WIDTH = 128
WINDOW = 1024
GROUP = QUERY_HEADS // KEY_VALUE_HEADS

score_scale = 168.0 ** (-0.5)
LOG2_E = 1.4426950408889634
masked_value = -1e30
CHUNKS = (4, 4, 4, 4)


def pack_kernel(_, key_ref, value_ref, out_ref):
    length = key_ref.shape[0]
    for head in range(out_ref.shape[0]):
        columns = slice(head * HEAD_WIDTH, (head + 1) * HEAD_WIDTH)
        out_ref[head, :length] = key_ref[:, columns]
        for start in range(0, length, HEAD_WIDTH):
            rows = slice(length + start, length + start + HEAD_WIDTH)
            out_ref[head, rows] = value_ref[start : start + HEAD_WIDTH, columns].T


def pack(flags, key_rows, value_matrix, first, heads):
    length = key_rows.shape[0]
    spec = pl.BlockSpec((length, heads * HEAD_WIDTH), lambda _: (0, first // heads))
    return pl.pallas_call(
        pack_kernel,
        out_shape=jax.ShapeDtypeStruct((heads, 2 * length, HEAD_WIDTH), key_rows.dtype),
        grid=(1,),
        in_specs=[pl.BlockSpec(memory_space=pltpu.SMEM), spec, spec],
        out_specs=pl.BlockSpec((heads, 2 * length, HEAD_WIDTH), lambda _: (0, 0, 0)),
        compiler_params=pltpu.CompilerParams(vmem_limit_bytes=8 << 20),
        cost_estimate=pl.CostEstimate(
            flops=0, transcendentals=0, bytes_accessed=8 * heads * length * HEAD_WIDTH
        ),
    )(flags, key_rows, value_matrix)


def attend_kernel(block_ref, q_ref, own_ref, far_ref, mid_ref, pair1_ref, pair2_ref, *rest):
    o_ref, *score_refs = rest[-5:-2]
    max_refs = rest[-2:]
    heads, length = own_ref.shape[0], q_ref.shape[0]
    block = block_ref[0]
    odd = lax.rem(block, 2)

    def bias_of(back):
        return jnp.where(block >= back, 0.0, masked_value).astype(jnp.float32)

    far_bias = bias_of(4)
    biases = (0.0, bias_of(2), bias_of(3 - 2 * odd), bias_of(1 + 2 * odd))
    others = (None, mid_ref, pair1_ref, pair2_ref)
    across = (((1,), (1,)), ((), ()))
    scale = score_scale * LOG2_E
    ones = jnp.ones((16, length), jnp.bfloat16)
    key_pos = lax.broadcasted_iota(jnp.int32, (length, length), 0)
    query_pos = lax.broadcasted_iota(jnp.int32, (length, length), 1)
    causal = key_pos <= query_pos

    def columns(head, g):
        return pl.ds(pl.multiple_of((head * GROUP + g) * HEAD_WIDTH, HEAD_WIDTH), HEAD_WIDTH)

    def score(head, g, part, row_max):
        query = q_ref[:, columns(head, g)]

        def product(ref):
            return lax.dot_general(
                ref[head, :length], query, across, preferred_element_type=jnp.float32
            )

        if part == 0:
            raw = jnp.where(causal, product(own_ref), product(far_ref) + far_bias)
        else:
            raw = product(others[part])
        score_refs[g][part * length : (part + 1) * length] = raw
        largest = jnp.max(raw.reshape(length // 8, 8, length), axis=0) + biases[part]
        return largest if row_max is None else jnp.maximum(row_max, largest)

    def keep_max(g, row_max):
        row_max = jnp.max(row_max, axis=0, keepdims=True) * scale
        max_refs[g][...] = jnp.broadcast_to(row_max, max_refs[g].shape)

    def weigh(head, g, part, total):
        shift = max_refs[g][0:1] - biases[part] * scale
        weights = jnp.exp2(score_refs[g][part * length : (part + 1) * length] * scale - shift)
        if part == 0:
            pieces = (
                (own_ref, jnp.where(causal, weights, 0.0)),
                (far_ref, jnp.where(causal, 0.0, weights)),
            )
        else:
            pieces = ((others[part], weights),)
        for ref, piece in pieces:
            values = jnp.concatenate(
                [
                    ref[head, length + start : length + start + HEAD_WIDTH]
                    for start in range(0, length, HEAD_WIDTH)
                ],
                axis=1,
            )
            product = jnp.dot(
                jnp.concatenate([values, ones], axis=0),
                piece.astype(jnp.bfloat16),
                preferred_element_type=jnp.float32,
            )
            total = product if total is None else total + product
        return total

    def finish(head, g, total):
        result = total[:HEAD_WIDTH] / total[HEAD_WIDTH : HEAD_WIDTH + 1]
        o_ref[:, columns(head, g)] = result.T.astype(o_ref.dtype)

    def overlap(head, g, next_head, next_g):
        row_max = total = None
        for part in range(4):
            row_max = score(next_head, next_g, part, row_max)
            total = weigh(head, g, part, total)
        keep_max(next_g, row_max)
        finish(head, g, total)

    row_max = None
    for part in range(4):
        row_max = score(0, 0, part, row_max)
    keep_max(0, row_max)

    def step(head, _):
        overlap(head, 0, head, 1)
        overlap(head, 1, jnp.minimum(head + 1, heads - 1), 0)
        return 0

    lax.fori_loop(0, heads, step, 0)


def attend(block, queries, pieces, first, heads, output):
    length = queries.shape[0]
    kv_spec = pl.BlockSpec((heads, 2 * length, HEAD_WIDTH), lambda _: (0, 0, 0))
    q_spec = pl.BlockSpec((length, heads * GROUP * HEAD_WIDTH), lambda _: (0, first // heads))
    specs = [pl.BlockSpec(memory_space=pltpu.SMEM), q_spec] + [kv_spec] * len(pieces)
    args = [block, queries, *pieces]
    aliases = {}
    if output is not None:
        aliases = {len(args): 0}
        specs.append(pl.BlockSpec(memory_space=pl.ANY))
        args.append(output)
    keys = len(pieces) * length
    return pl.pallas_call(
        attend_kernel,
        out_shape=jax.ShapeDtypeStruct(queries.shape, queries.dtype),
        grid=(1,),
        in_specs=specs,
        out_specs=q_spec,
        scratch_shapes=[pltpu.VMEM((WINDOW, length), jnp.float32)] * 2
        + [pltpu.VMEM((8, length), jnp.float32)] * 2,
        input_output_aliases=aliases,
        compiler_params=pltpu.CompilerParams(vmem_limit_bytes=16 << 20),
        cost_estimate=pl.CostEstimate(
            flops=heads * GROUP * length * keys * HEAD_WIDTH * 4,
            transcendentals=heads * GROUP * length * WINDOW,
            bytes_accessed=heads * HEAD_WIDTH * length * 2 * (2 * len(pieces) + 2 * GROUP),
        ),
    )(*args)


def per_device(queries, key_rows, value_matrix):
    length = queries.shape[0]
    devices = lax.axis_size("seq")
    assert WINDOW == 4 * length and devices % 4 == 0
    far = [(i, i + 4) for i in range(devices - 4)]
    swap = [(i, i + 2 if i % 4 < 2 else i - 2) for i in range(devices)]
    pair = [(i, i ^ 1) for i in range(devices)]
    block = lax.axis_index("seq").astype(jnp.int32)
    upper = lax.rem(block, 4) >= 2
    odd = lax.rem(block, 2) == 1
    flags = jnp.stack([block, upper.astype(jnp.int32), odd.astype(jnp.int32)])
    block = block.reshape(1)

    bounds = [0]
    for heads in CHUNKS:
        bounds.append(bounds[-1] + heads)
    assert bounds[-1] == KEY_VALUE_HEADS
    own = []
    for first, heads in zip(bounds, CHUNKS):
        assert first % heads == 0
        own.append(pack(flags, key_rows, value_matrix, first, heads))

    def send(piece, pairs):
        return lax.ppermute(piece, "seq", pairs)

    output = None
    for chunk, heads in enumerate(CHUNKS):
        mine = own[chunk]
        distant = send(mine, far)
        middle = send(jnp.where(upper, distant, mine), swap)
        pair1 = send(jnp.where(odd, distant, mine), pair)
        pair2 = send(middle, pair)
        output = attend(
            block, queries, (mine, distant, middle, pair1, pair2), bounds[chunk], heads, output
        )
    return output


def solution(mesh):
    rows = P(("groups", "seq"), None)
    return jax.shard_map(
        per_device, mesh=mesh, in_specs=(rows, rows, rows), out_specs=rows, check_vma=False
    )
```

time: 93.1 us -> 100 us (1.074)
  waiting for transfers between devices: 44.5 us -> 59.9 us
  local copies, waits for them, and re-layouts: 5.02 us -> 2.45 us
  other arithmetic: 2.74 us -> 0.37 us
  Pallas kernels: 26.7 us -> 24.9 us
  starting transfers between devices: 13.1 us -> 11.5 us
    ppermute x16, waiting for transfers between devices: 44.5 us -> 59.9 us  [send(): return lax.ppermute(piece, 'seq', pairs)]
    another operation x3 -> x0, local copies, waits for them, and re-layouts: 3.45 us -> none  [per_device(): own.append(jnp.stack([key_rows[:, columns], value_matrix[:, columns]]))]
    select_n x4, other arithmetic: 2.52 us -> 0.29 us  [per_device(): pair1 = send(jnp.where(odd, distant, mine), pair)]
    pallas_call x4 -> x8, Pallas kernels: 26.7 us -> 24.9 us  [the longest x4 22.3 us: attend(): pl.pallas_call(attend_kernel, out_shape=jax.ShapeDtypeStruct(queries.shap...]
    ppermute x16, starting transfers between devices: 13.1 us -> 11.5 us  [send(): return lax.ppermute(piece, 'seq', pairs)]
    unnamed x18 -> x6, local copies, waits for them, and re-layouts: 1.57 us -> 2.45 us
  transfers between devices with their start and end apart: 16 -> 16, of which waited for: 5 -> 6; matrix products, arithmetic and copies ran while one was open for 5% -> 0% of each run, Pallas kernels for 25% -> 19%
where the time goes in v2:
time: 100 us; the launch traced here: 99.3 us
  waiting for transfers between devices  59.9 us (60%)
  Pallas kernels  24.9 us (25%)
  starting transfers between devices  11.5 us (12%)
  local copies, waits for them, and re-layouts  2.45 us (2%)
    ppermute x16, waiting for transfers between devices, send(): return lax.ppermute(piece, 'seq', pairs)  59.9 us
    pallas_call x4, Pallas kernels, attend(): pl.pallas_call(attend_kernel, out_shape=jax.ShapeDtypeStruct(queries.shap...  22.3 us
    ppermute x16, starting transfers between devices, send(): return lax.ppermute(piece, 'seq', pairs)  11.5 us
    pallas_call x4, Pallas kernels, pack(): pl.pallas_call(pack_kernel, out_shape=jax.ShapeDtypeStruct((heads, 2 * le...  2.64 us
    unnamed x6, local copies, waits for them, and re-layouts  2.45 us
  transfers between devices with their start and end apart: 16, of which 6 were waited for; matrix products, arithmetic and copies ran while one was open for 0% of the time, Pallas kernels for 19%

profile of v2, /device:TPU:26, one launch (start us, length us, event | category | flops | bytes accessed | tf_op | source)
XLA Modules:
  0.0 99.3 jit_solution(5394833807028766563)
XLA Ops:
  0.0 0.1 pad_add_fusion._
  0.1 1.2 %copy-done.1 = bf16[256,2048]{1,0:T(8,128)(2,1)S(1)} copy-done((bf16[256,2048]{1,0:T(8,128)(2,1)S(1)}, bf16[256,2048]{1,0:T(8,128)(2,1)}, u32[]{:S(2)}) %copy-start.1) | copy-done | bytes 1048600
  1.3 1.2 %copy-done.2 = bf16[256,2048]{1,0:T(8,128)(2,1)S(1)} copy-done((bf16[256,2048]{1,0:T(8,128)(2,1)S(1)}, bf16[256,2048]{1,0:T(8,128)(2,1)}, u32[]{:S(2)}) %copy-start.2) | copy-done | bytes 1048600
  2.5 0.7 shard_map.40.own_ref
  3.2 1.3 %collective-permute-start.12 = (bf16[4,512,128]{2,1,0:T(8,128)(2,1)S(1)}, bf16[4,512,128]{2,1,0:T(8,128)(2,1)S(1)}, u32[]{:S(2)}, u32[]{:S(2)}) collective-permute-start(bf16[4,512,128]{2,1,0:T(8,128)(2,1)S(1)} %shard_map.40.own_ref), channel_id=1, source_target_pairs={{0,4},{1,5},{2,6},{3,7},{4,8},{5,9},{6,10},{7,11},{8,12},{9,13},{1... | collective-permute-start | bytes 1572872 | tf_op jit(solution)/shard_map/ppermute | solution.py:194
  4.5 0.7 shard_map.39.own_ref
  5.2 1.3 %collective-permute-start.8 = (bf16[4,512,128]{2,1,0:T(8,128)(2,1)S(1)}, bf16[4,512,128]{2,1,0:T(8,128)(2,1)S(1)}, u32[]{:S(2)}, u32[]{:S(2)}) collective-permute-start(bf16[4,512,128]{2,1,0:T(8,128)(2,1)S(1)} %shard_map.39.own_ref), channel_id=1, source_target_pairs={{0,4},{1,5},{2,6},{3,7},{4,8},{5,9},{6,10},{7,11},{8,12},{9,13},{1... | collective-permute-start | bytes 1572872 | tf_op jit(solution)/shard_map/ppermute | solution.py:194
  6.5 0.7 shard_map.38.own_ref
  7.1 1.3 %collective-permute-start.4 = (bf16[4,512,128]{2,1,0:T(8,128)(2,1)S(1)}, bf16[4,512,128]{2,1,0:T(8,128)(2,1)S(1)}, u32[]{:S(2)}, u32[]{:S(2)}) collective-permute-start(bf16[4,512,128]{2,1,0:T(8,128)(2,1)S(1)} %shard_map.38.own_ref), channel_id=1, source_target_pairs={{0,4},{1,5},{2,6},{3,7},{4,8},{5,9},{6,10},{7,11},{8,12},{9,13},{1... | collective-permute-start | bytes 1572872 | tf_op jit(solution)/shard_map/ppermute | solution.py:194
  8.4 0.7 shard_map.37.own_ref
  9.1 1.3 %collective-permute-start = (bf16[4,512,128]{2,1,0:T(8,128)(2,1)S(1)}, bf16[4,512,128]{2,1,0:T(8,128)(2,1)S(1)}, u32[]{:S(2)}, u32[]{:S(2)}) collective-permute-start(bf16[4,512,128]{2,1,0:T(8,128)(2,1)S(1)} %shard_map.37.own_ref), channel_id=1, source_target_pairs={{0,4},{1,5},{2,6},{3,7},{4,8},{5,9},{6,10},{7,11},{8,12},{9,13},{1... | collective-permute-start | bytes 1572872 | tf_op jit(solution)/shard_map/ppermute | solution.py:194
  10.4 9.5 %collective-permute-done.12.far_ref = bf16[4,512,128]{2,1,0:T(8,128)(2,1)S(1)} collective-permute-done((bf16[4,512,128]{2,1,0:T(8,128)(2,1)S(1)}, bf16[4,512,128]{2,1,0:T(8,128)(2,1)S(1)}, u32[]{:S(2)}, u32[]{:S(2)}) %collective-permute-start.12) | collective-permute-done | bytes 524320 | tf_op jit(solution)/shard_map/ppermute | solution.py:194
  19.9 0.1 broadcast_select_fusion
  20.0 1.6 %collective-permute-start.13 = (bf16[4,512,128]{2,1,0:T(8,128)(2,1)S(1)}, bf16[4,512,128]{2,1,0:T(8,128)(2,1)S(1)}, u32[]{:S(2)}, u32[]{:S(2)}) collective-permute-start(bf16[4,512,128]{2,1,0:T(8,128)(2,1)S(1)} %get-tuple-element.6), channel_id=1, source_target_pairs={{0,2},{1,3},{2,0},{3,1},{4,6},{5,7},{6,4},{7,5},{8,10},{9,11},{10,... | collective-permute-start | bytes 1572872 | tf_op jit(solution)/shard_map/ppermute | solution.py:194
  21.5 9.6 %collective-permute-done.8.far_ref = bf16[4,512,128]{2,1,0:T(8,128)(2,1)S(1)} collective-permute-done((bf16[4,512,128]{2,1,0:T(8,128)(2,1)S(1)}, bf16[4,512,128]{2,1,0:T(8,128)(2,1)S(1)}, u32[]{:S(2)}, u32[]{:S(2)}) %collective-permute-start.8) | collective-permute-done | bytes 524320 | tf_op jit(solution)/shard_map/ppermute | solution.py:194
  31.1 0.1 broadcast_select_fusion.1
  31.2 1.6 %collective-permute-start.9 = (bf16[4,512,128]{2,1,0:T(8,128)(2,1)S(1)}, bf16[4,512,128]{2,1,0:T(8,128)(2,1)S(1)}, u32[]{:S(2)}, u32[]{:S(2)}) collective-permute-start(bf16[4,512,128]{2,1,0:T(8,128)(2,1)S(1)} %get-tuple-element.8), channel_id=1, source_target_pairs={{0,2},{1,3},{2,0},{3,1},{4,6},{5,7},{6,4},{7,5},{8,10},{9,11},{10,... | collective-permute-start | bytes 1572872 | tf_op jit(solution)/shard_map/ppermute | solution.py:194
  32.8 9.6 %collective-permute-done.4.far_ref = bf16[4,512,128]{2,1,0:T(8,128)(2,1)S(1)} collective-permute-done((bf16[4,512,128]{2,1,0:T(8,128)(2,1)S(1)}, bf16[4,512,128]{2,1,0:T(8,128)(2,1)S(1)}, u32[]{:S(2)}, u32[]{:S(2)}) %collective-permute-start.4) | collective-permute-done | bytes 524320 | tf_op jit(solution)/shard_map/ppermute | solution.py:194
  42.4 0.1 broadcast_select_fusion.2
  42.4 10.0 %collective-permute-done.far_ref = bf16[4,512,128]{2,1,0:T(8,128)(2,1)S(1)} collective-permute-done((bf16[4,512,128]{2,1,0:T(8,128)(2,1)S(1)}, bf16[4,512,128]{2,1,0:T(8,128)(2,1)S(1)}, u32[]{:S(2)}, u32[]{:S(2)}) %collective-permute-start) | collective-permute-done | bytes 524320 | tf_op jit(solution)/shard_map/ppermute | solution.py:194
  52.5 1.5 %collective-permute-start.5 = (bf16[4,512,128]{2,1,0:T(8,128)(2,1)S(1)}, bf16[4,512,128]{2,1,0:T(8,128)(2,1)S(1)}, u32[]{:S(2)}, u32[]{:S(2)}) collective-permute-start(bf16[4,512,128]{2,1,0:T(8,128)(2,1)S(1)} %get-tuple-element.10), channel_id=1, source_target_pairs={{0,2},{1,3},{2,0},{3,1},{4,6},{5,7},{6,4},{7,5},{8,10},{9,11},{10,... | collective-permute-start | bytes 1572872 | tf_op jit(solution)/shard_map/ppermute | solution.py:194
  54.0 0.1 broadcast_select_fusion.3
  54.1 0.6 collective-permute-start.1
  54.7 0.5 collective-permute-start.11
  55.2 0.1 collective-permute-start.6
  55.2 12.0 %collective-permute-done.5.mid_ref = bf16[4,512,128]{2,1,0:T(8,128)(2,1)S(1)} collective-permute-done((bf16[4,512,128]{2,1,0:T(8,128)(2,1)S(1)}, bf16[4,512,128]{2,1,0:T(8,128)(2,1)S(1)}, u32[]{:S(2)}, u32[]{:S(2)}) %collective-permute-start.5) | collective-permute-done | bytes 524320 | tf_op jit(solution)/shard_map/ppermute | solution.py:194
  67.3 9.2 %collective-permute-done.1.mid_ref = bf16[4,512,128]{2,1,0:T(8,128)(2,1)S(1)} collective-permute-done((bf16[4,512,128]{2,1,0:T(8,128)(2,1)S(1)}, bf16[4,512,128]{2,1,0:T(8,128)(2,1)S(1)}, u32[]{:S(2)}, u32[]{:S(2)}) %collective-permute-start.1) | collective-permute-done | bytes 524320 | tf_op jit(solution)/shard_map/ppermute | solution.py:194
  76.5 0.5 collective-permute-start.3
  77.0 5.6 %shard_map.41.rest_0_ = bf16[256,4096]{1,0:T(8,128)(2,1)} custom-call(s32[1]{0:T(128)} %bitcast.block_ref, bf16[256,4096]{1,0:T(8,128)(2,1)S(1)} %copy-done, bf16[4,512,128]{2,1,0:T(8,128)(2,1)S(1)} %shard_map.40.own_ref, bf16[4,512,128]{2,1,0:T(8,128)(2,1)S(1)} %collective-permute-done.12.far_ref, bf16[4,512,128]{2,1,0:T(8,128)(2,1)S(1)} %collective-permute-done.13.mid_ref, ...), custom_call_target="tpu_custom_call" | custom-call | flops 1342177280 | bytes 3670016 | tf_op jit(solution)/shard_map/pallas_call | solution.py:153
  82.6 5.6 %shard_map.42.rest_0_ = bf16[256,4096]{1,0:T(8,128)(2,1)} custom-call(s32[1]{0:T(128)} %bitcast.block_ref, bf16[256,4096]{1,0:T(8,128)(2,1)S(1)} %copy-done, bf16[4,512,128]{2,1,0:T(8,128)(2,1)S(1)} %shard_map.39.own_ref, bf16[4,512,128]{2,1,0:T(8,128)(2,1)S(1)} %collective-permute-done.8.far_ref, ...), custom_call_target="tpu_custom_call", output_to_operand_aliasing={{}: (7, {})} | custom-call | flops 1342177280 | bytes 3670016 | tf_op jit(solution)/shard_map/pallas_call | solution.py:153
  88.2 5.6 %shard_map.43.rest_0_ = bf16[256,4096]{1,0:T(8,128)(2,1)} custom-call(s32[1]{0:T(128)} %bitcast.block_ref, bf16[256,4096]{1,0:T(8,128)(2,1)S(1)} %copy-done, bf16[4,512,128]{2,1,0:T(8,128)(2,1)S(1)} %shard_map.38.own_ref, bf16[4,512,128]{2,1,0:T(8,128)(2,1)S(1)} %collective-permute-done.4.far_ref, ...), custom_call_target="tpu_custom_call", output_to_operand_aliasing={{}: (7, {})} | custom-call | flops 1342177280 | bytes 3670016 | tf_op jit(solution)/shard_map/pallas_call | solution.py:153
  93.8 5.6 %shard_map.44 = bf16[256,4096]{1,0:T(8,128)(2,1)} custom-call(s32[1]{0:T(128)} %bitcast.block_ref, bf16[256,4096]{1,0:T(8,128)(2,1)S(1)} %copy-done, bf16[4,512,128]{2,1,0:T(8,128)(2,1)S(1)} %shard_map.37.own_ref, bf16[4,512,128]{2,1,0:T(8,128)(2,1)S(1)} %collective-permute-done.far_ref, ...), custom_call_target="tpu_custom_call", output_to_operand_aliasing={{}: (7, {})} | custom-call | flops 1342177280 | bytes 3670016 | tf_op jit(solution)/shard_map/pallas_call | solution.py:153
  (19 shorter events, 0.0 us)
Async XLA Ops:
  0.1 1.2 %copy-start.1 = (bf16[256,2048]{1,0:T(8,128)(2,1)S(1)}, bf16[256,2048]{1,0:T(8,128)(2,1)}, u32[]{:S(2)}) copy-start(bf16[256,2048]{1,0:T(8,128)(2,1)} %key_ref.7) | copy-start | bytes 3145732
  1.3 1.2 %copy-start.2 = (bf16[256,2048]{1,0:T(8,128)(2,1)S(1)}, bf16[256,2048]{1,0:T(8,128)(2,1)}, u32[]{:S(2)}) copy-start(bf16[256,2048]{1,0:T(8,128)(2,1)} %value_ref.7) | copy-start | bytes 3145732
  3.2 16.7 %collective-permute-start.12 = (bf16[4,512,128]{2,1,0:T(8,128)(2,1)S(1)}, bf16[4,512,128]{2,1,0:T(8,128)(2,1)S(1)}, u32[]{:S(2)}, u32[]{:S(2)}) collective-permute-start(bf16[4,512,128]{2,1,0:T(8,128)(2,1)S(1)} %shard_map.40.own_ref), channel_id=1, source_target_pairs={{0,4},{1,5},{2,6},{3,7},{4,8},{5,9},{6,10},{7,11},{8,12},{9,13},{1... | collective-permute-start | bytes 1572872 | tf_op jit(solution)/shard_map/ppermute | solution.py:194
  5.2 26.0 %collective-permute-start.8 = (bf16[4,512,128]{2,1,0:T(8,128)(2,1)S(1)}, bf16[4,512,128]{2,1,0:T(8,128)(2,1)S(1)}, u32[]{:S(2)}, u32[]{:S(2)}) collective-permute-start(bf16[4,512,128]{2,1,0:T(8,128)(2,1)S(1)} %shard_map.39.own_ref), channel_id=1, source_target_pairs={{0,4},{1,5},{2,6},{3,7},{4,8},{5,9},{6,10},{7,11},{8,12},{9,13},{1... | collective-permute-start | bytes 1572872 | tf_op jit(solution)/shard_map/ppermute | solution.py:194
  7.1 35.2 %collective-permute-start.4 = (bf16[4,512,128]{2,1,0:T(8,128)(2,1)S(1)}, bf16[4,512,128]{2,1,0:T(8,128)(2,1)S(1)}, u32[]{:S(2)}, u32[]{:S(2)}) collective-permute-start(bf16[4,512,128]{2,1,0:T(8,128)(2,1)S(1)} %shard_map.38.own_ref), channel_id=1, source_target_pairs={{0,4},{1,5},{2,6},{3,7},{4,8},{5,9},{6,10},{7,11},{8,12},{9,13},{1... | collective-permute-start | bytes 1572872 | tf_op jit(solution)/shard_map/ppermute | solution.py:194
  9.1 43.4 %collective-permute-start = (bf16[4,512,128]{2,1,0:T(8,128)(2,1)S(1)}, bf16[4,512,128]{2,1,0:T(8,128)(2,1)S(1)}, u32[]{:S(2)}, u32[]{:S(2)}) collective-permute-start(bf16[4,512,128]{2,1,0:T(8,128)(2,1)S(1)} %shard_map.37.own_ref), channel_id=1, source_target_pairs={{0,4},{1,5},{2,6},{3,7},{4,8},{5,9},{6,10},{7,11},{8,12},{9,13},{1... | collective-permute-start | bytes 1572872 | tf_op jit(solution)/shard_map/ppermute | solution.py:194
  20.0 34.1 %collective-permute-start.13 = (bf16[4,512,128]{2,1,0:T(8,128)(2,1)S(1)}, bf16[4,512,128]{2,1,0:T(8,128)(2,1)S(1)}, u32[]{:S(2)}, u32[]{:S(2)}) collective-permute-start(bf16[4,512,128]{2,1,0:T(8,128)(2,1)S(1)} %get-tuple-element.6), channel_id=1, source_target_pairs={{0,2},{1,3},{2,0},{3,1},{4,6},{5,7},{6,4},{7,5},{8,10},{9,11},{10,... | collective-permute-start | bytes 1572872 | tf_op jit(solution)/shard_map/ppermute | solution.py:194
  21.5 33.1 %collective-permute-start.14 = (bf16[4,512,128]{2,1,0:T(8,128)(2,1)S(1)}, bf16[4,512,128]{2,1,0:T(8,128)(2,1)S(1)}, u32[]{:S(2)}, u32[]{:S(2)}) collective-permute-start(bf16[4,512,128]{2,1,0:T(8,128)(2,1)S(1)} %get-tuple-element.5), channel_id=1, source_target_pairs={{0,1},{1,0},{2,3},{3,2},{4,5},{5,4},{6,7},{7,6},{8,9},{9,8},{10,11... | collective-permute-start | bytes 1572872 | tf_op jit(solution)/shard_map/ppermute | solution.py:194
  31.2 23.5 %collective-permute-start.9 = (bf16[4,512,128]{2,1,0:T(8,128)(2,1)S(1)}, bf16[4,512,128]{2,1,0:T(8,128)(2,1)S(1)}, u32[]{:S(2)}, u32[]{:S(2)}) collective-permute-start(bf16[4,512,128]{2,1,0:T(8,128)(2,1)S(1)} %get-tuple-element.8), channel_id=1, source_target_pairs={{0,2},{1,3},{2,0},{3,1},{4,6},{5,7},{6,4},{7,5},{8,10},{9,11},{10,... | collective-permute-start | bytes 1572872 | tf_op jit(solution)/shard_map/ppermute | solution.py:194
  42.4 34.7 %copy-start = (bf16[256,4096]{1,0:T(8,128)(2,1)S(1)}, bf16[256,4096]{1,0:T(8,128)(2,1)}, u32[]{:S(2)}) copy-start(bf16[256,4096]{1,0:T(8,128)(2,1)} %q_ref.7) | copy-start | bytes 6291460
  42.4 12.8 %collective-permute-start.10 = (bf16[4,512,128]{2,1,0:T(8,128)(2,1)S(1)}, bf16[4,512,128]{2,1,0:T(8,128)(2,1)S(1)}, u32[]{:S(2)}, u32[]{:S(2)}) collective-permute-start(bf16[4,512,128]{2,1,0:T(8,128)(2,1)S(1)} %get-tuple-element.7), channel_id=1, source_target_pairs={{0,1},{1,0},{2,3},{3,2},{4,5},{5,4},{6,7},{7,6},{8,9},{9,8},{10,11... | collective-permute-start | bytes 1572872 | tf_op jit(solution)/shard_map/ppermute | solution.py:194
  52.5 14.8 %collective-permute-start.5 = (bf16[4,512,128]{2,1,0:T(8,128)(2,1)S(1)}, bf16[4,512,128]{2,1,0:T(8,128)(2,1)S(1)}, u32[]{:S(2)}, u32[]{:S(2)}) collective-permute-start(bf16[4,512,128]{2,1,0:T(8,128)(2,1)S(1)} %get-tuple-element.10), channel_id=1, source_target_pairs={{0,2},{1,3},{2,0},{3,1},{4,6},{5,7},{6,4},{7,5},{8,10},{9,11},{10,... | collective-permute-start | bytes 1572872 | tf_op jit(solution)/shard_map/ppermute | solution.py:194
  54.1 22.4 %collective-permute-start.1 = (bf16[4,512,128]{2,1,0:T(8,128)(2,1)S(1)}, bf16[4,512,128]{2,1,0:T(8,128)(2,1)S(1)}, u32[]{:S(2)}, u32[]{:S(2)}) collective-permute-start(bf16[4,512,128]{2,1,0:T(8,128)(2,1)S(1)} %get-tuple-element.12), channel_id=1, source_target_pairs={{0,2},{1,3},{2,0},{3,1},{4,6},{5,7},{6,4},{7,5},{8,10},{9,11},{10,... | collective-permute-start | bytes 1572872 | tf_op jit(solution)/shard_map/ppermute | solution.py:194
  54.6 21.9 %collective-permute-start.15 = (bf16[4,512,128]{2,1,0:T(8,128)(2,1)S(1)}, bf16[4,512,128]{2,1,0:T(8,128)(2,1)S(1)}, u32[]{:S(2)}, u32[]{:S(2)}) collective-permute-start(bf16[4,512,128]{2,1,0:T(8,128)(2,1)S(1)} %collective-permute-done.13.mid_ref), channel_id=1, source_target_pairs={{0,1},{1,0},{2,3},{3,2},{4,5},{5,4},{6,7},{7,6},{8,9},{9,8},{10,11... | collective-permute-start | bytes 1572872 | tf_op jit(solution)/shard_map/ppermute | solution.py:194
  54.7 27.9 %collective-permute-start.11 = (bf16[4,512,128]{2,1,0:T(8,128)(2,1)S(1)}, bf16[4,512,128]{2,1,0:T(8,128)(2,1)S(1)}, u32[]{:S(2)}, u32[]{:S(2)}) collective-permute-start(bf16[4,512,128]{2,1,0:T(8,128)(2,1)S(1)} %collective-permute-done.9.mid_ref), channel_id=1, source_target_pairs={{0,1},{1,0},{2,3},{3,2},{4,5},{5,4},{6,7},{7,6},{8,9},{9,8},{10,11... | collective-permute-start | bytes 1572872 | tf_op jit(solution)/shard_map/ppermute | solution.py:194
  55.2 33.0 %collective-permute-start.6 = (bf16[4,512,128]{2,1,0:T(8,128)(2,1)S(1)}, bf16[4,512,128]{2,1,0:T(8,128)(2,1)S(1)}, u32[]{:S(2)}, u32[]{:S(2)}) collective-permute-start(bf16[4,512,128]{2,1,0:T(8,128)(2,1)S(1)} %get-tuple-element.9), channel_id=1, source_target_pairs={{0,1},{1,0},{2,3},{3,2},{4,5},{5,4},{6,7},{7,6},{8,9},{9,8},{10,11... | collective-permute-start | bytes 1572872 | tf_op jit(solution)/shard_map/ppermute | solution.py:194
  67.3 20.9 %collective-permute-start.7 = (bf16[4,512,128]{2,1,0:T(8,128)(2,1)S(1)}, bf16[4,512,128]{2,1,0:T(8,128)(2,1)S(1)}, u32[]{:S(2)}, u32[]{:S(2)}) collective-permute-start(bf16[4,512,128]{2,1,0:T(8,128)(2,1)S(1)} %collective-permute-done.5.mid_ref), channel_id=1, source_target_pairs={{0,1},{1,0},{2,3},{3,2},{4,5},{5,4},{6,7},{7,6},{8,9},{9,8},{10,11... | collective-permute-start | bytes 1572872 | tf_op jit(solution)/shard_map/ppermute | solution.py:194
  76.5 17.2 %collective-permute-start.2 = (bf16[4,512,128]{2,1,0:T(8,128)(2,1)S(1)}, bf16[4,512,128]{2,1,0:T(8,128)(2,1)S(1)}, u32[]{:S(2)}, u32[]{:S(2)}) collective-permute-start(bf16[4,512,128]{2,1,0:T(8,128)(2,1)S(1)} %get-tuple-element.11), channel_id=1, source_target_pairs={{0,1},{1,0},{2,3},{3,2},{4,5},{5,4},{6,7},{7,6},{8,9},{9,8},{10,11... | collective-permute-start | bytes 1572872 | tf_op jit(solution)/shard_map/ppermute | solution.py:194
  76.5 17.2 %collective-permute-start.3 = (bf16[4,512,128]{2,1,0:T(8,128)(2,1)S(1)}, bf16[4,512,128]{2,1,0:T(8,128)(2,1)S(1)}, u32[]{:S(2)}, u32[]{:S(2)}) collective-permute-start(bf16[4,512,128]{2,1,0:T(8,128)(2,1)S(1)} %collective-permute-done.1.mid_ref), channel_id=1, source_target_pairs={{0,1},{1,0},{2,3},{3,2},{4,5},{5,4},{6,7},{7,6},{8,9},{9,8},{10,11... | collective-permute-start | bytes 1572872 | tf_op jit(solution)/shard_map/ppermute | solution.py:194

commit v3 on v2

--- a/solution.py
+++ b/solution.py
@@ -15,10 +15,10 @@
 score_scale = 168.0 ** (-0.5)
 LOG2_E = 1.4426950408889634
 masked_value = -1e30
-CHUNKS = (4, 4, 4, 4)
-
-
-def pack_kernel(_, key_ref, value_ref, out_ref):
+CHUNKS = (2, 2, 2, 2, 2, 2, 2, 2)
+
+
+def pack_kernel(key_ref, value_ref, out_ref):
     length = key_ref.shape[0]
     for head in range(out_ref.shape[0]):
         columns = slice(head * HEAD_WIDTH, (head + 1) * HEAD_WIDTH)
@@ -28,27 +28,27 @@
             out_ref[head, rows] = value_ref[start : start + HEAD_WIDTH, columns].T
 
 
-def pack(flags, key_rows, value_matrix, first, heads):
+def pack(key_rows, value_matrix, first, heads):
     length = key_rows.shape[0]
     spec = pl.BlockSpec((length, heads * HEAD_WIDTH), lambda _: (0, first // heads))
     return pl.pallas_call(
         pack_kernel,
         out_shape=jax.ShapeDtypeStruct((heads, 2 * length, HEAD_WIDTH), key_rows.dtype),
         grid=(1,),
-        in_specs=[pl.BlockSpec(memory_space=pltpu.SMEM), spec, spec],
+        in_specs=[spec, spec],
         out_specs=pl.BlockSpec((heads, 2 * length, HEAD_WIDTH), lambda _: (0, 0, 0)),
         compiler_params=pltpu.CompilerParams(vmem_limit_bytes=8 << 20),
         cost_estimate=pl.CostEstimate(
             flops=0, transcendentals=0, bytes_accessed=8 * heads * length * HEAD_WIDTH
         ),
-    )(flags, key_rows, value_matrix)
-
-
-def attend_kernel(block_ref, q_ref, own_ref, far_ref, mid_ref, pair1_ref, pair2_ref, *rest):
+    )(key_rows, value_matrix)
+
+
+def attend_kernel(q_ref, own_ref, far_ref, mid_ref, pair1_ref, pair2_ref, *rest):
     o_ref, *score_refs = rest[-5:-2]
     max_refs = rest[-2:]
     heads, length = own_ref.shape[0], q_ref.shape[0]
-    block = block_ref[0]
+    block = lax.axis_index("seq")
     odd = lax.rem(block, 2)
 
     def bias_of(back):
@@ -138,12 +138,12 @@
     lax.fori_loop(0, heads, step, 0)
 
 
-def attend(block, queries, pieces, first, heads, output):
+def attend(queries, pieces, first, heads, output):
     length = queries.shape[0]
     kv_spec = pl.BlockSpec((heads, 2 * length, HEAD_WIDTH), lambda _: (0, 0, 0))
     q_spec = pl.BlockSpec((length, heads * GROUP * HEAD_WIDTH), lambda _: (0, first // heads))
-    specs = [pl.BlockSpec(memory_space=pltpu.SMEM), q_spec] + [kv_spec] * len(pieces)
-    args = [block, queries, *pieces]
+    specs = [q_spec] + [kv_spec] * len(pieces)
+    args = [queries, *pieces]
     aliases = {}
     if output is not None:
         aliases = {len(args): 0}
@@ -172,14 +172,15 @@
     length = queries.shape[0]
     devices = lax.axis_size("seq")
     assert WINDOW == 4 * length and devices % 4 == 0
-    far = [(i, i + 4) for i in range(devices - 4)]
+    far = [(i, (i + 4) % devices) for i in range(devices)]
     swap = [(i, i + 2 if i % 4 < 2 else i - 2) for i in range(devices)]
     pair = [(i, i ^ 1) for i in range(devices)]
     block = lax.axis_index("seq").astype(jnp.int32)
     upper = lax.rem(block, 4) >= 2
     odd = lax.rem(block, 2) == 1
-    flags = jnp.stack([block, upper.astype(jnp.int32), odd.astype(jnp.int32)])
-    block = block.reshape(1)
+    key_rows, value_matrix, upper, odd = lax.optimization_barrier(
+        (key_rows, value_matrix, upper, odd)
+    )
 
     bounds = [0]
     for heads in CHUNKS:
@@ -188,7 +189,7 @@
     own = []
     for first, heads in zip(bounds, CHUNKS):
         assert first % heads == 0
-        own.append(pack(flags, key_rows, value_matrix, first, heads))
+        own.append(pack(key_rows, value_matrix, first, heads))
 
     def send(piece, pairs):
         return lax.ppermute(piece, "seq", pairs)
@@ -201,7 +202,7 @@
         pair1 = send(jnp.where(odd, distant, mine), pair)
         pair2 = send(middle, pair)
         output = attend(
-            block, queries, (mine, distant, middle, pair1, pair2), bounds[chunk], heads, output
+            queries, (mine, distant, middle, pair1, pair2), bounds[chunk], heads, output
         )
     return output
 

time: 100 us -> 116 us (1.16)
  the two profiles are of different devices: /device:TPU:26 before, /device:TPU:0 now
where the time goes in v3:
time: 116 us
  waiting for transfers between devices  64.4 us (56%)
  Pallas kernels  26.4 us (23%)
  starting transfers between devices  22.3 us (19%)
  local copies, waits for them, and re-layouts  2.45 us (2%)
    ppermute x32, waiting for transfers between devices, send(): return lax.ppermute(piece, 'seq', pairs)  64.4 us
    pallas_call x8, Pallas kernels, attend(): pl.pallas_call(attend_kernel, out_shape=jax.ShapeDtypeStruct(queries.shap...  25.5 us
    ppermute x32, starting transfers between devices, send(): return lax.ppermute(piece, 'seq', pairs)  22.3 us
    unnamed x6, local copies, waits for them, and re-layouts  2.45 us
  transfers between devices with their start and end apart: 32, of which 14 were waited for; matrix products, arithmetic and copies ran while one was open for 0% of the time, Pallas kernels for 20%

profile of v3, /device:TPU:0, one launch (start us, length us, event | category | flops | bytes accessed | tf_op | source)
XLA Modules:
  0.0 116.0 jit_solution(10879282433052245694)
XLA Ops:
  2.6 3.1 %collective-permute-start.28 = (bf16[2,512,128]{2,1,0:T(8,128)(2,1)S(1)}, bf16[2,512,128]{2,1,0:T(8,128)(2,1)S(1)}, u32[]{:S(2)}, u32[]{:S(2)}) collective-permute-start(bf16[2,512,128]{2,1,0:T(8,128)(2,1)S(1)} %shard_map.44.own_ref), channel_id=1, source_target_pairs={{0,4},{1,5},{2,6},{3,7},{4,8},{5,9},{6,10},{7,11},{8,12},{9,13},{1... | collective-permute-start | bytes 786440 | tf_op jit(solution)/shard_map/ppermute | solution.py:195
  5.8 1.6 %collective-permute-start.24 = (bf16[2,512,128]{2,1,0:T(8,128)(2,1)S(1)}, bf16[2,512,128]{2,1,0:T(8,128)(2,1)S(1)}, u32[]{:S(2)}, u32[]{:S(2)}) collective-permute-start(bf16[2,512,128]{2,1,0:T(8,128)(2,1)S(1)} %shard_map.43.own_ref), channel_id=1, source_target_pairs={{0,4},{1,5},{2,6},{3,7},{4,8},{5,9},{6,10},{7,11},{8,12},{9,13},{1... | collective-permute-start | bytes 786440 | tf_op jit(solution)/shard_map/ppermute | solution.py:195
  7.5 1.6 %collective-permute-start.20 = (bf16[2,512,128]{2,1,0:T(8,128)(2,1)S(1)}, bf16[2,512,128]{2,1,0:T(8,128)(2,1)S(1)}, u32[]{:S(2)}, u32[]{:S(2)}) collective-permute-start(bf16[2,512,128]{2,1,0:T(8,128)(2,1)S(1)} %shard_map.42.own_ref), channel_id=1, source_target_pairs={{0,4},{1,5},{2,6},{3,7},{4,8},{5,9},{6,10},{7,11},{8,12},{9,13},{1... | collective-permute-start | bytes 786440 | tf_op jit(solution)/shard_map/ppermute | solution.py:195
  9.5 1.8 %collective-permute-start.12 = (bf16[2,512,128]{2,1,0:T(8,128)(2,1)S(1)}, bf16[2,512,128]{2,1,0:T(8,128)(2,1)S(1)}, u32[]{:S(2)}, u32[]{:S(2)}) collective-permute-start(bf16[2,512,128]{2,1,0:T(8,128)(2,1)S(1)} %shard_map.40.own_ref), channel_id=1, source_target_pairs={{0,4},{1,5},{2,6},{3,7},{4,8},{5,9},{6,10},{7,11},{8,12},{9,13},{1... | collective-permute-start | bytes 786440 | tf_op jit(solution)/shard_map/ppermute | solution.py:195
  11.7 3.2 %collective-permute-done.28.far_ref = bf16[2,512,128]{2,1,0:T(8,128)(2,1)S(1)} collective-permute-done((bf16[2,512,128]{2,1,0:T(8,128)(2,1)S(1)}, bf16[2,512,128]{2,1,0:T(8,128)(2,1)S(1)}, u32[]{:S(2)}, u32[]{:S(2)}) %collective-permute-start.28) | collective-permute-done | bytes 262176 | tf_op jit(solution)/shard_map/ppermute | solution.py:195
  14.9 5.6 %collective-permute-done.24.far_ref = bf16[2,512,128]{2,1,0:T(8,128)(2,1)S(1)} collective-permute-done((bf16[2,512,128]{2,1,0:T(8,128)(2,1)S(1)}, bf16[2,512,128]{2,1,0:T(8,128)(2,1)S(1)}, u32[]{:S(2)}, u32[]{:S(2)}) %collective-permute-start.24) | collective-permute-done | bytes 262176 | tf_op jit(solution)/shard_map/ppermute | solution.py:195
  20.5 5.6 %collective-permute-done.20.far_ref = bf16[2,512,128]{2,1,0:T(8,128)(2,1)S(1)} collective-permute-done((bf16[2,512,128]{2,1,0:T(8,128)(2,1)S(1)}, bf16[2,512,128]{2,1,0:T(8,128)(2,1)S(1)}, u32[]{:S(2)}, u32[]{:S(2)}) %collective-permute-start.20) | collective-permute-done | bytes 262176 | tf_op jit(solution)/shard_map/ppermute | solution.py:195
  26.1 5.6 %collective-permute-done.16.far_ref = bf16[2,512,128]{2,1,0:T(8,128)(2,1)S(1)} collective-permute-done((bf16[2,512,128]{2,1,0:T(8,128)(2,1)S(1)}, bf16[2,512,128]{2,1,0:T(8,128)(2,1)S(1)}, u32[]{:S(2)}, u32[]{:S(2)}) %collective-permute-start.16) | collective-permute-done | bytes 262176 | tf_op jit(solution)/shard_map/ppermute | solution.py:195
  31.7 1.7 %collective-permute-start.29 = (bf16[2,512,128]{2,1,0:T(8,128)(2,1)S(1)}, bf16[2,512,128]{2,1,0:T(8,128)(2,1)S(1)}, u32[]{:S(2)}, u32[]{:S(2)}) collective-permute-start(bf16[2,512,128]{2,1,0:T(8,128)(2,1)S(1)} %get-tuple-element.14), channel_id=1, source_target_pairs={{0,2},{1,3},{2,0},{3,1},{4,6},{5,7},{6,4},{7,5},{8,10},{9,11},{10,... | collective-permute-start | bytes 786440 | tf_op jit(solution)/shard_map/ppermute | solution.py:195
  33.4 3.9 %collective-permute-done.12.far_ref = bf16[2,512,128]{2,1,0:T(8,128)(2,1)S(1)} collective-permute-done((bf16[2,512,128]{2,1,0:T(8,128)(2,1)S(1)}, bf16[2,512,128]{2,1,0:T(8,128)(2,1)S(1)}, u32[]{:S(2)}, u32[]{:S(2)}) %collective-permute-start.12) | collective-permute-done | bytes 262176 | tf_op jit(solution)/shard_map/ppermute | solution.py:195
  37.4 5.6 %collective-permute-done.8.far_ref = bf16[2,512,128]{2,1,0:T(8,128)(2,1)S(1)} collective-permute-done((bf16[2,512,128]{2,1,0:T(8,128)(2,1)S(1)}, bf16[2,512,128]{2,1,0:T(8,128)(2,1)S(1)}, u32[]{:S(2)}, u32[]{:S(2)}) %collective-permute-start.8) | collective-permute-done | bytes 262176 | tf_op jit(solution)/shard_map/ppermute | solution.py:195
  42.9 1.7 %collective-permute-start.25 = (bf16[2,512,128]{2,1,0:T(8,128)(2,1)S(1)}, bf16[2,512,128]{2,1,0:T(8,128)(2,1)S(1)}, u32[]{:S(2)}, u32[]{:S(2)}) collective-permute-start(bf16[2,512,128]{2,1,0:T(8,128)(2,1)S(1)} %get-tuple-element.16), channel_id=1, source_target_pairs={{0,2},{1,3},{2,0},{3,1},{4,6},{5,7},{6,4},{7,5},{8,10},{9,11},{10,... | collective-permute-start | bytes 786440 | tf_op jit(solution)/shard_map/ppermute | solution.py:195
  44.7 3.9 %collective-permute-done.4.far_ref = bf16[2,512,128]{2,1,0:T(8,128)(2,1)S(1)} collective-permute-done((bf16[2,512,128]{2,1,0:T(8,128)(2,1)S(1)}, bf16[2,512,128]{2,1,0:T(8,128)(2,1)S(1)}, u32[]{:S(2)}, u32[]{:S(2)}) %collective-permute-start.4) | collective-permute-done | bytes 262176 | tf_op jit(solution)/shard_map/ppermute | solution.py:195
  48.6 4.7 %collective-permute-done.far_ref = bf16[2,512,128]{2,1,0:T(8,128)(2,1)S(1)} collective-permute-done((bf16[2,512,128]{2,1,0:T(8,128)(2,1)S(1)}, bf16[2,512,128]{2,1,0:T(8,128)(2,1)S(1)}, u32[]{:S(2)}, u32[]{:S(2)}) %collective-permute-start) | collective-permute-done | bytes 262176 | tf_op jit(solution)/shard_map/ppermute | solution.py:195
  53.3 1.5 %collective-permute-start.21 = (bf16[2,512,128]{2,1,0:T(8,128)(2,1)S(1)}, bf16[2,512,128]{2,1,0:T(8,128)(2,1)S(1)}, u32[]{:S(2)}, u32[]{:S(2)}) collective-permute-start(bf16[2,512,128]{2,1,0:T(8,128)(2,1)S(1)} %get-tuple-element.18), channel_id=1, source_target_pairs={{0,2},{1,3},{2,0},{3,1},{4,6},{5,7},{6,4},{7,5},{8,10},{9,11},{10,... | collective-permute-start | bytes 786440 | tf_op jit(solution)/shard_map/ppermute | solution.py:195
  55.7 1.5 %collective-permute-start.13 = (bf16[2,512,128]{2,1,0:T(8,128)(2,1)S(1)}, bf16[2,512,128]{2,1,0:T(8,128)(2,1)S(1)}, u32[]{:S(2)}, u32[]{:S(2)}) collective-permute-start(bf16[2,512,128]{2,1,0:T(8,128)(2,1)S(1)} %get-tuple-element.22), channel_id=1, source_target_pairs={{0,2},{1,3},{2,0},{3,1},{4,6},{5,7},{6,4},{7,5},{8,10},{9,11},{10,... | collective-permute-start | bytes 786440 | tf_op jit(solution)/shard_map/ppermute | solution.py:195
  57.3 5.2 %collective-permute-done.21.mid_ref = bf16[2,512,128]{2,1,0:T(8,128)(2,1)S(1)} collective-permute-done((bf16[2,512,128]{2,1,0:T(8,128)(2,1)S(1)}, bf16[2,512,128]{2,1,0:T(8,128)(2,1)S(1)}, u32[]{:S(2)}, u32[]{:S(2)}) %collective-permute-start.21) | collective-permute-done | bytes 262176 | tf_op jit(solution)/shard_map/ppermute | solution.py:195
  62.5 1.5 %collective-permute-start.9 = (bf16[2,512,128]{2,1,0:T(8,128)(2,1)S(1)}, bf16[2,512,128]{2,1,0:T(8,128)(2,1)S(1)}, u32[]{:S(2)}, u32[]{:S(2)}) collective-permute-start(bf16[2,512,128]{2,1,0:T(8,128)(2,1)S(1)} %get-tuple-element.24), channel_id=1, source_target_pairs={{0,2},{1,3},{2,0},{3,1},{4,6},{5,7},{6,4},{7,5},{8,10},{9,11},{10,... | collective-permute-start | bytes 786440 | tf_op jit(solution)/shard_map/ppermute | solution.py:195
  64.0 4.1 %collective-permute-done.17.mid_ref = bf16[2,512,128]{2,1,0:T(8,128)(2,1)S(1)} collective-permute-done((bf16[2,512,128]{2,1,0:T(8,128)(2,1)S(1)}, bf16[2,512,128]{2,1,0:T(8,128)(2,1)S(1)}, u32[]{:S(2)}, u32[]{:S(2)}) %collective-permute-start.17) | collective-permute-done | bytes 262176 | tf_op jit(solution)/shard_map/ppermute | solution.py:195
  68.2 1.6 %collective-permute-start.5 = (bf16[2,512,128]{2,1,0:T(8,128)(2,1)S(1)}, bf16[2,512,128]{2,1,0:T(8,128)(2,1)S(1)}, u32[]{:S(2)}, u32[]{:S(2)}) collective-permute-start(bf16[2,512,128]{2,1,0:T(8,128)(2,1)S(1)} %get-tuple-element.26), channel_id=1, source_target_pairs={{0,2},{1,3},{2,0},{3,1},{4,6},{5,7},{6,4},{7,5},{8,10},{9,11},{10,... | collective-permute-start | bytes 786440 | tf_op jit(solution)/shard_map/ppermute | solution.py:195
  69.8 4.0 %collective-permute-done.13.mid_ref = bf16[2,512,128]{2,1,0:T(8,128)(2,1)S(1)} collective-permute-done((bf16[2,512,128]{2,1,0:T(8,128)(2,1)S(1)}, bf16[2,512,128]{2,1,0:T(8,128)(2,1)S(1)}, u32[]{:S(2)}, u32[]{:S(2)}) %collective-permute-start.13) | collective-permute-done | bytes 262176 | tf_op jit(solution)/shard_map/ppermute | solution.py:195
  75.3 4.1 %collective-permute-done.9.mid_ref = bf16[2,512,128]{2,1,0:T(8,128)(2,1)S(1)} collective-permute-done((bf16[2,512,128]{2,1,0:T(8,128)(2,1)S(1)}, bf16[2,512,128]{2,1,0:T(8,128)(2,1)S(1)}, u32[]{:S(2)}, u32[]{:S(2)}) %collective-permute-start.9) | collective-permute-done | bytes 262176 | tf_op jit(solution)/shard_map/ppermute | solution.py:195
  79.9 5.1 %collective-permute-done.5.mid_ref = bf16[2,512,128]{2,1,0:T(8,128)(2,1)S(1)} collective-permute-done((bf16[2,512,128]{2,1,0:T(8,128)(2,1)S(1)}, bf16[2,512,128]{2,1,0:T(8,128)(2,1)S(1)}, u32[]{:S(2)}, u32[]{:S(2)}) %collective-permute-start.5) | collective-permute-done | bytes 262176 | tf_op jit(solution)/shard_map/ppermute | solution.py:195
  85.0 3.9 %collective-permute-done.1.mid_ref = bf16[2,512,128]{2,1,0:T(8,128)(2,1)S(1)} collective-permute-done((bf16[2,512,128]{2,1,0:T(8,128)(2,1)S(1)}, bf16[2,512,128]{2,1,0:T(8,128)(2,1)S(1)}, u32[]{:S(2)}, u32[]{:S(2)}) %collective-permute-start.1) | collective-permute-done | bytes 262176 | tf_op jit(solution)/shard_map/ppermute | solution.py:195
  89.4 3.2 %shard_map.45.rest_0_ = bf16[256,4096]{1,0:T(8,128)(2,1)} custom-call(bf16[256,4096]{1,0:T(8,128)(2,1)S(1)} %copy-done, bf16[2,512,128]{2,1,0:T(8,128)(2,1)S(1)} %shard_map.44.own_ref, bf16[2,512,128]{2,1,0:T(8,128)(2,1)S(1)} %collective-permute-done.28.far_ref, bf16[2,512,128]{2,1,0:T(8,128)(2,1)S(1)} %collective-permute-done.29.mid_ref, ...), custom_call_target="tpu_custom_call" | custom-call | flops 671088640 | bytes 1835008 | tf_op jit(solution)/shard_map/pallas_call | solution.py:153
  93.1 3.2 %shard_map.46.rest_0_ = bf16[256,4096]{1,0:T(8,128)(2,1)} custom-call(bf16[256,4096]{1,0:T(8,128)(2,1)S(1)} %copy-done, bf16[2,512,128]{2,1,0:T(8,128)(2,1)S(1)} %shard_map.43.own_ref, bf16[2,512,128]{2,1,0:T(8,128)(2,1)S(1)} %collective-permute-done.24.far_ref, ...), custom_call_target="tpu_custom_call", output_to_operand_aliasing={{}: (6, {})} | custom-call | flops 671088640 | bytes 1835008 | tf_op jit(solution)/shard_map/pallas_call | solution.py:153
  96.8 3.2 %shard_map.47.rest_0_ = bf16[256,4096]{1,0:T(8,128)(2,1)} custom-call(bf16[256,4096]{1,0:T(8,128)(2,1)S(1)} %copy-done, bf16[2,512,128]{2,1,0:T(8,128)(2,1)S(1)} %shard_map.42.own_ref, bf16[2,512,128]{2,1,0:T(8,128)(2,1)S(1)} %collective-permute-done.20.far_ref, ...), custom_call_target="tpu_custom_call", output_to_operand_aliasing={{}: (6, {})} | custom-call | flops 671088640 | bytes 1835008 | tf_op jit(solution)/shard_map/pallas_call | solution.py:153
  100.0 3.2 %shard_map.48.rest_0_ = bf16[256,4096]{1,0:T(8,128)(2,1)} custom-call(bf16[256,4096]{1,0:T(8,128)(2,1)S(1)} %copy-done, bf16[2,512,128]{2,1,0:T(8,128)(2,1)S(1)} %shard_map.41.own_ref, bf16[2,512,128]{2,1,0:T(8,128)(2,1)S(1)} %collective-permute-done.16.far_ref, ...), custom_call_target="tpu_custom_call", output_to_operand_aliasing={{}: (6, {})} | custom-call | flops 671088640 | bytes 1835008 | tf_op jit(solution)/shard_map/pallas_call | solution.py:153
  103.2 3.2 %shard_map.49.rest_0_ = bf16[256,4096]{1,0:T(8,128)(2,1)} custom-call(bf16[256,4096]{1,0:T(8,128)(2,1)S(1)} %copy-done, bf16[2,512,128]{2,1,0:T(8,128)(2,1)S(1)} %shard_map.40.own_ref, bf16[2,512,128]{2,1,0:T(8,128)(2,1)S(1)} %collective-permute-done.12.far_ref, ...), custom_call_target="tpu_custom_call", output_to_operand_aliasing={{}: (6, {})} | custom-call | flops 671088640 | bytes 1835008 | tf_op jit(solution)/shard_map/pallas_call | solution.py:153
  106.4 3.2 %shard_map.50.rest_0_ = bf16[256,4096]{1,0:T(8,128)(2,1)} custom-call(bf16[256,4096]{1,0:T(8,128)(2,1)S(1)} %copy-done, bf16[2,512,128]{2,1,0:T(8,128)(2,1)S(1)} %shard_map.39.own_ref, bf16[2,512,128]{2,1,0:T(8,128)(2,1)S(1)} %collective-permute-done.8.far_ref, ...), custom_call_target="tpu_custom_call", output_to_operand_aliasing={{}: (6, {})} | custom-call | flops 671088640 | bytes 1835008 | tf_op jit(solution)/shard_map/pallas_call | solution.py:153
  109.6 3.2 %shard_map.51.rest_0_ = bf16[256,4096]{1,0:T(8,128)(2,1)} custom-call(bf16[256,4096]{1,0:T(8,128)(2,1)S(1)} %copy-done, bf16[2,512,128]{2,1,0:T(8,128)(2,1)S(1)} %shard_map.38.own_ref, bf16[2,512,128]{2,1,0:T(8,128)(2,1)S(1)} %collective-permute-done.4.far_ref, ...), custom_call_target="tpu_custom_call", output_to_operand_aliasing={{}: (6, {})} | custom-call | flops 671088640 | bytes 1835008 | tf_op jit(solution)/shard_map/pallas_call | solution.py:153
  112.8 3.2 %shard_map.52 = bf16[256,4096]{1,0:T(8,128)(2,1)} custom-call(bf16[256,4096]{1,0:T(8,128)(2,1)S(1)} %copy-done, bf16[2,512,128]{2,1,0:T(8,128)(2,1)S(1)} %shard_map.37.own_ref, bf16[2,512,128]{2,1,0:T(8,128)(2,1)S(1)} %collective-permute-done.far_ref, bf16[2,512,128]{2,1,0:T(8,128)(2,1)S(1)} %collective-permute-done.1.mid_ref, ...), custom_call_target="tpu_custom_call", output_to_operand_aliasing={{}: (6, {})} | custom-call | flops 671088640 | bytes 1835008 | tf_op jit(solution)/shard_map/pallas_call | solution.py:153
  (62 shorter events, 8.2 us)
Async XLA Ops:
  2.6 12.3 %collective-permute-start.28 = (bf16[2,512,128]{2,1,0:T(8,128)(2,1)S(1)}, bf16[2,512,128]{2,1,0:T(8,128)(2,1)S(1)}, u32[]{:S(2)}, u32[]{:S(2)}) collective-permute-start(bf16[2,512,128]{2,1,0:T(8,128)(2,1)S(1)} %shard_map.44.own_ref), channel_id=1, source_target_pairs={{0,4},{1,5},{2,6},{3,7},{4,8},{5,9},{6,10},{7,11},{8,12},{9,13},{1... | collective-permute-start | bytes 786440 | tf_op jit(solution)/shard_map/ppermute | solution.py:195
  5.8 14.7 %collective-permute-start.24 = (bf16[2,512,128]{2,1,0:T(8,128)(2,1)S(1)}, bf16[2,512,128]{2,1,0:T(8,128)(2,1)S(1)}, u32[]{:S(2)}, u32[]{:S(2)}) collective-permute-start(bf16[2,512,128]{2,1,0:T(8,128)(2,1)S(1)} %shard_map.43.own_ref), channel_id=1, source_target_pairs={{0,4},{1,5},{2,6},{3,7},{4,8},{5,9},{6,10},{7,11},{8,12},{9,13},{1... | collective-permute-start | bytes 786440 | tf_op jit(solution)/shard_map/ppermute | solution.py:195
  7.5 18.6 %collective-permute-start.20 = (bf16[2,512,128]{2,1,0:T(8,128)(2,1)S(1)}, bf16[2,512,128]{2,1,0:T(8,128)(2,1)S(1)}, u32[]{:S(2)}, u32[]{:S(2)}) collective-permute-start(bf16[2,512,128]{2,1,0:T(8,128)(2,1)S(1)} %shard_map.42.own_ref), channel_id=1, source_target_pairs={{0,4},{1,5},{2,6},{3,7},{4,8},{5,9},{6,10},{7,11},{8,12},{9,13},{1... | collective-permute-start | bytes 786440 | tf_op jit(solution)/shard_map/ppermute | solution.py:195
  9.3 22.4 %collective-permute-start.16 = (bf16[2,512,128]{2,1,0:T(8,128)(2,1)S(1)}, bf16[2,512,128]{2,1,0:T(8,128)(2,1)S(1)}, u32[]{:S(2)}, u32[]{:S(2)}) collective-permute-start(bf16[2,512,128]{2,1,0:T(8,128)(2,1)S(1)} %shard_map.41.own_ref), channel_id=1, source_target_pairs={{0,4},{1,5},{2,6},{3,7},{4,8},{5,9},{6,10},{7,11},{8,12},{9,13},{1... | collective-permute-start | bytes 786440 | tf_op jit(solution)/shard_map/ppermute | solution.py:195
  9.5 27.9 %collective-permute-start.12 = (bf16[2,512,128]{2,1,0:T(8,128)(2,1)S(1)}, bf16[2,512,128]{2,1,0:T(8,128)(2,1)S(1)}, u32[]{:S(2)}, u32[]{:S(2)}) collective-permute-start(bf16[2,512,128]{2,1,0:T(8,128)(2,1)S(1)} %shard_map.40.own_ref), channel_id=1, source_target_pairs={{0,4},{1,5},{2,6},{3,7},{4,8},{5,9},{6,10},{7,11},{8,12},{9,13},{1... | collective-permute-start | bytes 786440 | tf_op jit(solution)/shard_map/ppermute | solution.py:195
  14.9 28.1 %collective-permute-start.8 = (bf16[2,512,128]{2,1,0:T(8,128)(2,1)S(1)}, bf16[2,512,128]{2,1,0:T(8,128)(2,1)S(1)}, u32[]{:S(2)}, u32[]{:S(2)}) collective-permute-start(bf16[2,512,128]{2,1,0:T(8,128)(2,1)S(1)} %shard_map.39.own_ref), channel_id=1, source_target_pairs={{0,4},{1,5},{2,6},{3,7},{4,8},{5,9},{6,10},{7,11},{8,12},{9,13},{1... | collective-permute-start | bytes 786440 | tf_op jit(solution)/shard_map/ppermute | solution.py:195
  20.5 28.1 %collective-permute-start.4 = (bf16[2,512,128]{2,1,0:T(8,128)(2,1)S(1)}, bf16[2,512,128]{2,1,0:T(8,128)(2,1)S(1)}, u32[]{:S(2)}, u32[]{:S(2)}) collective-permute-start(bf16[2,512,128]{2,1,0:T(8,128)(2,1)S(1)} %shard_map.38.own_ref), channel_id=1, source_target_pairs={{0,4},{1,5},{2,6},{3,7},{4,8},{5,9},{6,10},{7,11},{8,12},{9,13},{1... | collective-permute-start | bytes 786440 | tf_op jit(solution)/shard_map/ppermute | solution.py:195
  26.1 27.2 %collective-permute-start = (bf16[2,512,128]{2,1,0:T(8,128)(2,1)S(1)}, bf16[2,512,128]{2,1,0:T(8,128)(2,1)S(1)}, u32[]{:S(2)}, u32[]{:S(2)}) collective-permute-start(bf16[2,512,128]{2,1,0:T(8,128)(2,1)S(1)} %shard_map.37.own_ref), channel_id=1, source_target_pairs={{0,4},{1,5},{2,6},{3,7},{4,8},{5,9},{6,10},{7,11},{8,12},{9,13},{1... | collective-permute-start | bytes 786440 | tf_op jit(solution)/shard_map/ppermute | solution.py:195
  31.7 23.1 %collective-permute-start.29 = (bf16[2,512,128]{2,1,0:T(8,128)(2,1)S(1)}, bf16[2,512,128]{2,1,0:T(8,128)(2,1)S(1)}, u32[]{:S(2)}, u32[]{:S(2)}) collective-permute-start(bf16[2,512,128]{2,1,0:T(8,128)(2,1)S(1)} %get-tuple-element.14), channel_id=1, source_target_pairs={{0,2},{1,3},{2,0},{3,1},{4,6},{5,7},{6,4},{7,5},{8,10},{9,11},{10,... | collective-permute-start | bytes 786440 | tf_op jit(solution)/shard_map/ppermute | solution.py:195
  37.3 17.5 %collective-permute-start.30 = (bf16[2,512,128]{2,1,0:T(8,128)(2,1)S(1)}, bf16[2,512,128]{2,1,0:T(8,128)(2,1)S(1)}, u32[]{:S(2)}, u32[]{:S(2)}) collective-permute-start(bf16[2,512,128]{2,1,0:T(8,128)(2,1)S(1)} %get-tuple-element.13), channel_id=1, source_target_pairs={{0,1},{1,0},{2,3},{3,2},{4,5},{5,4},{6,7},{7,6},{8,9},{9,8},{10,11... | collective-permute-start | bytes 786440 | tf_op jit(solution)/shard_map/ppermute | solution.py:195
  42.9 12.5 %collective-permute-start.25 = (bf16[2,512,128]{2,1,0:T(8,128)(2,1)S(1)}, bf16[2,512,128]{2,1,0:T(8,128)(2,1)S(1)}, u32[]{:S(2)}, u32[]{:S(2)}) collective-permute-start(bf16[2,512,128]{2,1,0:T(8,128)(2,1)S(1)} %get-tuple-element.16), channel_id=1, source_target_pairs={{0,2},{1,3},{2,0},{3,1},{4,6},{5,7},{6,4},{7,5},{8,10},{9,11},{10,... | collective-permute-start | bytes 786440 | tf_op jit(solution)/shard_map/ppermute | solution.py:195
  48.6 7.2 %collective-permute-start.26 = (bf16[2,512,128]{2,1,0:T(8,128)(2,1)S(1)}, bf16[2,512,128]{2,1,0:T(8,128)(2,1)S(1)}, u32[]{:S(2)}, u32[]{:S(2)}) collective-permute-start(bf16[2,512,128]{2,1,0:T(8,128)(2,1)S(1)} %get-tuple-element.15), channel_id=1, source_target_pairs={{0,1},{1,0},{2,3},{3,2},{4,5},{5,4},{6,7},{7,6},{8,9},{9,8},{10,11... | collective-permute-start | bytes 786440 | tf_op jit(solution)/shard_map/ppermute | solution.py:195
  53.3 9.2 %collective-permute-start.21 = (bf16[2,512,128]{2,1,0:T(8,128)(2,1)S(1)}, bf16[2,512,128]{2,1,0:T(8,128)(2,1)S(1)}, u32[]{:S(2)}, u32[]{:S(2)}) collective-permute-start(bf16[2,512,128]{2,1,0:T(8,128)(2,1)S(1)} %get-tuple-element.18), channel_id=1, source_target_pairs={{0,2},{1,3},{2,0},{3,1},{4,6},{5,7},{6,4},{7,5},{8,10},{9,11},{10,... | collective-permute-start | bytes 786440 | tf_op jit(solution)/shard_map/ppermute | solution.py:195
  54.9 7.7 %collective-permute-start.22 = (bf16[2,512,128]{2,1,0:T(8,128)(2,1)S(1)}, bf16[2,512,128]{2,1,0:T(8,128)(2,1)S(1)}, u32[]{:S(2)}, u32[]{:S(2)}) collective-permute-start(bf16[2,512,128]{2,1,0:T(8,128)(2,1)S(1)} %get-tuple-element.17), channel_id=1, source_target_pairs={{0,1},{1,0},{2,3},{3,2},{4,5},{5,4},{6,7},{7,6},{8,9},{9,8},{10,11... | collective-permute-start | bytes 786440 | tf_op jit(solution)/shard_map/ppermute | solution.py:195
  54.9 13.3 %collective-permute-start.17 = (bf16[2,512,128]{2,1,0:T(8,128)(2,1)S(1)}, bf16[2,512,128]{2,1,0:T(8,128)(2,1)S(1)}, u32[]{:S(2)}, u32[]{:S(2)}) collective-permute-start(bf16[2,512,128]{2,1,0:T(8,128)(2,1)S(1)} %get-tuple-element.20), channel_id=1, source_target_pairs={{0,2},{1,3},{2,0},{3,1},{4,6},{5,7},{6,4},{7,5},{8,10},{9,11},{10,... | collective-permute-start | bytes 786440 | tf_op jit(solution)/shard_map/ppermute | solution.py:195
  55.5 12.7 %collective-permute-start.18 = (bf16[2,512,128]{2,1,0:T(8,128)(2,1)S(1)}, bf16[2,512,128]{2,1,0:T(8,128)(2,1)S(1)}, u32[]{:S(2)}, u32[]{:S(2)}) collective-permute-start(bf16[2,512,128]{2,1,0:T(8,128)(2,1)S(1)} %get-tuple-element.19), channel_id=1, source_target_pairs={{0,1},{1,0},{2,3},{3,2},{4,5},{5,4},{6,7},{7,6},{8,9},{9,8},{10,11... | collective-permute-start | bytes 786440 | tf_op jit(solution)/shard_map/ppermute | solution.py:195
  55.7 18.0 %collective-permute-start.13 = (bf16[2,512,128]{2,1,0:T(8,128)(2,1)S(1)}, bf16[2,512,128]{2,1,0:T(8,128)(2,1)S(1)}, u32[]{:S(2)}, u32[]{:S(2)}) collective-permute-start(bf16[2,512,128]{2,1,0:T(8,128)(2,1)S(1)} %get-tuple-element.22), channel_id=1, source_target_pairs={{0,2},{1,3},{2,0},{3,1},{4,6},{5,7},{6,4},{7,5},{8,10},{9,11},{10,... | collective-permute-start | bytes 786440 | tf_op jit(solution)/shard_map/ppermute | solution.py:195
  62.5 12.8 %collective-permute-start.14 = (bf16[2,512,128]{2,1,0:T(8,128)(2,1)S(1)}, bf16[2,512,128]{2,1,0:T(8,128)(2,1)S(1)}, u32[]{:S(2)}, u32[]{:S(2)}) collective-permute-start(bf16[2,512,128]{2,1,0:T(8,128)(2,1)S(1)} %get-tuple-element.21), channel_id=1, source_target_pairs={{0,1},{1,0},{2,3},{3,2},{4,5},{5,4},{6,7},{7,6},{8,9},{9,8},{10,11... | collective-permute-start | bytes 786440 | tf_op jit(solution)/shard_map/ppermute | solution.py:195
  62.5 16.8 %collective-permute-start.9 = (bf16[2,512,128]{2,1,0:T(8,128)(2,1)S(1)}, bf16[2,512,128]{2,1,0:T(8,128)(2,1)S(1)}, u32[]{:S(2)}, u32[]{:S(2)}) collective-permute-start(bf16[2,512,128]{2,1,0:T(8,128)(2,1)S(1)} %get-tuple-element.24), channel_id=1, source_target_pairs={{0,2},{1,3},{2,0},{3,1},{4,6},{5,7},{6,4},{7,5},{8,10},{9,11},{10,... | collective-permute-start | bytes 786440 | tf_op jit(solution)/shard_map/ppermute | solution.py:195
  68.1 11.2 %collective-permute-start.10 = (bf16[2,512,128]{2,1,0:T(8,128)(2,1)S(1)}, bf16[2,512,128]{2,1,0:T(8,128)(2,1)S(1)}, u32[]{:S(2)}, u32[]{:S(2)}) collective-permute-start(bf16[2,512,128]{2,1,0:T(8,128)(2,1)S(1)} %get-tuple-element.23), channel_id=1, source_target_pairs={{0,1},{1,0},{2,3},{3,2},{4,5},{5,4},{6,7},{7,6},{8,9},{9,8},{10,11... | collective-permute-start | bytes 786440 | tf_op jit(solution)/shard_map/ppermute | solution.py:195
  68.2 16.8 %collective-permute-start.5 = (bf16[2,512,128]{2,1,0:T(8,128)(2,1)S(1)}, bf16[2,512,128]{2,1,0:T(8,128)(2,1)S(1)}, u32[]{:S(2)}, u32[]{:S(2)}) collective-permute-start(bf16[2,512,128]{2,1,0:T(8,128)(2,1)S(1)} %get-tuple-element.26), channel_id=1, source_target_pairs={{0,2},{1,3},{2,0},{3,1},{4,6},{5,7},{6,4},{7,5},{8,10},{9,11},{10,... | collective-permute-start | bytes 786440 | tf_op jit(solution)/shard_map/ppermute | solution.py:195
  73.7 15.1 %collective-permute-start.1 = (bf16[2,512,128]{2,1,0:T(8,128)(2,1)S(1)}, bf16[2,512,128]{2,1,0:T(8,128)(2,1)S(1)}, u32[]{:S(2)}, u32[]{:S(2)}) collective-permute-start(bf16[2,512,128]{2,1,0:T(8,128)(2,1)S(1)} %get-tuple-element.28), channel_id=1, source_target_pairs={{0,2},{1,3},{2,0},{3,1},{4,6},{5,7},{6,4},{7,5},{8,10},{9,11},{10,... | collective-permute-start | bytes 786440 | tf_op jit(solution)/shard_map/ppermute | solution.py:195
  75.3 13.6 %collective-permute-start.31 = (bf16[2,512,128]{2,1,0:T(8,128)(2,1)S(1)}, bf16[2,512,128]{2,1,0:T(8,128)(2,1)S(1)}, u32[]{:S(2)}, u32[]{:S(2)}) collective-permute-start(bf16[2,512,128]{2,1,0:T(8,128)(2,1)S(1)} %collective-permute-done.29.mid_ref), channel_id=1, source_target_pairs={{0,1},{1,0},{2,3},{3,2},{4,5},{5,4},{6,7},{7,6},{8,9},{9,8},{10,11... | collective-permute-start | bytes 786440 | tf_op jit(solution)/shard_map/ppermute | solution.py:195
  79.4 13.2 %collective-permute-start.27 = (bf16[2,512,128]{2,1,0:T(8,128)(2,1)S(1)}, bf16[2,512,128]{2,1,0:T(8,128)(2,1)S(1)}, u32[]{:S(2)}, u32[]{:S(2)}) collective-permute-start(bf16[2,512,128]{2,1,0:T(8,128)(2,1)S(1)} %collective-permute-done.25.mid_ref), channel_id=1, source_target_pairs={{0,1},{1,0},{2,3},{3,2},{4,5},{5,4},{6,7},{7,6},{8,9},{9,8},{10,11... | collective-permute-start | bytes 786440 | tf_op jit(solution)/shard_map/ppermute | solution.py:195
  79.4 13.2 %collective-permute-start.23 = (bf16[2,512,128]{2,1,0:T(8,128)(2,1)S(1)}, bf16[2,512,128]{2,1,0:T(8,128)(2,1)S(1)}, u32[]{:S(2)}, u32[]{:S(2)}) collective-permute-start(bf16[2,512,128]{2,1,0:T(8,128)(2,1)S(1)} %collective-permute-done.21.mid_ref), channel_id=1, source_target_pairs={{0,1},{1,0},{2,3},{3,2},{4,5},{5,4},{6,7},{7,6},{8,9},{9,8},{10,11... | collective-permute-start | bytes 786440 | tf_op jit(solution)/shard_map/ppermute | solution.py:195
  85.0 11.3 %collective-permute-start.19 = (bf16[2,512,128]{2,1,0:T(8,128)(2,1)S(1)}, bf16[2,512,128]{2,1,0:T(8,128)(2,1)S(1)}, u32[]{:S(2)}, u32[]{:S(2)}) collective-permute-start(bf16[2,512,128]{2,1,0:T(8,128)(2,1)S(1)} %collective-permute-done.17.mid_ref), channel_id=1, source_target_pairs={{0,1},{1,0},{2,3},{3,2},{4,5},{5,4},{6,7},{7,6},{8,9},{9,8},{10,11... | collective-permute-start | bytes 786440 | tf_op jit(solution)/shard_map/ppermute | solution.py:195
  88.9 7.5 %collective-permute-start.15 = (bf16[2,512,128]{2,1,0:T(8,128)(2,1)S(1)}, bf16[2,512,128]{2,1,0:T(8,128)(2,1)S(1)}, u32[]{:S(2)}, u32[]{:S(2)}) collective-permute-start(bf16[2,512,128]{2,1,0:T(8,128)(2,1)S(1)} %collective-permute-done.13.mid_ref), channel_id=1, source_target_pairs={{0,1},{1,0},{2,3},{3,2},{4,5},{5,4},{6,7},{7,6},{8,9},{9,8},{10,11... | collective-permute-start | bytes 786440 | tf_op jit(solution)/shard_map/ppermute | solution.py:195
  88.9 17.5 %collective-permute-start.11 = (bf16[2,512,128]{2,1,0:T(8,128)(2,1)S(1)}, bf16[2,512,128]{2,1,0:T(8,128)(2,1)S(1)}, u32[]{:S(2)}, u32[]{:S(2)}) collective-permute-start(bf16[2,512,128]{2,1,0:T(8,128)(2,1)S(1)} %collective-permute-done.9.mid_ref), channel_id=1, source_target_pairs={{0,1},{1,0},{2,3},{3,2},{4,5},{5,4},{6,7},{7,6},{8,9},{9,8},{10,11... | collective-permute-start | bytes 786440 | tf_op jit(solution)/shard_map/ppermute | solution.py:195
  92.6 17.0 %collective-permute-start.6 = (bf16[2,512,128]{2,1,0:T(8,128)(2,1)S(1)}, bf16[2,512,128]{2,1,0:T(8,128)(2,1)S(1)}, u32[]{:S(2)}, u32[]{:S(2)}) collective-permute-start(bf16[2,512,128]{2,1,0:T(8,128)(2,1)S(1)} %get-tuple-element.25), channel_id=1, source_target_pairs={{0,1},{1,0},{2,3},{3,2},{4,5},{5,4},{6,7},{7,6},{8,9},{9,8},{10,11... | collective-permute-start | bytes 786440 | tf_op jit(solution)/shard_map/ppermute | solution.py:195
  92.6 17.0 %collective-permute-start.7 = (bf16[2,512,128]{2,1,0:T(8,128)(2,1)S(1)}, bf16[2,512,128]{2,1,0:T(8,128)(2,1)S(1)}, u32[]{:S(2)}, u32[]{:S(2)}) collective-permute-start(bf16[2,512,128]{2,1,0:T(8,128)(2,1)S(1)} %collective-permute-done.5.mid_ref), channel_id=1, source_target_pairs={{0,1},{1,0},{2,3},{3,2},{4,5},{5,4},{6,7},{7,6},{8,9},{9,8},{10,11... | collective-permute-start | bytes 786440 | tf_op jit(solution)/shard_map/ppermute | solution.py:195
  96.3 16.5 %collective-permute-start.2 = (bf16[2,512,128]{2,1,0:T(8,128)(2,1)S(1)}, bf16[2,512,128]{2,1,0:T(8,128)(2,1)S(1)}, u32[]{:S(2)}, u32[]{:S(2)}) collective-permute-start(bf16[2,512,128]{2,1,0:T(8,128)(2,1)S(1)} %get-tuple-element.27), channel_id=1, source_target_pairs={{0,1},{1,0},{2,3},{3,2},{4,5},{5,4},{6,7},{7,6},{8,9},{9,8},{10,11... | collective-permute-start | bytes 786440 | tf_op jit(solution)/shard_map/ppermute | solution.py:195
  96.4 16.4 %collective-permute-start.3 = (bf16[2,512,128]{2,1,0:T(8,128)(2,1)S(1)}, bf16[2,512,128]{2,1,0:T(8,128)(2,1)S(1)}, u32[]{:S(2)}, u32[]{:S(2)}) collective-permute-start(bf16[2,512,128]{2,1,0:T(8,128)(2,1)S(1)} %collective-permute-done.1.mid_ref), channel_id=1, source_target_pairs={{0,1},{1,0},{2,3},{3,2},{4,5},{5,4},{6,7},{7,6},{8,9},{9,8},{10,11... | collective-permute-start | bytes 786440 | tf_op jit(solution)/shard_map/ppermute | solution.py:195
  (3 other events, 43.3 us)

commit v4 on v3

--- a/solution.py
+++ b/solution.py
@@ -16,6 +16,7 @@
 LOG2_E = 1.4426950408889634
 masked_value = -1e30
 CHUNKS = (2, 2, 2, 2, 2, 2, 2, 2)
+UNROLL = 2
 
 
 def pack_kernel(key_ref, value_ref, out_ref):
@@ -31,6 +32,9 @@
 def pack(key_rows, value_matrix, first, heads):
     length = key_rows.shape[0]
     spec = pl.BlockSpec((length, heads * HEAD_WIDTH), lambda _: (0, first // heads))
+    if first == 0:
+        key_rows = pltpu.with_memory_space_constraint(key_rows, pltpu.HBM)
+        value_matrix = pltpu.with_memory_space_constraint(value_matrix, pltpu.HBM)
     return pl.pallas_call(
         pack_kernel,
         out_shape=jax.ShapeDtypeStruct((heads, 2 * length, HEAD_WIDTH), key_rows.dtype),
@@ -45,8 +49,7 @@
 
 
 def attend_kernel(q_ref, own_ref, far_ref, mid_ref, pair1_ref, pair2_ref, *rest):
-    o_ref, *score_refs = rest[-5:-2]
-    max_refs = rest[-2:]
+    o_ref, score_ref, max_ref = rest[-3:]
     heads, length = own_ref.shape[0], q_ref.shape[0]
     block = lax.axis_index("seq")
     odd = lax.rem(block, 2)
@@ -64,11 +67,12 @@
     query_pos = lax.broadcasted_iota(jnp.int32, (length, length), 1)
     causal = key_pos <= query_pos
 
-    def columns(head, g):
-        return pl.ds(pl.multiple_of((head * GROUP + g) * HEAD_WIDTH, HEAD_WIDTH), HEAD_WIDTH)
-
-    def score(head, g, part, row_max):
-        query = q_ref[:, columns(head, g)]
+    def columns(unit):
+        return pl.ds(pl.multiple_of(unit * HEAD_WIDTH, HEAD_WIDTH), HEAD_WIDTH)
+
+    def score(unit, part, row_max):
+        head = lax.div(unit, GROUP)
+        query = q_ref[:, columns(unit)]
 
         def product(ref):
             return lax.dot_general(
@@ -79,17 +83,18 @@
             raw = jnp.where(causal, product(own_ref), product(far_ref) + far_bias)
         else:
             raw = product(others[part])
-        score_refs[g][part * length : (part + 1) * length] = raw
+        score_ref[part * length : (part + 1) * length] = raw
         largest = jnp.max(raw.reshape(length // 8, 8, length), axis=0) + biases[part]
         return largest if row_max is None else jnp.maximum(row_max, largest)
 
-    def keep_max(g, row_max):
+    def keep_max(row_max):
         row_max = jnp.max(row_max, axis=0, keepdims=True) * scale
-        max_refs[g][...] = jnp.broadcast_to(row_max, max_refs[g].shape)
-
-    def weigh(head, g, part, total):
-        shift = max_refs[g][0:1] - biases[part] * scale
-        weights = jnp.exp2(score_refs[g][part * length : (part + 1) * length] * scale - shift)
+        max_ref[...] = jnp.broadcast_to(row_max, max_ref.shape)
+
+    def weigh(unit, part, total):
+        head = lax.div(unit, GROUP)
+        shift = max_ref[0:1] - biases[part] * scale
+        weights = jnp.exp2(score_ref[part * length : (part + 1) * length] * scale - shift)
         if part == 0:
             pieces = (
                 (own_ref, jnp.where(causal, weights, 0.0)),
@@ -113,29 +118,23 @@
             total = product if total is None else total + product
         return total
 
-    def finish(head, g, total):
-        result = total[:HEAD_WIDTH] / total[HEAD_WIDTH : HEAD_WIDTH + 1]
-        o_ref[:, columns(head, g)] = result.T.astype(o_ref.dtype)
-
-    def overlap(head, g, next_head, next_g):
+    row_max = None
+    for part in range(4):
+        row_max = score(0, part, row_max)
+    keep_max(row_max)
+    units = heads * GROUP
+
+    def step(unit, _):
         row_max = total = None
         for part in range(4):
-            row_max = score(next_head, next_g, part, row_max)
-            total = weigh(head, g, part, total)
-        keep_max(next_g, row_max)
-        finish(head, g, total)
-
-    row_max = None
-    for part in range(4):
-        row_max = score(0, 0, part, row_max)
-    keep_max(0, row_max)
-
-    def step(head, _):
-        overlap(head, 0, head, 1)
-        overlap(head, 1, jnp.minimum(head + 1, heads - 1), 0)
+            total = weigh(unit, part, total)
+            row_max = score(jnp.minimum(unit + 1, units - 1), part, row_max)
+        keep_max(row_max)
+        result = total[:HEAD_WIDTH] / total[HEAD_WIDTH : HEAD_WIDTH + 1]
+        o_ref[:, columns(unit)] = result.T.astype(o_ref.dtype)
         return 0
 
-    lax.fori_loop(0, heads, step, 0)
+    lax.fori_loop(0, units, step, 0, unroll=UNROLL)
 
 
 def attend(queries, pieces, first, heads, output):
@@ -156,8 +155,10 @@
         grid=(1,),
         in_specs=specs,
         out_specs=q_spec,
-        scratch_shapes=[pltpu.VMEM((WINDOW, length), jnp.float32)] * 2
-        + [pltpu.VMEM((8, length), jnp.float32)] * 2,
+        scratch_shapes=[
+            pltpu.VMEM((WINDOW, length), jnp.float32),
+            pltpu.VMEM((8, length), jnp.float32),
+        ],
         input_output_aliases=aliases,
         compiler_params=pltpu.CompilerParams(vmem_limit_bytes=16 << 20),
         cost_estimate=pl.CostEstimate(

time: 116 us -> 114 us (0.983)
  local copies, waits for them, and re-layouts: 2.45 us -> 0.01 us
    unnamed x6, local copies, waits for them, and re-layouts: 2.45 us -> 0.01 us
where the time goes in v4:
time: 114 us
  waiting for transfers between devices  64.4 us (56%)
  Pallas kernels  26.7 us (23%)
  starting transfers between devices  22.3 us (20%)
    ppermute x32, waiting for transfers between devices, send(): return lax.ppermute(piece, 'seq', pairs)  64.4 us
    pallas_call x8, Pallas kernels, attend(): pl.pallas_call(attend_kernel, out_shape=jax.ShapeDtypeStruct(queries.shap...  24.7 us
    ppermute x32, starting transfers between devices, send(): return lax.ppermute(piece, 'seq', pairs)  22.3 us
  transfers between devices with their start and end apart: 32, of which 14 were waited for; matrix products, arithmetic and copies ran while one was open for 0% of the time, Pallas kernels for 20%

profile of v4, /device:TPU:0, one launch (start us, length us, event | category | flops | bytes accessed | tf_op | source)
XLA Modules:
  0.0 113.9 jit_solution(10046287325108469617)
XLA Ops:
  1.2 3.1 %collective-permute-start.28 = (bf16[2,512,128]{2,1,0:T(8,128)(2,1)S(1)}, bf16[2,512,128]{2,1,0:T(8,128)(2,1)S(1)}, u32[]{:S(2)}, u32[]{:S(2)}) collective-permute-start(bf16[2,512,128]{2,1,0:T(8,128)(2,1)S(1)} %shard_map.44.own_ref), channel_id=1, source_target_pairs={{0,4},{1,5},{2,6},{3,7},{4,8},{5,9},{6,10},{7,11},{8,12},{9,13},{1... | collective-permute-start | bytes 786440 | tf_op jit(solution)/shard_map/ppermute | solution.py:196
  4.5 1.6 %collective-permute-start.24 = (bf16[2,512,128]{2,1,0:T(8,128)(2,1)S(1)}, bf16[2,512,128]{2,1,0:T(8,128)(2,1)S(1)}, u32[]{:S(2)}, u32[]{:S(2)}) collective-permute-start(bf16[2,512,128]{2,1,0:T(8,128)(2,1)S(1)} %shard_map.43.own_ref), channel_id=1, source_target_pairs={{0,4},{1,5},{2,6},{3,7},{4,8},{5,9},{6,10},{7,11},{8,12},{9,13},{1... | collective-permute-start | bytes 786440 | tf_op jit(solution)/shard_map/ppermute | solution.py:196
  6.2 1.6 %collective-permute-start.20 = (bf16[2,512,128]{2,1,0:T(8,128)(2,1)S(1)}, bf16[2,512,128]{2,1,0:T(8,128)(2,1)S(1)}, u32[]{:S(2)}, u32[]{:S(2)}) collective-permute-start(bf16[2,512,128]{2,1,0:T(8,128)(2,1)S(1)} %shard_map.42.own_ref), channel_id=1, source_target_pairs={{0,4},{1,5},{2,6},{3,7},{4,8},{5,9},{6,10},{7,11},{8,12},{9,13},{1... | collective-permute-start | bytes 786440 | tf_op jit(solution)/shard_map/ppermute | solution.py:196
  10.3 3.2 %collective-permute-done.28.far_ref = bf16[2,512,128]{2,1,0:T(8,128)(2,1)S(1)} collective-permute-done((bf16[2,512,128]{2,1,0:T(8,128)(2,1)S(1)}, bf16[2,512,128]{2,1,0:T(8,128)(2,1)S(1)}, u32[]{:S(2)}, u32[]{:S(2)}) %collective-permute-start.28) | collective-permute-done | bytes 262176 | tf_op jit(solution)/shard_map/ppermute | solution.py:196
  13.6 5.6 %collective-permute-done.24.far_ref = bf16[2,512,128]{2,1,0:T(8,128)(2,1)S(1)} collective-permute-done((bf16[2,512,128]{2,1,0:T(8,128)(2,1)S(1)}, bf16[2,512,128]{2,1,0:T(8,128)(2,1)S(1)}, u32[]{:S(2)}, u32[]{:S(2)}) %collective-permute-start.24) | collective-permute-done | bytes 262176 | tf_op jit(solution)/shard_map/ppermute | solution.py:196
  19.2 5.6 %collective-permute-done.20.far_ref = bf16[2,512,128]{2,1,0:T(8,128)(2,1)S(1)} collective-permute-done((bf16[2,512,128]{2,1,0:T(8,128)(2,1)S(1)}, bf16[2,512,128]{2,1,0:T(8,128)(2,1)S(1)}, u32[]{:S(2)}, u32[]{:S(2)}) %collective-permute-start.20) | collective-permute-done | bytes 262176 | tf_op jit(solution)/shard_map/ppermute | solution.py:196
  24.8 5.6 %collective-permute-done.16.far_ref = bf16[2,512,128]{2,1,0:T(8,128)(2,1)S(1)} collective-permute-done((bf16[2,512,128]{2,1,0:T(8,128)(2,1)S(1)}, bf16[2,512,128]{2,1,0:T(8,128)(2,1)S(1)}, u32[]{:S(2)}, u32[]{:S(2)}) %collective-permute-start.16) | collective-permute-done | bytes 262176 | tf_op jit(solution)/shard_map/ppermute | solution.py:196
  30.4 1.7 %collective-permute-start.29 = (bf16[2,512,128]{2,1,0:T(8,128)(2,1)S(1)}, bf16[2,512,128]{2,1,0:T(8,128)(2,1)S(1)}, u32[]{:S(2)}, u32[]{:S(2)}) collective-permute-start(bf16[2,512,128]{2,1,0:T(8,128)(2,1)S(1)} %get-tuple-element.14), channel_id=1, source_target_pairs={{0,2},{1,3},{2,0},{3,1},{4,6},{5,7},{6,4},{7,5},{8,10},{9,11},{10,... | collective-permute-start | bytes 786440 | tf_op jit(solution)/shard_map/ppermute | solution.py:196
  32.1 3.9 %collective-permute-done.12.far_ref = bf16[2,512,128]{2,1,0:T(8,128)(2,1)S(1)} collective-permute-done((bf16[2,512,128]{2,1,0:T(8,128)(2,1)S(1)}, bf16[2,512,128]{2,1,0:T(8,128)(2,1)S(1)}, u32[]{:S(2)}, u32[]{:S(2)}) %collective-permute-start.12) | collective-permute-done | bytes 262176 | tf_op jit(solution)/shard_map/ppermute | solution.py:196
  36.0 5.6 %collective-permute-done.8.far_ref = bf16[2,512,128]{2,1,0:T(8,128)(2,1)S(1)} collective-permute-done((bf16[2,512,128]{2,1,0:T(8,128)(2,1)S(1)}, bf16[2,512,128]{2,1,0:T(8,128)(2,1)S(1)}, u32[]{:S(2)}, u32[]{:S(2)}) %collective-permute-start.8) | collective-permute-done | bytes 262176 | tf_op jit(solution)/shard_map/ppermute | solution.py:196
  41.6 1.7 %collective-permute-start.25 = (bf16[2,512,128]{2,1,0:T(8,128)(2,1)S(1)}, bf16[2,512,128]{2,1,0:T(8,128)(2,1)S(1)}, u32[]{:S(2)}, u32[]{:S(2)}) collective-permute-start(bf16[2,512,128]{2,1,0:T(8,128)(2,1)S(1)} %get-tuple-element.16), channel_id=1, source_target_pairs={{0,2},{1,3},{2,0},{3,1},{4,6},{5,7},{6,4},{7,5},{8,10},{9,11},{10,... | collective-permute-start | bytes 786440 | tf_op jit(solution)/shard_map/ppermute | solution.py:196
  43.4 3.9 %collective-permute-done.4.far_ref = bf16[2,512,128]{2,1,0:T(8,128)(2,1)S(1)} collective-permute-done((bf16[2,512,128]{2,1,0:T(8,128)(2,1)S(1)}, bf16[2,512,128]{2,1,0:T(8,128)(2,1)S(1)}, u32[]{:S(2)}, u32[]{:S(2)}) %collective-permute-start.4) | collective-permute-done | bytes 262176 | tf_op jit(solution)/shard_map/ppermute | solution.py:196
  47.3 4.7 %collective-permute-done.far_ref = bf16[2,512,128]{2,1,0:T(8,128)(2,1)S(1)} collective-permute-done((bf16[2,512,128]{2,1,0:T(8,128)(2,1)S(1)}, bf16[2,512,128]{2,1,0:T(8,128)(2,1)S(1)}, u32[]{:S(2)}, u32[]{:S(2)}) %collective-permute-start) | collective-permute-done | bytes 262176 | tf_op jit(solution)/shard_map/ppermute | solution.py:196
  52.0 1.5 %collective-permute-start.21 = (bf16[2,512,128]{2,1,0:T(8,128)(2,1)S(1)}, bf16[2,512,128]{2,1,0:T(8,128)(2,1)S(1)}, u32[]{:S(2)}, u32[]{:S(2)}) collective-permute-start(bf16[2,512,128]{2,1,0:T(8,128)(2,1)S(1)} %get-tuple-element.18), channel_id=1, source_target_pairs={{0,2},{1,3},{2,0},{3,1},{4,6},{5,7},{6,4},{7,5},{8,10},{9,11},{10,... | collective-permute-start | bytes 786440 | tf_op jit(solution)/shard_map/ppermute | solution.py:196
  54.4 1.5 %collective-permute-start.13 = (bf16[2,512,128]{2,1,0:T(8,128)(2,1)S(1)}, bf16[2,512,128]{2,1,0:T(8,128)(2,1)S(1)}, u32[]{:S(2)}, u32[]{:S(2)}) collective-permute-start(bf16[2,512,128]{2,1,0:T(8,128)(2,1)S(1)} %get-tuple-element.22), channel_id=1, source_target_pairs={{0,2},{1,3},{2,0},{3,1},{4,6},{5,7},{6,4},{7,5},{8,10},{9,11},{10,... | collective-permute-start | bytes 786440 | tf_op jit(solution)/shard_map/ppermute | solution.py:196
  55.9 5.2 %collective-permute-done.21.mid_ref = bf16[2,512,128]{2,1,0:T(8,128)(2,1)S(1)} collective-permute-done((bf16[2,512,128]{2,1,0:T(8,128)(2,1)S(1)}, bf16[2,512,128]{2,1,0:T(8,128)(2,1)S(1)}, u32[]{:S(2)}, u32[]{:S(2)}) %collective-permute-start.21) | collective-permute-done | bytes 262176 | tf_op jit(solution)/shard_map/ppermute | solution.py:196
  61.2 1.5 %collective-permute-start.9 = (bf16[2,512,128]{2,1,0:T(8,128)(2,1)S(1)}, bf16[2,512,128]{2,1,0:T(8,128)(2,1)S(1)}, u32[]{:S(2)}, u32[]{:S(2)}) collective-permute-start(bf16[2,512,128]{2,1,0:T(8,128)(2,1)S(1)} %get-tuple-element.24), channel_id=1, source_target_pairs={{0,2},{1,3},{2,0},{3,1},{4,6},{5,7},{6,4},{7,5},{8,10},{9,11},{10,... | collective-permute-start | bytes 786440 | tf_op jit(solution)/shard_map/ppermute | solution.py:196
  62.7 4.1 %collective-permute-done.17.mid_ref = bf16[2,512,128]{2,1,0:T(8,128)(2,1)S(1)} collective-permute-done((bf16[2,512,128]{2,1,0:T(8,128)(2,1)S(1)}, bf16[2,512,128]{2,1,0:T(8,128)(2,1)S(1)}, u32[]{:S(2)}, u32[]{:S(2)}) %collective-permute-start.17) | collective-permute-done | bytes 262176 | tf_op jit(solution)/shard_map/ppermute | solution.py:196
  66.8 1.6 %collective-permute-start.5 = (bf16[2,512,128]{2,1,0:T(8,128)(2,1)S(1)}, bf16[2,512,128]{2,1,0:T(8,128)(2,1)S(1)}, u32[]{:S(2)}, u32[]{:S(2)}) collective-permute-start(bf16[2,512,128]{2,1,0:T(8,128)(2,1)S(1)} %get-tuple-element.26), channel_id=1, source_target_pairs={{0,2},{1,3},{2,0},{3,1},{4,6},{5,7},{6,4},{7,5},{8,10},{9,11},{10,... | collective-permute-start | bytes 786440 | tf_op jit(solution)/shard_map/ppermute | solution.py:196
  68.4 4.0 %collective-permute-done.13.mid_ref = bf16[2,512,128]{2,1,0:T(8,128)(2,1)S(1)} collective-permute-done((bf16[2,512,128]{2,1,0:T(8,128)(2,1)S(1)}, bf16[2,512,128]{2,1,0:T(8,128)(2,1)S(1)}, u32[]{:S(2)}, u32[]{:S(2)}) %collective-permute-start.13) | collective-permute-done | bytes 262176 | tf_op jit(solution)/shard_map/ppermute | solution.py:196
  72.4 1.5 %collective-permute-start.1 = (bf16[2,512,128]{2,1,0:T(8,128)(2,1)S(1)}, bf16[2,512,128]{2,1,0:T(8,128)(2,1)S(1)}, u32[]{:S(2)}, u32[]{:S(2)}) collective-permute-start(bf16[2,512,128]{2,1,0:T(8,128)(2,1)S(1)} %get-tuple-element.28), channel_id=1, source_target_pairs={{0,2},{1,3},{2,0},{3,1},{4,6},{5,7},{6,4},{7,5},{8,10},{9,11},{10,... | collective-permute-start | bytes 786440 | tf_op jit(solution)/shard_map/ppermute | solution.py:196
  73.9 4.1 %collective-permute-done.9.mid_ref = bf16[2,512,128]{2,1,0:T(8,128)(2,1)S(1)} collective-permute-done((bf16[2,512,128]{2,1,0:T(8,128)(2,1)S(1)}, bf16[2,512,128]{2,1,0:T(8,128)(2,1)S(1)}, u32[]{:S(2)}, u32[]{:S(2)}) %collective-permute-start.9) | collective-permute-done | bytes 262176 | tf_op jit(solution)/shard_map/ppermute | solution.py:196
  78.5 5.1 %collective-permute-done.5.mid_ref = bf16[2,512,128]{2,1,0:T(8,128)(2,1)S(1)} collective-permute-done((bf16[2,512,128]{2,1,0:T(8,128)(2,1)S(1)}, bf16[2,512,128]{2,1,0:T(8,128)(2,1)S(1)}, u32[]{:S(2)}, u32[]{:S(2)}) %collective-permute-start.5) | collective-permute-done | bytes 262176 | tf_op jit(solution)/shard_map/ppermute | solution.py:196
  83.6 3.9 %collective-permute-done.1.mid_ref = bf16[2,512,128]{2,1,0:T(8,128)(2,1)S(1)} collective-permute-done((bf16[2,512,128]{2,1,0:T(8,128)(2,1)S(1)}, bf16[2,512,128]{2,1,0:T(8,128)(2,1)S(1)}, u32[]{:S(2)}, u32[]{:S(2)}) %collective-permute-start.1) | collective-permute-done | bytes 262176 | tf_op jit(solution)/shard_map/ppermute | solution.py:196
  88.1 3.1 %shard_map.45.rest_0_ = bf16[256,4096]{1,0:T(8,128)(2,1)} custom-call(bf16[256,4096]{1,0:T(8,128)(2,1)S(1)} %copy-done, bf16[2,512,128]{2,1,0:T(8,128)(2,1)S(1)} %shard_map.44.own_ref, bf16[2,512,128]{2,1,0:T(8,128)(2,1)S(1)} %collective-permute-done.28.far_ref, bf16[2,512,128]{2,1,0:T(8,128)(2,1)S(1)} %collective-permute-done.29.mid_ref, ...), custom_call_target="tpu_custom_call" | custom-call | flops 671088640 | bytes 1835008 | tf_op jit(solution)/shard_map/pallas_call | solution.py:152
  91.7 3.1 %shard_map.46.rest_0_ = bf16[256,4096]{1,0:T(8,128)(2,1)} custom-call(bf16[256,4096]{1,0:T(8,128)(2,1)S(1)} %copy-done, bf16[2,512,128]{2,1,0:T(8,128)(2,1)S(1)} %shard_map.43.own_ref, bf16[2,512,128]{2,1,0:T(8,128)(2,1)S(1)} %collective-permute-done.24.far_ref, ...), custom_call_target="tpu_custom_call", output_to_operand_aliasing={{}: (6, {})} | custom-call | flops 671088640 | bytes 1835008 | tf_op jit(solution)/shard_map/pallas_call | solution.py:152
  95.3 3.1 %shard_map.47.rest_0_ = bf16[256,4096]{1,0:T(8,128)(2,1)} custom-call(bf16[256,4096]{1,0:T(8,128)(2,1)S(1)} %copy-done, bf16[2,512,128]{2,1,0:T(8,128)(2,1)S(1)} %shard_map.42.own_ref, bf16[2,512,128]{2,1,0:T(8,128)(2,1)S(1)} %collective-permute-done.20.far_ref, ...), custom_call_target="tpu_custom_call", output_to_operand_aliasing={{}: (6, {})} | custom-call | flops 671088640 | bytes 1835008 | tf_op jit(solution)/shard_map/pallas_call | solution.py:152
  98.4 3.1 %shard_map.48.rest_0_ = bf16[256,4096]{1,0:T(8,128)(2,1)} custom-call(bf16[256,4096]{1,0:T(8,128)(2,1)S(1)} %copy-done, bf16[2,512,128]{2,1,0:T(8,128)(2,1)S(1)} %shard_map.41.own_ref, bf16[2,512,128]{2,1,0:T(8,128)(2,1)S(1)} %collective-permute-done.16.far_ref, ...), custom_call_target="tpu_custom_call", output_to_operand_aliasing={{}: (6, {})} | custom-call | flops 671088640 | bytes 1835008 | tf_op jit(solution)/shard_map/pallas_call | solution.py:152
  101.5 3.1 %shard_map.49.rest_0_ = bf16[256,4096]{1,0:T(8,128)(2,1)} custom-call(bf16[256,4096]{1,0:T(8,128)(2,1)S(1)} %copy-done, bf16[2,512,128]{2,1,0:T(8,128)(2,1)S(1)} %shard_map.40.own_ref, bf16[2,512,128]{2,1,0:T(8,128)(2,1)S(1)} %collective-permute-done.12.far_ref, ...), custom_call_target="tpu_custom_call", output_to_operand_aliasing={{}: (6, {})} | custom-call | flops 671088640 | bytes 1835008 | tf_op jit(solution)/shard_map/pallas_call | solution.py:152
  104.6 3.1 %shard_map.50.rest_0_ = bf16[256,4096]{1,0:T(8,128)(2,1)} custom-call(bf16[256,4096]{1,0:T(8,128)(2,1)S(1)} %copy-done, bf16[2,512,128]{2,1,0:T(8,128)(2,1)S(1)} %shard_map.39.own_ref, bf16[2,512,128]{2,1,0:T(8,128)(2,1)S(1)} %collective-permute-done.8.far_ref, ...), custom_call_target="tpu_custom_call", output_to_operand_aliasing={{}: (6, {})} | custom-call | flops 671088640 | bytes 1835008 | tf_op jit(solution)/shard_map/pallas_call | solution.py:152
  107.7 3.1 %shard_map.51.rest_0_ = bf16[256,4096]{1,0:T(8,128)(2,1)} custom-call(bf16[256,4096]{1,0:T(8,128)(2,1)S(1)} %copy-done, bf16[2,512,128]{2,1,0:T(8,128)(2,1)S(1)} %shard_map.38.own_ref, bf16[2,512,128]{2,1,0:T(8,128)(2,1)S(1)} %collective-permute-done.4.far_ref, ...), custom_call_target="tpu_custom_call", output_to_operand_aliasing={{}: (6, {})} | custom-call | flops 671088640 | bytes 1835008 | tf_op jit(solution)/shard_map/pallas_call | solution.py:152
  110.8 3.1 %shard_map.52 = bf16[256,4096]{1,0:T(8,128)(2,1)} custom-call(bf16[256,4096]{1,0:T(8,128)(2,1)S(1)} %copy-done, bf16[2,512,128]{2,1,0:T(8,128)(2,1)S(1)} %shard_map.37.own_ref, bf16[2,512,128]{2,1,0:T(8,128)(2,1)S(1)} %collective-permute-done.far_ref, bf16[2,512,128]{2,1,0:T(8,128)(2,1)S(1)} %collective-permute-done.1.mid_ref, ...), custom_call_target="tpu_custom_call", output_to_operand_aliasing={{}: (6, {})} | custom-call | flops 671088640 | bytes 1835008 | tf_op jit(solution)/shard_map/pallas_call | solution.py:152
  (62 shorter events, 7.2 us)
Async XLA Ops:
  1.2 12.3 %collective-permute-start.28 = (bf16[2,512,128]{2,1,0:T(8,128)(2,1)S(1)}, bf16[2,512,128]{2,1,0:T(8,128)(2,1)S(1)}, u32[]{:S(2)}, u32[]{:S(2)}) collective-permute-start(bf16[2,512,128]{2,1,0:T(8,128)(2,1)S(1)} %shard_map.44.own_ref), channel_id=1, source_target_pairs={{0,4},{1,5},{2,6},{3,7},{4,8},{5,9},{6,10},{7,11},{8,12},{9,13},{1... | collective-permute-start | bytes 786440 | tf_op jit(solution)/shard_map/ppermute | solution.py:196
  4.5 14.7 %collective-permute-start.24 = (bf16[2,512,128]{2,1,0:T(8,128)(2,1)S(1)}, bf16[2,512,128]{2,1,0:T(8,128)(2,1)S(1)}, u32[]{:S(2)}, u32[]{:S(2)}) collective-permute-start(bf16[2,512,128]{2,1,0:T(8,128)(2,1)S(1)} %shard_map.43.own_ref), channel_id=1, source_target_pairs={{0,4},{1,5},{2,6},{3,7},{4,8},{5,9},{6,10},{7,11},{8,12},{9,13},{1... | collective-permute-start | bytes 786440 | tf_op jit(solution)/shard_map/ppermute | solution.py:196
  6.2 18.5 %collective-permute-start.20 = (bf16[2,512,128]{2,1,0:T(8,128)(2,1)S(1)}, bf16[2,512,128]{2,1,0:T(8,128)(2,1)S(1)}, u32[]{:S(2)}, u32[]{:S(2)}) collective-permute-start(bf16[2,512,128]{2,1,0:T(8,128)(2,1)S(1)} %shard_map.42.own_ref), channel_id=1, source_target_pairs={{0,4},{1,5},{2,6},{3,7},{4,8},{5,9},{6,10},{7,11},{8,12},{9,13},{1... | collective-permute-start | bytes 786440 | tf_op jit(solution)/shard_map/ppermute | solution.py:196
  8.0 22.4 %collective-permute-start.16 = (bf16[2,512,128]{2,1,0:T(8,128)(2,1)S(1)}, bf16[2,512,128]{2,1,0:T(8,128)(2,1)S(1)}, u32[]{:S(2)}, u32[]{:S(2)}) collective-permute-start(bf16[2,512,128]{2,1,0:T(8,128)(2,1)S(1)} %shard_map.41.own_ref), channel_id=1, source_target_pairs={{0,4},{1,5},{2,6},{3,7},{4,8},{5,9},{6,10},{7,11},{8,12},{9,13},{1... | collective-permute-start | bytes 786440 | tf_op jit(solution)/shard_map/ppermute | solution.py:196
  8.5 27.5 %collective-permute-start.12 = (bf16[2,512,128]{2,1,0:T(8,128)(2,1)S(1)}, bf16[2,512,128]{2,1,0:T(8,128)(2,1)S(1)}, u32[]{:S(2)}, u32[]{:S(2)}) collective-permute-start(bf16[2,512,128]{2,1,0:T(8,128)(2,1)S(1)} %shard_map.40.own_ref), channel_id=1, source_target_pairs={{0,4},{1,5},{2,6},{3,7},{4,8},{5,9},{6,10},{7,11},{8,12},{9,13},{1... | collective-permute-start | bytes 786440 | tf_op jit(solution)/shard_map/ppermute | solution.py:196
  13.5 28.1 %collective-permute-start.8 = (bf16[2,512,128]{2,1,0:T(8,128)(2,1)S(1)}, bf16[2,512,128]{2,1,0:T(8,128)(2,1)S(1)}, u32[]{:S(2)}, u32[]{:S(2)}) collective-permute-start(bf16[2,512,128]{2,1,0:T(8,128)(2,1)S(1)} %shard_map.39.own_ref), channel_id=1, source_target_pairs={{0,4},{1,5},{2,6},{3,7},{4,8},{5,9},{6,10},{7,11},{8,12},{9,13},{1... | collective-permute-start | bytes 786440 | tf_op jit(solution)/shard_map/ppermute | solution.py:196
  19.1 28.1 %collective-permute-start.4 = (bf16[2,512,128]{2,1,0:T(8,128)(2,1)S(1)}, bf16[2,512,128]{2,1,0:T(8,128)(2,1)S(1)}, u32[]{:S(2)}, u32[]{:S(2)}) collective-permute-start(bf16[2,512,128]{2,1,0:T(8,128)(2,1)S(1)} %shard_map.38.own_ref), channel_id=1, source_target_pairs={{0,4},{1,5},{2,6},{3,7},{4,8},{5,9},{6,10},{7,11},{8,12},{9,13},{1... | collective-permute-start | bytes 786440 | tf_op jit(solution)/shard_map/ppermute | solution.py:196
  24.8 27.2 %collective-permute-start = (bf16[2,512,128]{2,1,0:T(8,128)(2,1)S(1)}, bf16[2,512,128]{2,1,0:T(8,128)(2,1)S(1)}, u32[]{:S(2)}, u32[]{:S(2)}) collective-permute-start(bf16[2,512,128]{2,1,0:T(8,128)(2,1)S(1)} %shard_map.37.own_ref), channel_id=1, source_target_pairs={{0,4},{1,5},{2,6},{3,7},{4,8},{5,9},{6,10},{7,11},{8,12},{9,13},{1... | collective-permute-start | bytes 786440 | tf_op jit(solution)/shard_map/ppermute | solution.py:196
  30.4 23.1 %collective-permute-start.29 = (bf16[2,512,128]{2,1,0:T(8,128)(2,1)S(1)}, bf16[2,512,128]{2,1,0:T(8,128)(2,1)S(1)}, u32[]{:S(2)}, u32[]{:S(2)}) collective-permute-start(bf16[2,512,128]{2,1,0:T(8,128)(2,1)S(1)} %get-tuple-element.14), channel_id=1, source_target_pairs={{0,2},{1,3},{2,0},{3,1},{4,6},{5,7},{6,4},{7,5},{8,10},{9,11},{10,... | collective-permute-start | bytes 786440 | tf_op jit(solution)/shard_map/ppermute | solution.py:196
  36.0 17.5 %collective-permute-start.30 = (bf16[2,512,128]{2,1,0:T(8,128)(2,1)S(1)}, bf16[2,512,128]{2,1,0:T(8,128)(2,1)S(1)}, u32[]{:S(2)}, u32[]{:S(2)}) collective-permute-start(bf16[2,512,128]{2,1,0:T(8,128)(2,1)S(1)} %get-tuple-element.13), channel_id=1, source_target_pairs={{0,1},{1,0},{2,3},{3,2},{4,5},{5,4},{6,7},{7,6},{8,9},{9,8},{10,11... | collective-permute-start | bytes 786440 | tf_op jit(solution)/shard_map/ppermute | solution.py:196
  41.6 12.5 %collective-permute-start.25 = (bf16[2,512,128]{2,1,0:T(8,128)(2,1)S(1)}, bf16[2,512,128]{2,1,0:T(8,128)(2,1)S(1)}, u32[]{:S(2)}, u32[]{:S(2)}) collective-permute-start(bf16[2,512,128]{2,1,0:T(8,128)(2,1)S(1)} %get-tuple-element.16), channel_id=1, source_target_pairs={{0,2},{1,3},{2,0},{3,1},{4,6},{5,7},{6,4},{7,5},{8,10},{9,11},{10,... | collective-permute-start | bytes 786440 | tf_op jit(solution)/shard_map/ppermute | solution.py:196
  47.2 7.2 %collective-permute-start.26 = (bf16[2,512,128]{2,1,0:T(8,128)(2,1)S(1)}, bf16[2,512,128]{2,1,0:T(8,128)(2,1)S(1)}, u32[]{:S(2)}, u32[]{:S(2)}) collective-permute-start(bf16[2,512,128]{2,1,0:T(8,128)(2,1)S(1)} %get-tuple-element.15), channel_id=1, source_target_pairs={{0,1},{1,0},{2,3},{3,2},{4,5},{5,4},{6,7},{7,6},{8,9},{9,8},{10,11... | collective-permute-start | bytes 786440 | tf_op jit(solution)/shard_map/ppermute | solution.py:196
  52.0 9.2 %collective-permute-start.21 = (bf16[2,512,128]{2,1,0:T(8,128)(2,1)S(1)}, bf16[2,512,128]{2,1,0:T(8,128)(2,1)S(1)}, u32[]{:S(2)}, u32[]{:S(2)}) collective-permute-start(bf16[2,512,128]{2,1,0:T(8,128)(2,1)S(1)} %get-tuple-element.18), channel_id=1, source_target_pairs={{0,2},{1,3},{2,0},{3,1},{4,6},{5,7},{6,4},{7,5},{8,10},{9,11},{10,... | collective-permute-start | bytes 786440 | tf_op jit(solution)/shard_map/ppermute | solution.py:196
  53.5 7.7 %collective-permute-start.22 = (bf16[2,512,128]{2,1,0:T(8,128)(2,1)S(1)}, bf16[2,512,128]{2,1,0:T(8,128)(2,1)S(1)}, u32[]{:S(2)}, u32[]{:S(2)}) collective-permute-start(bf16[2,512,128]{2,1,0:T(8,128)(2,1)S(1)} %get-tuple-element.17), channel_id=1, source_target_pairs={{0,1},{1,0},{2,3},{3,2},{4,5},{5,4},{6,7},{7,6},{8,9},{9,8},{10,11... | collective-permute-start | bytes 786440 | tf_op jit(solution)/shard_map/ppermute | solution.py:196
  53.5 13.3 %collective-permute-start.17 = (bf16[2,512,128]{2,1,0:T(8,128)(2,1)S(1)}, bf16[2,512,128]{2,1,0:T(8,128)(2,1)S(1)}, u32[]{:S(2)}, u32[]{:S(2)}) collective-permute-start(bf16[2,512,128]{2,1,0:T(8,128)(2,1)S(1)} %get-tuple-element.20), channel_id=1, source_target_pairs={{0,2},{1,3},{2,0},{3,1},{4,6},{5,7},{6,4},{7,5},{8,10},{9,11},{10,... | collective-permute-start | bytes 786440 | tf_op jit(solution)/shard_map/ppermute | solution.py:196
  54.2 12.7 %collective-permute-start.18 = (bf16[2,512,128]{2,1,0:T(8,128)(2,1)S(1)}, bf16[2,512,128]{2,1,0:T(8,128)(2,1)S(1)}, u32[]{:S(2)}, u32[]{:S(2)}) collective-permute-start(bf16[2,512,128]{2,1,0:T(8,128)(2,1)S(1)} %get-tuple-element.19), channel_id=1, source_target_pairs={{0,1},{1,0},{2,3},{3,2},{4,5},{5,4},{6,7},{7,6},{8,9},{9,8},{10,11... | collective-permute-start | bytes 786440 | tf_op jit(solution)/shard_map/ppermute | solution.py:196
  54.4 18.0 %collective-permute-start.13 = (bf16[2,512,128]{2,1,0:T(8,128)(2,1)S(1)}, bf16[2,512,128]{2,1,0:T(8,128)(2,1)S(1)}, u32[]{:S(2)}, u32[]{:S(2)}) collective-permute-start(bf16[2,512,128]{2,1,0:T(8,128)(2,1)S(1)} %get-tuple-element.22), channel_id=1, source_target_pairs={{0,2},{1,3},{2,0},{3,1},{4,6},{5,7},{6,4},{7,5},{8,10},{9,11},{10,... | collective-permute-start | bytes 786440 | tf_op jit(solution)/shard_map/ppermute | solution.py:196
  61.2 12.8 %collective-permute-start.14 = (bf16[2,512,128]{2,1,0:T(8,128)(2,1)S(1)}, bf16[2,512,128]{2,1,0:T(8,128)(2,1)S(1)}, u32[]{:S(2)}, u32[]{:S(2)}) collective-permute-start(bf16[2,512,128]{2,1,0:T(8,128)(2,1)S(1)} %get-tuple-element.21), channel_id=1, source_target_pairs={{0,1},{1,0},{2,3},{3,2},{4,5},{5,4},{6,7},{7,6},{8,9},{9,8},{10,11... | collective-permute-start | bytes 786440 | tf_op jit(solution)/shard_map/ppermute | solution.py:196
  61.2 16.8 %collective-permute-start.9 = (bf16[2,512,128]{2,1,0:T(8,128)(2,1)S(1)}, bf16[2,512,128]{2,1,0:T(8,128)(2,1)S(1)}, u32[]{:S(2)}, u32[]{:S(2)}) collective-permute-start(bf16[2,512,128]{2,1,0:T(8,128)(2,1)S(1)} %get-tuple-element.24), channel_id=1, source_target_pairs={{0,2},{1,3},{2,0},{3,1},{4,6},{5,7},{6,4},{7,5},{8,10},{9,11},{10,... | collective-permute-start | bytes 786440 | tf_op jit(solution)/shard_map/ppermute | solution.py:196
  66.8 11.2 %collective-permute-start.10 = (bf16[2,512,128]{2,1,0:T(8,128)(2,1)S(1)}, bf16[2,512,128]{2,1,0:T(8,128)(2,1)S(1)}, u32[]{:S(2)}, u32[]{:S(2)}) collective-permute-start(bf16[2,512,128]{2,1,0:T(8,128)(2,1)S(1)} %get-tuple-element.23), channel_id=1, source_target_pairs={{0,1},{1,0},{2,3},{3,2},{4,5},{5,4},{6,7},{7,6},{8,9},{9,8},{10,11... | collective-permute-start | bytes 786440 | tf_op jit(solution)/shard_map/ppermute | solution.py:196
  66.8 16.8 %collective-permute-start.5 = (bf16[2,512,128]{2,1,0:T(8,128)(2,1)S(1)}, bf16[2,512,128]{2,1,0:T(8,128)(2,1)S(1)}, u32[]{:S(2)}, u32[]{:S(2)}) collective-permute-start(bf16[2,512,128]{2,1,0:T(8,128)(2,1)S(1)} %get-tuple-element.26), channel_id=1, source_target_pairs={{0,2},{1,3},{2,0},{3,1},{4,6},{5,7},{6,4},{7,5},{8,10},{9,11},{10,... | collective-permute-start | bytes 786440 | tf_op jit(solution)/shard_map/ppermute | solution.py:196
  72.4 15.1 %collective-permute-start.1 = (bf16[2,512,128]{2,1,0:T(8,128)(2,1)S(1)}, bf16[2,512,128]{2,1,0:T(8,128)(2,1)S(1)}, u32[]{:S(2)}, u32[]{:S(2)}) collective-permute-start(bf16[2,512,128]{2,1,0:T(8,128)(2,1)S(1)} %get-tuple-element.28), channel_id=1, source_target_pairs={{0,2},{1,3},{2,0},{3,1},{4,6},{5,7},{6,4},{7,5},{8,10},{9,11},{10,... | collective-permute-start | bytes 786440 | tf_op jit(solution)/shard_map/ppermute | solution.py:196
  73.9 13.6 %collective-permute-start.31 = (bf16[2,512,128]{2,1,0:T(8,128)(2,1)S(1)}, bf16[2,512,128]{2,1,0:T(8,128)(2,1)S(1)}, u32[]{:S(2)}, u32[]{:S(2)}) collective-permute-start(bf16[2,512,128]{2,1,0:T(8,128)(2,1)S(1)} %collective-permute-done.29.mid_ref), channel_id=1, source_target_pairs={{0,1},{1,0},{2,3},{3,2},{4,5},{5,4},{6,7},{7,6},{8,9},{9,8},{10,11... | collective-permute-start | bytes 786440 | tf_op jit(solution)/shard_map/ppermute | solution.py:196
  78.0 13.1 %collective-permute-start.27 = (bf16[2,512,128]{2,1,0:T(8,128)(2,1)S(1)}, bf16[2,512,128]{2,1,0:T(8,128)(2,1)S(1)}, u32[]{:S(2)}, u32[]{:S(2)}) collective-permute-start(bf16[2,512,128]{2,1,0:T(8,128)(2,1)S(1)} %collective-permute-done.25.mid_ref), channel_id=1, source_target_pairs={{0,1},{1,0},{2,3},{3,2},{4,5},{5,4},{6,7},{7,6},{8,9},{9,8},{10,11... | collective-permute-start | bytes 786440 | tf_op jit(solution)/shard_map/ppermute | solution.py:196
  78.0 13.1 %collective-permute-start.23 = (bf16[2,512,128]{2,1,0:T(8,128)(2,1)S(1)}, bf16[2,512,128]{2,1,0:T(8,128)(2,1)S(1)}, u32[]{:S(2)}, u32[]{:S(2)}) collective-permute-start(bf16[2,512,128]{2,1,0:T(8,128)(2,1)S(1)} %collective-permute-done.21.mid_ref), channel_id=1, source_target_pairs={{0,1},{1,0},{2,3},{3,2},{4,5},{5,4},{6,7},{7,6},{8,9},{9,8},{10,11... | collective-permute-start | bytes 786440 | tf_op jit(solution)/shard_map/ppermute | solution.py:196
  83.6 11.1 %collective-permute-start.19 = (bf16[2,512,128]{2,1,0:T(8,128)(2,1)S(1)}, bf16[2,512,128]{2,1,0:T(8,128)(2,1)S(1)}, u32[]{:S(2)}, u32[]{:S(2)}) collective-permute-start(bf16[2,512,128]{2,1,0:T(8,128)(2,1)S(1)} %collective-permute-done.17.mid_ref), channel_id=1, source_target_pairs={{0,1},{1,0},{2,3},{3,2},{4,5},{5,4},{6,7},{7,6},{8,9},{9,8},{10,11... | collective-permute-start | bytes 786440 | tf_op jit(solution)/shard_map/ppermute | solution.py:196
  87.6 7.3 %collective-permute-start.15 = (bf16[2,512,128]{2,1,0:T(8,128)(2,1)S(1)}, bf16[2,512,128]{2,1,0:T(8,128)(2,1)S(1)}, u32[]{:S(2)}, u32[]{:S(2)}) collective-permute-start(bf16[2,512,128]{2,1,0:T(8,128)(2,1)S(1)} %collective-permute-done.13.mid_ref), channel_id=1, source_target_pairs={{0,1},{1,0},{2,3},{3,2},{4,5},{5,4},{6,7},{7,6},{8,9},{9,8},{10,11... | collective-permute-start | bytes 786440 | tf_op jit(solution)/shard_map/ppermute | solution.py:196
  87.6 17.0 %collective-permute-start.11 = (bf16[2,512,128]{2,1,0:T(8,128)(2,1)S(1)}, bf16[2,512,128]{2,1,0:T(8,128)(2,1)S(1)}, u32[]{:S(2)}, u32[]{:S(2)}) collective-permute-start(bf16[2,512,128]{2,1,0:T(8,128)(2,1)S(1)} %collective-permute-done.9.mid_ref), channel_id=1, source_target_pairs={{0,1},{1,0},{2,3},{3,2},{4,5},{5,4},{6,7},{7,6},{8,9},{9,8},{10,11... | collective-permute-start | bytes 786440 | tf_op jit(solution)/shard_map/ppermute | solution.py:196
  91.2 16.5 %collective-permute-start.6 = (bf16[2,512,128]{2,1,0:T(8,128)(2,1)S(1)}, bf16[2,512,128]{2,1,0:T(8,128)(2,1)S(1)}, u32[]{:S(2)}, u32[]{:S(2)}) collective-permute-start(bf16[2,512,128]{2,1,0:T(8,128)(2,1)S(1)} %get-tuple-element.25), channel_id=1, source_target_pairs={{0,1},{1,0},{2,3},{3,2},{4,5},{5,4},{6,7},{7,6},{8,9},{9,8},{10,11... | collective-permute-start | bytes 786440 | tf_op jit(solution)/shard_map/ppermute | solution.py:196
  91.2 16.5 %collective-permute-start.7 = (bf16[2,512,128]{2,1,0:T(8,128)(2,1)S(1)}, bf16[2,512,128]{2,1,0:T(8,128)(2,1)S(1)}, u32[]{:S(2)}, u32[]{:S(2)}) collective-permute-start(bf16[2,512,128]{2,1,0:T(8,128)(2,1)S(1)} %collective-permute-done.5.mid_ref), channel_id=1, source_target_pairs={{0,1},{1,0},{2,3},{3,2},{4,5},{5,4},{6,7},{7,6},{8,9},{9,8},{10,11... | collective-permute-start | bytes 786440 | tf_op jit(solution)/shard_map/ppermute | solution.py:196
  94.8 16.0 %collective-permute-start.2 = (bf16[2,512,128]{2,1,0:T(8,128)(2,1)S(1)}, bf16[2,512,128]{2,1,0:T(8,128)(2,1)S(1)}, u32[]{:S(2)}, u32[]{:S(2)}) collective-permute-start(bf16[2,512,128]{2,1,0:T(8,128)(2,1)S(1)} %get-tuple-element.27), channel_id=1, source_target_pairs={{0,1},{1,0},{2,3},{3,2},{4,5},{5,4},{6,7},{7,6},{8,9},{9,8},{10,11... | collective-permute-start | bytes 786440 | tf_op jit(solution)/shard_map/ppermute | solution.py:196
  94.8 15.9 %collective-permute-start.3 = (bf16[2,512,128]{2,1,0:T(8,128)(2,1)S(1)}, bf16[2,512,128]{2,1,0:T(8,128)(2,1)S(1)}, u32[]{:S(2)}, u32[]{:S(2)}) collective-permute-start(bf16[2,512,128]{2,1,0:T(8,128)(2,1)S(1)} %collective-permute-done.1.mid_ref), channel_id=1, source_target_pairs={{0,1},{1,0},{2,3},{3,2},{4,5},{5,4},{6,7},{7,6},{8,9},{9,8},{10,11... | collective-permute-start | bytes 786440 | tf_op jit(solution)/shard_map/ppermute | solution.py:196
  (3 other events, 49.5 us)

commit v5 on v4

--- a/solution.py
+++ b/solution.py
@@ -173,7 +173,8 @@
     length = queries.shape[0]
     devices = lax.axis_size("seq")
     assert WINDOW == 4 * length and devices % 4 == 0
-    far = [(i, (i + 4) % devices) for i in range(devices)]
+    ring = [(i, (i + 4) % devices) for i in range(devices)]
+    chain = ring[:-4]
     swap = [(i, i + 2 if i % 4 < 2 else i - 2) for i in range(devices)]
     pair = [(i, i ^ 1) for i in range(devices)]
     block = lax.axis_index("seq").astype(jnp.int32)
@@ -198,7 +199,7 @@
     output = None
     for chunk, heads in enumerate(CHUNKS):
         mine = own[chunk]
-        distant = send(mine, far)
+        distant = send(mine, ring if chunk else chain)
         middle = send(jnp.where(upper, distant, mine), swap)
         pair1 = send(jnp.where(odd, distant, mine), pair)
         pair2 = send(middle, pair)

time: 114 us -> 113 us (level)
  the two profiles are of different devices: /device:TPU:0 before, /device:TPU:26 now
where the time goes in v5:
time: 113 us; the launch traced here: 112 us
  waiting for transfers between devices  64.2 us (57%)
  Pallas kernels  26.8 us (24%)
  starting transfers between devices  20.7 us (18%)
    ppermute x32, waiting for transfers between devices, send(): return lax.ppermute(piece, 'seq', pairs)  64.2 us
    pallas_call x8, Pallas kernels, attend(): pl.pallas_call(attend_kernel, out_shape=jax.ShapeDtypeStruct(queries.shap...  24.8 us
    ppermute x32, starting transfers between devices, send(): return lax.ppermute(piece, 'seq', pairs)  20.7 us
  transfers between devices with their start and end apart: 32, of which 14 were waited for; matrix products, arithmetic and copies ran while one was open for 0% of the time, Pallas kernels for 20%

profile of v5, /device:TPU:26, one launch (start us, length us, event | category | flops | bytes accessed | tf_op | source)
XLA Modules:
  0.0 112.1 jit_solution(7588920892953777104)
XLA Ops:
  2.7 2.5 %collective-permute-start.24 = (bf16[2,512,128]{2,1,0:T(8,128)(2,1)S(1)}, bf16[2,512,128]{2,1,0:T(8,128)(2,1)S(1)}, u32[]{:S(2)}, u32[]{:S(2)}) collective-permute-start(bf16[2,512,128]{2,1,0:T(8,128)(2,1)S(1)} %shard_map.43.own_ref), channel_id=1, source_target_pairs={{0,4},{1,5},{2,6},{3,7},{4,8},{5,9},{6,10},{7,11},{8,12},{9,13},{1... | collective-permute-start | bytes 786440 | tf_op jit(solution)/shard_map/ppermute | solution.py:197
  5.3 1.6 %collective-permute-start.20 = (bf16[2,512,128]{2,1,0:T(8,128)(2,1)S(1)}, bf16[2,512,128]{2,1,0:T(8,128)(2,1)S(1)}, u32[]{:S(2)}, u32[]{:S(2)}) collective-permute-start(bf16[2,512,128]{2,1,0:T(8,128)(2,1)S(1)} %shard_map.42.own_ref), channel_id=1, source_target_pairs={{0,4},{1,5},{2,6},{3,7},{4,8},{5,9},{6,10},{7,11},{8,12},{9,13},{1... | collective-permute-start | bytes 786440 | tf_op jit(solution)/shard_map/ppermute | solution.py:197
  7.0 1.6 %collective-permute-start.16 = (bf16[2,512,128]{2,1,0:T(8,128)(2,1)S(1)}, bf16[2,512,128]{2,1,0:T(8,128)(2,1)S(1)}, u32[]{:S(2)}, u32[]{:S(2)}) collective-permute-start(bf16[2,512,128]{2,1,0:T(8,128)(2,1)S(1)} %shard_map.41.own_ref), channel_id=1, source_target_pairs={{0,4},{1,5},{2,6},{3,7},{4,8},{5,9},{6,10},{7,11},{8,12},{9,13},{1... | collective-permute-start | bytes 786440 | tf_op jit(solution)/shard_map/ppermute | solution.py:197
  9.2 3.1 %collective-permute-done.28.far_ref = bf16[2,512,128]{2,1,0:T(8,128)(2,1)S(1)} collective-permute-done((bf16[2,512,128]{2,1,0:T(8,128)(2,1)S(1)}, bf16[2,512,128]{2,1,0:T(8,128)(2,1)S(1)}, u32[]{:S(2)}, u32[]{:S(2)}) %collective-permute-start.28) | collective-permute-done | bytes 262176 | tf_op jit(solution)/shard_map/ppermute | solution.py:197
  12.4 5.6 %collective-permute-done.24.far_ref = bf16[2,512,128]{2,1,0:T(8,128)(2,1)S(1)} collective-permute-done((bf16[2,512,128]{2,1,0:T(8,128)(2,1)S(1)}, bf16[2,512,128]{2,1,0:T(8,128)(2,1)S(1)}, u32[]{:S(2)}, u32[]{:S(2)}) %collective-permute-start.24) | collective-permute-done | bytes 262176 | tf_op jit(solution)/shard_map/ppermute | solution.py:197
  18.0 5.6 %collective-permute-done.20.far_ref = bf16[2,512,128]{2,1,0:T(8,128)(2,1)S(1)} collective-permute-done((bf16[2,512,128]{2,1,0:T(8,128)(2,1)S(1)}, bf16[2,512,128]{2,1,0:T(8,128)(2,1)S(1)}, u32[]{:S(2)}, u32[]{:S(2)}) %collective-permute-start.20) | collective-permute-done | bytes 262176 | tf_op jit(solution)/shard_map/ppermute | solution.py:197
  23.6 5.6 %collective-permute-done.16.far_ref = bf16[2,512,128]{2,1,0:T(8,128)(2,1)S(1)} collective-permute-done((bf16[2,512,128]{2,1,0:T(8,128)(2,1)S(1)}, bf16[2,512,128]{2,1,0:T(8,128)(2,1)S(1)}, u32[]{:S(2)}, u32[]{:S(2)}) %collective-permute-start.16) | collective-permute-done | bytes 262176 | tf_op jit(solution)/shard_map/ppermute | solution.py:197
  29.2 1.5 %collective-permute-start.29 = (bf16[2,512,128]{2,1,0:T(8,128)(2,1)S(1)}, bf16[2,512,128]{2,1,0:T(8,128)(2,1)S(1)}, u32[]{:S(2)}, u32[]{:S(2)}) collective-permute-start(bf16[2,512,128]{2,1,0:T(8,128)(2,1)S(1)} %get-tuple-element.14), channel_id=1, source_target_pairs={{0,2},{1,3},{2,0},{3,1},{4,6},{5,7},{6,4},{7,5},{8,10},{9,11},{10,... | collective-permute-start | bytes 786440 | tf_op jit(solution)/shard_map/ppermute | solution.py:197
  30.7 4.1 %collective-permute-done.12.far_ref = bf16[2,512,128]{2,1,0:T(8,128)(2,1)S(1)} collective-permute-done((bf16[2,512,128]{2,1,0:T(8,128)(2,1)S(1)}, bf16[2,512,128]{2,1,0:T(8,128)(2,1)S(1)}, u32[]{:S(2)}, u32[]{:S(2)}) %collective-permute-start.12) | collective-permute-done | bytes 262176 | tf_op jit(solution)/shard_map/ppermute | solution.py:197
  34.8 5.6 %collective-permute-done.8.far_ref = bf16[2,512,128]{2,1,0:T(8,128)(2,1)S(1)} collective-permute-done((bf16[2,512,128]{2,1,0:T(8,128)(2,1)S(1)}, bf16[2,512,128]{2,1,0:T(8,128)(2,1)S(1)}, u32[]{:S(2)}, u32[]{:S(2)}) %collective-permute-start.8) | collective-permute-done | bytes 262176 | tf_op jit(solution)/shard_map/ppermute | solution.py:197
  40.4 1.5 %collective-permute-start.25 = (bf16[2,512,128]{2,1,0:T(8,128)(2,1)S(1)}, bf16[2,512,128]{2,1,0:T(8,128)(2,1)S(1)}, u32[]{:S(2)}, u32[]{:S(2)}) collective-permute-start(bf16[2,512,128]{2,1,0:T(8,128)(2,1)S(1)} %get-tuple-element.16), channel_id=1, source_target_pairs={{0,2},{1,3},{2,0},{3,1},{4,6},{5,7},{6,4},{7,5},{8,10},{9,11},{10,... | collective-permute-start | bytes 786440 | tf_op jit(solution)/shard_map/ppermute | solution.py:197
  41.9 4.1 %collective-permute-done.4.far_ref = bf16[2,512,128]{2,1,0:T(8,128)(2,1)S(1)} collective-permute-done((bf16[2,512,128]{2,1,0:T(8,128)(2,1)S(1)}, bf16[2,512,128]{2,1,0:T(8,128)(2,1)S(1)}, u32[]{:S(2)}, u32[]{:S(2)}) %collective-permute-start.4) | collective-permute-done | bytes 262176 | tf_op jit(solution)/shard_map/ppermute | solution.py:197
  46.1 4.4 %collective-permute-done.far_ref = bf16[2,512,128]{2,1,0:T(8,128)(2,1)S(1)} collective-permute-done((bf16[2,512,128]{2,1,0:T(8,128)(2,1)S(1)}, bf16[2,512,128]{2,1,0:T(8,128)(2,1)S(1)}, u32[]{:S(2)}, u32[]{:S(2)}) %collective-permute-start) | collective-permute-done | bytes 262176 | tf_op jit(solution)/shard_map/ppermute | solution.py:197
  50.5 1.5 %collective-permute-start.21 = (bf16[2,512,128]{2,1,0:T(8,128)(2,1)S(1)}, bf16[2,512,128]{2,1,0:T(8,128)(2,1)S(1)}, u32[]{:S(2)}, u32[]{:S(2)}) collective-permute-start(bf16[2,512,128]{2,1,0:T(8,128)(2,1)S(1)} %get-tuple-element.18), channel_id=1, source_target_pairs={{0,2},{1,3},{2,0},{3,1},{4,6},{5,7},{6,4},{7,5},{8,10},{9,11},{10,... | collective-permute-start | bytes 786440 | tf_op jit(solution)/shard_map/ppermute | solution.py:197
  52.9 1.5 %collective-permute-start.13 = (bf16[2,512,128]{2,1,0:T(8,128)(2,1)S(1)}, bf16[2,512,128]{2,1,0:T(8,128)(2,1)S(1)}, u32[]{:S(2)}, u32[]{:S(2)}) collective-permute-start(bf16[2,512,128]{2,1,0:T(8,128)(2,1)S(1)} %get-tuple-element.22), channel_id=1, source_target_pairs={{0,2},{1,3},{2,0},{3,1},{4,6},{5,7},{6,4},{7,5},{8,10},{9,11},{10,... | collective-permute-start | bytes 786440 | tf_op jit(solution)/shard_map/ppermute | solution.py:197
  54.4 5.2 %collective-permute-done.21.mid_ref = bf16[2,512,128]{2,1,0:T(8,128)(2,1)S(1)} collective-permute-done((bf16[2,512,128]{2,1,0:T(8,128)(2,1)S(1)}, bf16[2,512,128]{2,1,0:T(8,128)(2,1)S(1)}, u32[]{:S(2)}, u32[]{:S(2)}) %collective-permute-start.21) | collective-permute-done | bytes 262176 | tf_op jit(solution)/shard_map/ppermute | solution.py:197
  59.7 1.5 %collective-permute-start.9 = (bf16[2,512,128]{2,1,0:T(8,128)(2,1)S(1)}, bf16[2,512,128]{2,1,0:T(8,128)(2,1)S(1)}, u32[]{:S(2)}, u32[]{:S(2)}) collective-permute-start(bf16[2,512,128]{2,1,0:T(8,128)(2,1)S(1)} %get-tuple-element.24), channel_id=1, source_target_pairs={{0,2},{1,3},{2,0},{3,1},{4,6},{5,7},{6,4},{7,5},{8,10},{9,11},{10,... | collective-permute-start | bytes 786440 | tf_op jit(solution)/shard_map/ppermute | solution.py:197
  61.2 4.1 %collective-permute-done.17.mid_ref = bf16[2,512,128]{2,1,0:T(8,128)(2,1)S(1)} collective-permute-done((bf16[2,512,128]{2,1,0:T(8,128)(2,1)S(1)}, bf16[2,512,128]{2,1,0:T(8,128)(2,1)S(1)}, u32[]{:S(2)}, u32[]{:S(2)}) %collective-permute-start.17) | collective-permute-done | bytes 262176 | tf_op jit(solution)/shard_map/ppermute | solution.py:197
  65.4 1.6 %collective-permute-start.5 = (bf16[2,512,128]{2,1,0:T(8,128)(2,1)S(1)}, bf16[2,512,128]{2,1,0:T(8,128)(2,1)S(1)}, u32[]{:S(2)}, u32[]{:S(2)}) collective-permute-start(bf16[2,512,128]{2,1,0:T(8,128)(2,1)S(1)} %get-tuple-element.26), channel_id=1, source_target_pairs={{0,2},{1,3},{2,0},{3,1},{4,6},{5,7},{6,4},{7,5},{8,10},{9,11},{10,... | collective-permute-start | bytes 786440 | tf_op jit(solution)/shard_map/ppermute | solution.py:197
  66.9 4.0 %collective-permute-done.13.mid_ref = bf16[2,512,128]{2,1,0:T(8,128)(2,1)S(1)} collective-permute-done((bf16[2,512,128]{2,1,0:T(8,128)(2,1)S(1)}, bf16[2,512,128]{2,1,0:T(8,128)(2,1)S(1)}, u32[]{:S(2)}, u32[]{:S(2)}) %collective-permute-start.13) | collective-permute-done | bytes 262176 | tf_op jit(solution)/shard_map/ppermute | solution.py:197
  70.9 1.5 %collective-permute-start.1 = (bf16[2,512,128]{2,1,0:T(8,128)(2,1)S(1)}, bf16[2,512,128]{2,1,0:T(8,128)(2,1)S(1)}, u32[]{:S(2)}, u32[]{:S(2)}) collective-permute-start(bf16[2,512,128]{2,1,0:T(8,128)(2,1)S(1)} %get-tuple-element.28), channel_id=1, source_target_pairs={{0,2},{1,3},{2,0},{3,1},{4,6},{5,7},{6,4},{7,5},{8,10},{9,11},{10,... | collective-permute-start | bytes 786440 | tf_op jit(solution)/shard_map/ppermute | solution.py:197
  72.4 4.1 %collective-permute-done.9.mid_ref = bf16[2,512,128]{2,1,0:T(8,128)(2,1)S(1)} collective-permute-done((bf16[2,512,128]{2,1,0:T(8,128)(2,1)S(1)}, bf16[2,512,128]{2,1,0:T(8,128)(2,1)S(1)}, u32[]{:S(2)}, u32[]{:S(2)}) %collective-permute-start.9) | collective-permute-done | bytes 262176 | tf_op jit(solution)/shard_map/ppermute | solution.py:197
  77.0 5.1 %collective-permute-done.5.mid_ref = bf16[2,512,128]{2,1,0:T(8,128)(2,1)S(1)} collective-permute-done((bf16[2,512,128]{2,1,0:T(8,128)(2,1)S(1)}, bf16[2,512,128]{2,1,0:T(8,128)(2,1)S(1)}, u32[]{:S(2)}, u32[]{:S(2)}) %collective-permute-start.5) | collective-permute-done | bytes 262176 | tf_op jit(solution)/shard_map/ppermute | solution.py:197
  82.2 3.6 %collective-permute-done.1.mid_ref = bf16[2,512,128]{2,1,0:T(8,128)(2,1)S(1)} collective-permute-done((bf16[2,512,128]{2,1,0:T(8,128)(2,1)S(1)}, bf16[2,512,128]{2,1,0:T(8,128)(2,1)S(1)}, u32[]{:S(2)}, u32[]{:S(2)}) %collective-permute-start.1) | collective-permute-done | bytes 262176 | tf_op jit(solution)/shard_map/ppermute | solution.py:197
  86.3 3.1 %shard_map.45.rest_0_ = bf16[256,4096]{1,0:T(8,128)(2,1)} custom-call(bf16[256,4096]{1,0:T(8,128)(2,1)S(1)} %copy-done, bf16[2,512,128]{2,1,0:T(8,128)(2,1)S(1)} %shard_map.44.own_ref, bf16[2,512,128]{2,1,0:T(8,128)(2,1)S(1)} %collective-permute-done.28.far_ref, bf16[2,512,128]{2,1,0:T(8,128)(2,1)S(1)} %collective-permute-done.29.mid_ref, ...), custom_call_target="tpu_custom_call" | custom-call | flops 671088640 | bytes 1835008 | tf_op jit(solution)/shard_map/pallas_call | solution.py:152
  89.9 3.1 %shard_map.46.rest_0_ = bf16[256,4096]{1,0:T(8,128)(2,1)} custom-call(bf16[256,4096]{1,0:T(8,128)(2,1)S(1)} %copy-done, bf16[2,512,128]{2,1,0:T(8,128)(2,1)S(1)} %shard_map.43.own_ref, bf16[2,512,128]{2,1,0:T(8,128)(2,1)S(1)} %collective-permute-done.24.far_ref, ...), custom_call_target="tpu_custom_call", output_to_operand_aliasing={{}: (6, {})} | custom-call | flops 671088640 | bytes 1835008 | tf_op jit(solution)/shard_map/pallas_call | solution.py:152
  93.5 3.1 %shard_map.47.rest_0_ = bf16[256,4096]{1,0:T(8,128)(2,1)} custom-call(bf16[256,4096]{1,0:T(8,128)(2,1)S(1)} %copy-done, bf16[2,512,128]{2,1,0:T(8,128)(2,1)S(1)} %shard_map.42.own_ref, bf16[2,512,128]{2,1,0:T(8,128)(2,1)S(1)} %collective-permute-done.20.far_ref, ...), custom_call_target="tpu_custom_call", output_to_operand_aliasing={{}: (6, {})} | custom-call | flops 671088640 | bytes 1835008 | tf_op jit(solution)/shard_map/pallas_call | solution.py:152
  96.6 3.1 %shard_map.48.rest_0_ = bf16[256,4096]{1,0:T(8,128)(2,1)} custom-call(bf16[256,4096]{1,0:T(8,128)(2,1)S(1)} %copy-done, bf16[2,512,128]{2,1,0:T(8,128)(2,1)S(1)} %shard_map.41.own_ref, bf16[2,512,128]{2,1,0:T(8,128)(2,1)S(1)} %collective-permute-done.16.far_ref, ...), custom_call_target="tpu_custom_call", output_to_operand_aliasing={{}: (6, {})} | custom-call | flops 671088640 | bytes 1835008 | tf_op jit(solution)/shard_map/pallas_call | solution.py:152
  99.7 3.1 %shard_map.49.rest_0_ = bf16[256,4096]{1,0:T(8,128)(2,1)} custom-call(bf16[256,4096]{1,0:T(8,128)(2,1)S(1)} %copy-done, bf16[2,512,128]{2,1,0:T(8,128)(2,1)S(1)} %shard_map.40.own_ref, bf16[2,512,128]{2,1,0:T(8,128)(2,1)S(1)} %collective-permute-done.12.far_ref, ...), custom_call_target="tpu_custom_call", output_to_operand_aliasing={{}: (6, {})} | custom-call | flops 671088640 | bytes 1835008 | tf_op jit(solution)/shard_map/pallas_call | solution.py:152
  102.8 3.1 %shard_map.50.rest_0_ = bf16[256,4096]{1,0:T(8,128)(2,1)} custom-call(bf16[256,4096]{1,0:T(8,128)(2,1)S(1)} %copy-done, bf16[2,512,128]{2,1,0:T(8,128)(2,1)S(1)} %shard_map.39.own_ref, bf16[2,512,128]{2,1,0:T(8,128)(2,1)S(1)} %collective-permute-done.8.far_ref, ...), custom_call_target="tpu_custom_call", output_to_operand_aliasing={{}: (6, {})} | custom-call | flops 671088640 | bytes 1835008 | tf_op jit(solution)/shard_map/pallas_call | solution.py:152
  105.9 3.1 %shard_map.51.rest_0_ = bf16[256,4096]{1,0:T(8,128)(2,1)} custom-call(bf16[256,4096]{1,0:T(8,128)(2,1)S(1)} %copy-done, bf16[2,512,128]{2,1,0:T(8,128)(2,1)S(1)} %shard_map.38.own_ref, bf16[2,512,128]{2,1,0:T(8,128)(2,1)S(1)} %collective-permute-done.4.far_ref, ...), custom_call_target="tpu_custom_call", output_to_operand_aliasing={{}: (6, {})} | custom-call | flops 671088640 | bytes 1835008 | tf_op jit(solution)/shard_map/pallas_call | solution.py:152
  109.0 3.1 %shard_map.52 = bf16[256,4096]{1,0:T(8,128)(2,1)} custom-call(bf16[256,4096]{1,0:T(8,128)(2,1)S(1)} %copy-done, bf16[2,512,128]{2,1,0:T(8,128)(2,1)S(1)} %shard_map.37.own_ref, bf16[2,512,128]{2,1,0:T(8,128)(2,1)S(1)} %collective-permute-done.far_ref, bf16[2,512,128]{2,1,0:T(8,128)(2,1)S(1)} %collective-permute-done.1.mid_ref, ...), custom_call_target="tpu_custom_call", output_to_operand_aliasing={{}: (6, {})} | custom-call | flops 671088640 | bytes 1835008 | tf_op jit(solution)/shard_map/pallas_call | solution.py:152
  (62 shorter events, 6.6 us)
Async XLA Ops:
  1.2 11.1 %collective-permute-start.28 = (bf16[2,512,128]{2,1,0:T(8,128)(2,1)S(1)}, bf16[2,512,128]{2,1,0:T(8,128)(2,1)S(1)}, u32[]{:S(2)}, u32[]{:S(2)}) collective-permute-start(bf16[2,512,128]{2,1,0:T(8,128)(2,1)S(1)} %shard_map.44.own_ref), channel_id=1, source_target_pairs={{0,4},{1,5},{2,6},{3,7},{4,8},{5,9},{6,10},{7,11},{8,12},{9,13},{1... | collective-permute-start | bytes 786440 | tf_op jit(solution)/shard_map/ppermute | solution.py:197
  2.7 15.2 %collective-permute-start.24 = (bf16[2,512,128]{2,1,0:T(8,128)(2,1)S(1)}, bf16[2,512,128]{2,1,0:T(8,128)(2,1)S(1)}, u32[]{:S(2)}, u32[]{:S(2)}) collective-permute-start(bf16[2,512,128]{2,1,0:T(8,128)(2,1)S(1)} %shard_map.43.own_ref), channel_id=1, source_target_pairs={{0,4},{1,5},{2,6},{3,7},{4,8},{5,9},{6,10},{7,11},{8,12},{9,13},{1... | collective-permute-start | bytes 786440 | tf_op jit(solution)/shard_map/ppermute | solution.py:197
  5.3 18.3 %collective-permute-start.20 = (bf16[2,512,128]{2,1,0:T(8,128)(2,1)S(1)}, bf16[2,512,128]{2,1,0:T(8,128)(2,1)S(1)}, u32[]{:S(2)}, u32[]{:S(2)}) collective-permute-start(bf16[2,512,128]{2,1,0:T(8,128)(2,1)S(1)} %shard_map.42.own_ref), channel_id=1, source_target_pairs={{0,4},{1,5},{2,6},{3,7},{4,8},{5,9},{6,10},{7,11},{8,12},{9,13},{1... | collective-permute-start | bytes 786440 | tf_op jit(solution)/shard_map/ppermute | solution.py:197
  7.0 22.1 %collective-permute-start.16 = (bf16[2,512,128]{2,1,0:T(8,128)(2,1)S(1)}, bf16[2,512,128]{2,1,0:T(8,128)(2,1)S(1)}, u32[]{:S(2)}, u32[]{:S(2)}) collective-permute-start(bf16[2,512,128]{2,1,0:T(8,128)(2,1)S(1)} %shard_map.41.own_ref), channel_id=1, source_target_pairs={{0,4},{1,5},{2,6},{3,7},{4,8},{5,9},{6,10},{7,11},{8,12},{9,13},{1... | collective-permute-start | bytes 786440 | tf_op jit(solution)/shard_map/ppermute | solution.py:197
  8.8 26.0 %collective-permute-start.12 = (bf16[2,512,128]{2,1,0:T(8,128)(2,1)S(1)}, bf16[2,512,128]{2,1,0:T(8,128)(2,1)S(1)}, u32[]{:S(2)}, u32[]{:S(2)}) collective-permute-start(bf16[2,512,128]{2,1,0:T(8,128)(2,1)S(1)} %shard_map.40.own_ref), channel_id=1, source_target_pairs={{0,4},{1,5},{2,6},{3,7},{4,8},{5,9},{6,10},{7,11},{8,12},{9,13},{1... | collective-permute-start | bytes 786440 | tf_op jit(solution)/shard_map/ppermute | solution.py:197
  12.3 28.1 %collective-permute-start.8 = (bf16[2,512,128]{2,1,0:T(8,128)(2,1)S(1)}, bf16[2,512,128]{2,1,0:T(8,128)(2,1)S(1)}, u32[]{:S(2)}, u32[]{:S(2)}) collective-permute-start(bf16[2,512,128]{2,1,0:T(8,128)(2,1)S(1)} %shard_map.39.own_ref), channel_id=1, source_target_pairs={{0,4},{1,5},{2,6},{3,7},{4,8},{5,9},{6,10},{7,11},{8,12},{9,13},{1... | collective-permute-start | bytes 786440 | tf_op jit(solution)/shard_map/ppermute | solution.py:197
  17.9 28.1 %collective-permute-start.4 = (bf16[2,512,128]{2,1,0:T(8,128)(2,1)S(1)}, bf16[2,512,128]{2,1,0:T(8,128)(2,1)S(1)}, u32[]{:S(2)}, u32[]{:S(2)}) collective-permute-start(bf16[2,512,128]{2,1,0:T(8,128)(2,1)S(1)} %shard_map.38.own_ref), channel_id=1, source_target_pairs={{0,4},{1,5},{2,6},{3,7},{4,8},{5,9},{6,10},{7,11},{8,12},{9,13},{1... | collective-permute-start | bytes 786440 | tf_op jit(solution)/shard_map/ppermute | solution.py:197
  23.5 27.0 %collective-permute-start = (bf16[2,512,128]{2,1,0:T(8,128)(2,1)S(1)}, bf16[2,512,128]{2,1,0:T(8,128)(2,1)S(1)}, u32[]{:S(2)}, u32[]{:S(2)}) collective-permute-start(bf16[2,512,128]{2,1,0:T(8,128)(2,1)S(1)} %shard_map.37.own_ref), channel_id=1, source_target_pairs={{0,4},{1,5},{2,6},{3,7},{4,8},{5,9},{6,10},{7,11},{8,12},{9,13},{1... | collective-permute-start | bytes 786440 | tf_op jit(solution)/shard_map/ppermute | solution.py:197
  29.2 22.9 %collective-permute-start.29 = (bf16[2,512,128]{2,1,0:T(8,128)(2,1)S(1)}, bf16[2,512,128]{2,1,0:T(8,128)(2,1)S(1)}, u32[]{:S(2)}, u32[]{:S(2)}) collective-permute-start(bf16[2,512,128]{2,1,0:T(8,128)(2,1)S(1)} %get-tuple-element.14), channel_id=1, source_target_pairs={{0,2},{1,3},{2,0},{3,1},{4,6},{5,7},{6,4},{7,5},{8,10},{9,11},{10,... | collective-permute-start | bytes 786440 | tf_op jit(solution)/shard_map/ppermute | solution.py:197
  34.8 17.3 %collective-permute-start.30 = (bf16[2,512,128]{2,1,0:T(8,128)(2,1)S(1)}, bf16[2,512,128]{2,1,0:T(8,128)(2,1)S(1)}, u32[]{:S(2)}, u32[]{:S(2)}) collective-permute-start(bf16[2,512,128]{2,1,0:T(8,128)(2,1)S(1)} %get-tuple-element.13), channel_id=1, source_target_pairs={{0,1},{1,0},{2,3},{3,2},{4,5},{5,4},{6,7},{7,6},{8,9},{9,8},{10,11... | collective-permute-start | bytes 786440 | tf_op jit(solution)/shard_map/ppermute | solution.py:197
  40.4 12.3 %collective-permute-start.25 = (bf16[2,512,128]{2,1,0:T(8,128)(2,1)S(1)}, bf16[2,512,128]{2,1,0:T(8,128)(2,1)S(1)}, u32[]{:S(2)}, u32[]{:S(2)}) collective-permute-start(bf16[2,512,128]{2,1,0:T(8,128)(2,1)S(1)} %get-tuple-element.16), channel_id=1, source_target_pairs={{0,2},{1,3},{2,0},{3,1},{4,6},{5,7},{6,4},{7,5},{8,10},{9,11},{10,... | collective-permute-start | bytes 786440 | tf_op jit(solution)/shard_map/ppermute | solution.py:197
  46.0 6.9 %collective-permute-start.26 = (bf16[2,512,128]{2,1,0:T(8,128)(2,1)S(1)}, bf16[2,512,128]{2,1,0:T(8,128)(2,1)S(1)}, u32[]{:S(2)}, u32[]{:S(2)}) collective-permute-start(bf16[2,512,128]{2,1,0:T(8,128)(2,1)S(1)} %get-tuple-element.15), channel_id=1, source_target_pairs={{0,1},{1,0},{2,3},{3,2},{4,5},{5,4},{6,7},{7,6},{8,9},{9,8},{10,11... | collective-permute-start | bytes 786440 | tf_op jit(solution)/shard_map/ppermute | solution.py:197
  50.5 9.2 %collective-permute-start.21 = (bf16[2,512,128]{2,1,0:T(8,128)(2,1)S(1)}, bf16[2,512,128]{2,1,0:T(8,128)(2,1)S(1)}, u32[]{:S(2)}, u32[]{:S(2)}) collective-permute-start(bf16[2,512,128]{2,1,0:T(8,128)(2,1)S(1)} %get-tuple-element.18), channel_id=1, source_target_pairs={{0,2},{1,3},{2,0},{3,1},{4,6},{5,7},{6,4},{7,5},{8,10},{9,11},{10,... | collective-permute-start | bytes 786440 | tf_op jit(solution)/shard_map/ppermute | solution.py:197
  52.0 7.7 %collective-permute-start.22 = (bf16[2,512,128]{2,1,0:T(8,128)(2,1)S(1)}, bf16[2,512,128]{2,1,0:T(8,128)(2,1)S(1)}, u32[]{:S(2)}, u32[]{:S(2)}) collective-permute-start(bf16[2,512,128]{2,1,0:T(8,128)(2,1)S(1)} %get-tuple-element.17), channel_id=1, source_target_pairs={{0,1},{1,0},{2,3},{3,2},{4,5},{5,4},{6,7},{7,6},{8,9},{9,8},{10,11... | collective-permute-start | bytes 786440 | tf_op jit(solution)/shard_map/ppermute | solution.py:197
  52.0 13.3 %collective-permute-start.17 = (bf16[2,512,128]{2,1,0:T(8,128)(2,1)S(1)}, bf16[2,512,128]{2,1,0:T(8,128)(2,1)S(1)}, u32[]{:S(2)}, u32[]{:S(2)}) collective-permute-start(bf16[2,512,128]{2,1,0:T(8,128)(2,1)S(1)} %get-tuple-element.20), channel_id=1, source_target_pairs={{0,2},{1,3},{2,0},{3,1},{4,6},{5,7},{6,4},{7,5},{8,10},{9,11},{10,... | collective-permute-start | bytes 786440 | tf_op jit(solution)/shard_map/ppermute | solution.py:197
  52.7 12.7 %collective-permute-start.18 = (bf16[2,512,128]{2,1,0:T(8,128)(2,1)S(1)}, bf16[2,512,128]{2,1,0:T(8,128)(2,1)S(1)}, u32[]{:S(2)}, u32[]{:S(2)}) collective-permute-start(bf16[2,512,128]{2,1,0:T(8,128)(2,1)S(1)} %get-tuple-element.19), channel_id=1, source_target_pairs={{0,1},{1,0},{2,3},{3,2},{4,5},{5,4},{6,7},{7,6},{8,9},{9,8},{10,11... | collective-permute-start | bytes 786440 | tf_op jit(solution)/shard_map/ppermute | solution.py:197
  52.9 18.0 %collective-permute-start.13 = (bf16[2,512,128]{2,1,0:T(8,128)(2,1)S(1)}, bf16[2,512,128]{2,1,0:T(8,128)(2,1)S(1)}, u32[]{:S(2)}, u32[]{:S(2)}) collective-permute-start(bf16[2,512,128]{2,1,0:T(8,128)(2,1)S(1)} %get-tuple-element.22), channel_id=1, source_target_pairs={{0,2},{1,3},{2,0},{3,1},{4,6},{5,7},{6,4},{7,5},{8,10},{9,11},{10,... | collective-permute-start | bytes 786440 | tf_op jit(solution)/shard_map/ppermute | solution.py:197
  59.7 12.8 %collective-permute-start.14 = (bf16[2,512,128]{2,1,0:T(8,128)(2,1)S(1)}, bf16[2,512,128]{2,1,0:T(8,128)(2,1)S(1)}, u32[]{:S(2)}, u32[]{:S(2)}) collective-permute-start(bf16[2,512,128]{2,1,0:T(8,128)(2,1)S(1)} %get-tuple-element.21), channel_id=1, source_target_pairs={{0,1},{1,0},{2,3},{3,2},{4,5},{5,4},{6,7},{7,6},{8,9},{9,8},{10,11... | collective-permute-start | bytes 786440 | tf_op jit(solution)/shard_map/ppermute | solution.py:197
  59.7 16.8 %collective-permute-start.9 = (bf16[2,512,128]{2,1,0:T(8,128)(2,1)S(1)}, bf16[2,512,128]{2,1,0:T(8,128)(2,1)S(1)}, u32[]{:S(2)}, u32[]{:S(2)}) collective-permute-start(bf16[2,512,128]{2,1,0:T(8,128)(2,1)S(1)} %get-tuple-element.24), channel_id=1, source_target_pairs={{0,2},{1,3},{2,0},{3,1},{4,6},{5,7},{6,4},{7,5},{8,10},{9,11},{10,... | collective-permute-start | bytes 786440 | tf_op jit(solution)/shard_map/ppermute | solution.py:197
  65.3 11.2 %collective-permute-start.10 = (bf16[2,512,128]{2,1,0:T(8,128)(2,1)S(1)}, bf16[2,512,128]{2,1,0:T(8,128)(2,1)S(1)}, u32[]{:S(2)}, u32[]{:S(2)}) collective-permute-start(bf16[2,512,128]{2,1,0:T(8,128)(2,1)S(1)} %get-tuple-element.23), channel_id=1, source_target_pairs={{0,1},{1,0},{2,3},{3,2},{4,5},{5,4},{6,7},{7,6},{8,9},{9,8},{10,11... | collective-permute-start | bytes 786440 | tf_op jit(solution)/shard_map/ppermute | solution.py:197
  65.4 16.8 %collective-permute-start.5 = (bf16[2,512,128]{2,1,0:T(8,128)(2,1)S(1)}, bf16[2,512,128]{2,1,0:T(8,128)(2,1)S(1)}, u32[]{:S(2)}, u32[]{:S(2)}) collective-permute-start(bf16[2,512,128]{2,1,0:T(8,128)(2,1)S(1)} %get-tuple-element.26), channel_id=1, source_target_pairs={{0,2},{1,3},{2,0},{3,1},{4,6},{5,7},{6,4},{7,5},{8,10},{9,11},{10,... | collective-permute-start | bytes 786440 | tf_op jit(solution)/shard_map/ppermute | solution.py:197
  70.9 14.9 %collective-permute-start.1 = (bf16[2,512,128]{2,1,0:T(8,128)(2,1)S(1)}, bf16[2,512,128]{2,1,0:T(8,128)(2,1)S(1)}, u32[]{:S(2)}, u32[]{:S(2)}) collective-permute-start(bf16[2,512,128]{2,1,0:T(8,128)(2,1)S(1)} %get-tuple-element.28), channel_id=1, source_target_pairs={{0,2},{1,3},{2,0},{3,1},{4,6},{5,7},{6,4},{7,5},{8,10},{9,11},{10,... | collective-permute-start | bytes 786440 | tf_op jit(solution)/shard_map/ppermute | solution.py:197
  72.4 13.3 %collective-permute-start.31 = (bf16[2,512,128]{2,1,0:T(8,128)(2,1)S(1)}, bf16[2,512,128]{2,1,0:T(8,128)(2,1)S(1)}, u32[]{:S(2)}, u32[]{:S(2)}) collective-permute-start(bf16[2,512,128]{2,1,0:T(8,128)(2,1)S(1)} %collective-permute-done.29.mid_ref), channel_id=1, source_target_pairs={{0,1},{1,0},{2,3},{3,2},{4,5},{5,4},{6,7},{7,6},{8,9},{9,8},{10,11... | collective-permute-start | bytes 786440 | tf_op jit(solution)/shard_map/ppermute | solution.py:197
  76.5 12.9 %collective-permute-start.27 = (bf16[2,512,128]{2,1,0:T(8,128)(2,1)S(1)}, bf16[2,512,128]{2,1,0:T(8,128)(2,1)S(1)}, u32[]{:S(2)}, u32[]{:S(2)}) collective-permute-start(bf16[2,512,128]{2,1,0:T(8,128)(2,1)S(1)} %collective-permute-done.25.mid_ref), channel_id=1, source_target_pairs={{0,1},{1,0},{2,3},{3,2},{4,5},{5,4},{6,7},{7,6},{8,9},{9,8},{10,11... | collective-permute-start | bytes 786440 | tf_op jit(solution)/shard_map/ppermute | solution.py:197
  76.5 12.9 %collective-permute-start.23 = (bf16[2,512,128]{2,1,0:T(8,128)(2,1)S(1)}, bf16[2,512,128]{2,1,0:T(8,128)(2,1)S(1)}, u32[]{:S(2)}, u32[]{:S(2)}) collective-permute-start(bf16[2,512,128]{2,1,0:T(8,128)(2,1)S(1)} %collective-permute-done.21.mid_ref), channel_id=1, source_target_pairs={{0,1},{1,0},{2,3},{3,2},{4,5},{5,4},{6,7},{7,6},{8,9},{9,8},{10,11... | collective-permute-start | bytes 786440 | tf_op jit(solution)/shard_map/ppermute | solution.py:197
  82.1 10.9 %collective-permute-start.19 = (bf16[2,512,128]{2,1,0:T(8,128)(2,1)S(1)}, bf16[2,512,128]{2,1,0:T(8,128)(2,1)S(1)}, u32[]{:S(2)}, u32[]{:S(2)}) collective-permute-start(bf16[2,512,128]{2,1,0:T(8,128)(2,1)S(1)} %collective-permute-done.17.mid_ref), channel_id=1, source_target_pairs={{0,1},{1,0},{2,3},{3,2},{4,5},{5,4},{6,7},{7,6},{8,9},{9,8},{10,11... | collective-permute-start | bytes 786440 | tf_op jit(solution)/shard_map/ppermute | solution.py:197
  85.8 7.3 %collective-permute-start.15 = (bf16[2,512,128]{2,1,0:T(8,128)(2,1)S(1)}, bf16[2,512,128]{2,1,0:T(8,128)(2,1)S(1)}, u32[]{:S(2)}, u32[]{:S(2)}) collective-permute-start(bf16[2,512,128]{2,1,0:T(8,128)(2,1)S(1)} %collective-permute-done.13.mid_ref), channel_id=1, source_target_pairs={{0,1},{1,0},{2,3},{3,2},{4,5},{5,4},{6,7},{7,6},{8,9},{9,8},{10,11... | collective-permute-start | bytes 786440 | tf_op jit(solution)/shard_map/ppermute | solution.py:197
  85.8 17.0 %collective-permute-start.11 = (bf16[2,512,128]{2,1,0:T(8,128)(2,1)S(1)}, bf16[2,512,128]{2,1,0:T(8,128)(2,1)S(1)}, u32[]{:S(2)}, u32[]{:S(2)}) collective-permute-start(bf16[2,512,128]{2,1,0:T(8,128)(2,1)S(1)} %collective-permute-done.9.mid_ref), channel_id=1, source_target_pairs={{0,1},{1,0},{2,3},{3,2},{4,5},{5,4},{6,7},{7,6},{8,9},{9,8},{10,11... | collective-permute-start | bytes 786440 | tf_op jit(solution)/shard_map/ppermute | solution.py:197
  89.4 16.5 %collective-permute-start.6 = (bf16[2,512,128]{2,1,0:T(8,128)(2,1)S(1)}, bf16[2,512,128]{2,1,0:T(8,128)(2,1)S(1)}, u32[]{:S(2)}, u32[]{:S(2)}) collective-permute-start(bf16[2,512,128]{2,1,0:T(8,128)(2,1)S(1)} %get-tuple-element.25), channel_id=1, source_target_pairs={{0,1},{1,0},{2,3},{3,2},{4,5},{5,4},{6,7},{7,6},{8,9},{9,8},{10,11... | collective-permute-start | bytes 786440 | tf_op jit(solution)/shard_map/ppermute | solution.py:197
  89.4 16.5 %collective-permute-start.7 = (bf16[2,512,128]{2,1,0:T(8,128)(2,1)S(1)}, bf16[2,512,128]{2,1,0:T(8,128)(2,1)S(1)}, u32[]{:S(2)}, u32[]{:S(2)}) collective-permute-start(bf16[2,512,128]{2,1,0:T(8,128)(2,1)S(1)} %collective-permute-done.5.mid_ref), channel_id=1, source_target_pairs={{0,1},{1,0},{2,3},{3,2},{4,5},{5,4},{6,7},{7,6},{8,9},{9,8},{10,11... | collective-permute-start | bytes 786440 | tf_op jit(solution)/shard_map/ppermute | solution.py:197
  93.0 16.0 %collective-permute-start.2 = (bf16[2,512,128]{2,1,0:T(8,128)(2,1)S(1)}, bf16[2,512,128]{2,1,0:T(8,128)(2,1)S(1)}, u32[]{:S(2)}, u32[]{:S(2)}) collective-permute-start(bf16[2,512,128]{2,1,0:T(8,128)(2,1)S(1)} %get-tuple-element.27), channel_id=1, source_target_pairs={{0,1},{1,0},{2,3},{3,2},{4,5},{5,4},{6,7},{7,6},{8,9},{9,8},{10,11... | collective-permute-start | bytes 786440 | tf_op jit(solution)/shard_map/ppermute | solution.py:197
  93.1 15.9 %collective-permute-start.3 = (bf16[2,512,128]{2,1,0:T(8,128)(2,1)S(1)}, bf16[2,512,128]{2,1,0:T(8,128)(2,1)S(1)}, u32[]{:S(2)}, u32[]{:S(2)}) collective-permute-start(bf16[2,512,128]{2,1,0:T(8,128)(2,1)S(1)} %collective-permute-done.1.mid_ref), channel_id=1, source_target_pairs={{0,1},{1,0},{2,3},{3,2},{4,5},{5,4},{6,7},{7,6},{8,9},{9,8},{10,11... | collective-permute-start | bytes 786440 | tf_op jit(solution)/shard_map/ppermute | solution.py:197
  (3 other events, 45.4 us)
